TPU v7x, 128 devices: a whole 4x4x4 slice. The times are simulated.
128 devices in a mesh: tm: 8 (over x, core), space: 16 (over y, z).
Axes of the slice: x: 4, y: 4, z: 4, core: 2. Of those that a mesh axis runs over, the one named last changes fastest.
Arguments:
- adjoint_field: float32 [1024, 48, 9216], P('tm', 'space'), may hold values from -6 to 6
- absorption: float32 [48, 9216], P('space'), may hold values from 0.25 to 2
- mode_rates: float32 [16], replicated, may hold values from 0.1 to 40
- mode_weights: float32 [16], replicated, may hold values from 0.1 to 0.5
Outputs:
- adjoint_image: float32 [1024, 48, 9216], P('tm', 'space')
All inputs are finite; a program needn't handle non-finite values.
Results may differ from a plain program's by a relative error of at most 0.0001.
Values sent between devices are 32-bit elements; how exact they have to be, the bound alone decides.
A program may use at most 192 MiB of HBM per device.

v0:
```python
import jax
import jax.numpy as jnp
from jax import lax
from jax.sharding import PartitionSpec as P

NY = 96
BAND = 16


DIFFUSION = 0.2
ORDER_EXP = 0.4
STENCIL = (-1.0 / 12.0, 16.0 / 12.0, -30.0 / 12.0, 16.0 / 12.0, -1.0 / 12.0)


def shifted(block, axis, distance):
    devices = range(lax.axis_size(axis))
    route = [(i - distance, i) for i in devices if i - distance in devices]
    return lax.ppermute(block, axis, route)


def with_halo(cells, sides, width):
    for axis, dim in sides:
        count = lax.axis_size(axis)
        ends = count - 1
        head = lax.slice_in_dim(cells, 0, width, axis=dim)
        tail = lax.slice_in_dim(cells, cells.shape[dim] - width, cells.shape[dim], axis=dim)
        cells = jnp.concatenate(
            [
                lax.ppermute(tail, axis, [(i, (i + 1) % count) for i in range(ends)]),
                cells,
                lax.ppermute(head, axis, [((i + 1) % count, i) for i in range(ends)]),
            ],
            axis=dim,
        )
    return cells


def caputo_weights(count):
    steps_idx = jnp.arange(count, dtype=jnp.float32)
    increments = (steps_idx + 1.0) ** ORDER_EXP - steps_idx**ORDER_EXP
    earlier = jnp.concatenate([jnp.zeros((1,), jnp.float32), increments[:-1]])
    return increments - earlier


def mode_tables(mode_rates, mode_weights, total_steps):
    scaled = mode_rates / total_steps
    decays = jnp.exp(-scaled)
    mode_gain = mode_weights * jnp.sqrt(-jnp.expm1(-2.0 * scaled))
    return (scaled, decays, mode_gain)


def plane_masks(row_len, plane_len):
    column = jnp.arange(plane_len, dtype=jnp.int32) % row_len
    return [
        ((column + offset >= 0) & (column + offset < row_len)).astype(jnp.float32)
        for offset in (-2, -1, 1, 2)
    ]


def laplacian(padded, slab_depth, row_len):
    plane_len = padded.shape[-1]
    center = padded[..., 2 : 2 + slab_depth, :]
    summed = 3.0 * STENCIL[2] * center
    for offset in (-2, -1, 1, 2):
        summed = summed + STENCIL[offset + 2] * padded[..., 2 + offset : 2 + offset + slab_depth, :]
    widths = [(0, 0)] * (center.ndim - 1) + [(2 * row_len, 2 * row_len)]
    spread = jnp.pad(center, widths)
    y_masks = plane_masks(row_len, plane_len)
    for position, offset in enumerate((-2, -1, 1, 2)):
        weight = STENCIL[offset + 2]
        anchor = 2 * row_len + offset * row_len
        summed = summed + weight * spread[..., anchor : anchor + plane_len]
        anchor = 2 * row_len + offset
        summed = summed + weight * y_masks[position] * spread[..., anchor : anchor + plane_len]
    return summed


def per_device(adjoint_field, absorption, mode_rates, mode_weights):
    steps_dev, slab_depth, plane_len = adjoint_field.shape
    group_count = lax.axis_size("tm")
    total_steps = steps_dev * group_count
    scaled, decays, mode_gain = mode_tables(mode_rates, mode_weights, total_steps)
    cell_count = slab_depth * plane_len
    next_head = shifted(adjoint_field[: BAND - 1], "tm", -1)
    extended = jnp.concatenate([adjoint_field, next_head], axis=0)
    span_len = steps_dev + BAND - 1
    row_idx = jnp.arange(steps_dev, dtype=jnp.int32)[:, None]
    col_idx = jnp.arange(span_len, dtype=jnp.int32)[None, :]
    lag_steps = col_idx - row_idx
    lag_clip = jnp.clip(lag_steps, 0, span_len).astype(jnp.float32)
    far_table = jnp.sum(
        mode_gain[:, None, None] * jnp.exp(-scaled[:, None, None] * lag_clip[None]), axis=0
    )
    band_onehot = (
        lag_steps[None, :, :] == jnp.arange(BAND, dtype=jnp.int32)[:, None, None]
    ).astype(jnp.float32)
    near_part = jnp.sum(caputo_weights(BAND)[:, None, None] * band_onehot, axis=0)
    inside = col_idx < steps_dev
    in_band = (lag_steps >= 0) & (lag_steps < BAND)
    kernel = jnp.where(
        inside,
        near_part + jnp.where(lag_steps >= BAND, far_table, 0.0),
        jnp.where(in_band, near_part - far_table, 0.0),
    )
    flat_field = extended.reshape(span_len, cell_count)
    history = jnp.dot(
        kernel, flat_field, precision=lax.Precision.HIGHEST, preferred_element_type=jnp.float32
    )
    step_pos = jnp.arange(steps_dev, dtype=jnp.float32)
    projector = jnp.exp(-scaled[:, None] * step_pos[None, :])
    block_sums = jnp.dot(
        projector,
        flat_field[:steps_dev],
        precision=lax.Precision.HIGHEST,
        preferred_element_type=jnp.float32,
    )
    block_decay = jnp.exp(-scaled * steps_dev)[:, None]

    def relay_step(turn_idx, carried):
        return shifted(block_sums + block_decay * carried, "tm", -1)

    carried = lax.fori_loop(0, group_count - 1, relay_step, jnp.zeros_like(block_sums))
    remote_gain = mode_gain[None, :] * jnp.exp(-scaled[None, :] * (steps_dev - step_pos)[:, None])
    history = history + jnp.dot(
        remote_gain, carried, precision=lax.Precision.HIGHEST, preferred_element_type=jnp.float32
    )
    padded = with_halo(adjoint_field, (("space", 1),), 2)
    diffusion_term = laplacian(padded, slab_depth, NY)
    outcome = (
        history.reshape(adjoint_field.shape)
        + absorption[None] * adjoint_field
        - DIFFUSION * diffusion_term
    )
    return outcome


def solution(mesh):
    return jax.shard_map(
        per_device,
        mesh=mesh,
        in_specs=(P("tm", "space", None), P("space", None), P(), P()),
        out_specs=P("tm", "space", None),
        check_vma=False,
    )
```

profile of v0, /device:TPU:1, one launch (start us, length us, event | category | flops | bytes accessed | tf_op | source)
XLA Modules:
  0.0 435.2 jit_solution(4803071066318597514)
XLA Ops:
  0.0 1.6 slice.57
  1.6 3.3 collective-permute-start.1
  4.9 15.1 %copy.29 = f32[128,3,9216]{0,2,1:T(8,128)} copy(f32[128,3,9216]{2,0,1:T(8,128)} %param.6) | data formatting | bytes 28311552 | tf_op args[0]
  20.0 13.2 %fusion.82 = (f32[128,2,9216]{0,2,1:T(8,128)}, f32[128,2,9216]{0,2,1:T(8,128)}) fusion(f32[128,3,9216]{0,2,1:T(8,128)} %copy.29), kind=kLoop, calls=%fused_computation.109 | loop fusion | bytes 37748736 | tf_op jit(solution)/shard_map/slice | solution.py:26
  33.2 7.3 %collective-permute-start.2 = (f32[128,2,9216]{0,2,1:T(8,128)}, f32[128,2,9216]{0,2,1:T(8,128)}, u32[]{:S(2)}, u32[]{:S(2)}) collective-permute-start(f32[128,2,9216]{0,2,1:T(8,128)} %get-tuple-element.36), channel_id=1, source_target_pairs={{0,1},{1,2},{2,3},{3,4},{4,5},{5,6},{6,7},{7,8},{8,9},{9,10},{10,1... | collective-permute-start | bytes 28311560 | tf_op jit(solution)/shard_map/ppermute | solution.py:29
  44.8 14.2 %fusion.66 = f32[16,27648]{1,0:T(8,128)S(1)} fusion(f32[128,27648]{0,1:T(8,128)} %bitcast.14, f32[16]{0:T(128)S(1)} %get-tuple-element.39), kind=kOutput, calls=%fused_computation.85 | convolution fusion | flops 679479296 | bytes 15925312 | tf_op jit(solution)/shard_map/dot_general | solution.py:111
  59.0 6.8 %pad_maximum_fusion = f32[143,3,9216]{2,0,1:T(8,128)S(1)} fusion(f32[15,3,9216]{2,0,1:T(8,128)} %collective-permute-done.1, f32[128,3,9216]{2,0,1:T(8,128)} %param.6), kind=kLoop, calls=%fused_computation.6 | loop fusion | flops 3953664 | bytes 31629312 | tf_op jit(solution)/shard_map/concatenate | solution.py:85
  65.9 28.9 %copy.28 = f32[143,3,9216]{2,1,0:T(4,128)} copy(f32[143,3,9216]{2,0,1:T(8,128)S(1)} %pad_maximum_fusion) | data formatting | bytes 31629312 | tf_op jit(solution)/shard_map/concatenate | solution.py:85
  94.8 12.4 %pad.17 = f32[144,3,9216]{2,1,0:T(4,128)S(1)} pad(f32[143,3,9216]{2,1,0:T(4,128)} %copy.28, f32[]{:T(128)} %constant.18.clone.1), padding=0_1x0_0x0_0 | pad | bytes 31739908
  107.2 13.5 %copy.39 = f32[18,8,3,9216]{3,1,2,0:T(8,128)} copy(f32[18,8,3,9216]{3,2,1,0:T(4,128)S(1)} %bitcast.15) | data formatting | bytes 31850496
  120.7 19.6 %fusion.26 = f32[128,27648]{1,0:T(8,128)} fusion(f32[143,27648]{1,0:T(8,128)} %bitcast.16, f32[128,143]{0,1:T(8,128)S(1)} %get-tuple-element.42, f32[128,143]{0,1:T(8,128)S(1)} %get-tuple-element.41, pred[143]{0:T(512)(128)(4,1)S(1)} %copy-done.7), kind=kOutput, calls=%fused_computation.44 | convolution fusion | flops 6073011200 | bytes 30117008 | tf_op jit(solution)/shard_map/dot_general | solution.py:106
  140.5 180.1 %while.10 = (s32[]{:T(128)}, f32[16,27648]{1,0:T(8,128)S(1)}, f32[16,1]{0,1:T(1,128)S(1)}, f32[16,27648]{1,0:T(8,128)S(1)}, s32[]{:T(128)}) while((s32[]{:T(128)}, f32[16,27648]{1,0:T(8,128)S(1)}, f32[16,1]{0,1:T(1,128)S(1)}, f32[16,27648]{1,0:T(8,128)S(1)}, s32[]{:T(128)}) %tuple.24), condition=%wide.region_3.4_spmd, body=%wide.region_2.3_spmd.sunk | while | flops 884738 | bytes 12386469 | solution.py:122
  140.5 1.5 multiply_add_fusion.2
  141.9 1.9 collective-permute-start
  143.9 22.5 %collective-permute-done = f32[16,27648]{1,0:T(8,128)S(1)} collective-permute-done((f32[16,27648]{1,0:T(8,128)}, f32[16,27648]{1,0:T(8,128)S(1)}, u32[]{:S(2)}, u32[]{:S(2)}) %collective-permute-start) | collective-permute-done | bytes 1769504 | tf_op jit(solution)/shard_map/while/body/eval_jaxpr/ppermute | solution.py:18
  166.4 1.5 multiply_add_fusion.2
  167.8 1.9 collective-permute-start
  169.7 22.5 %collective-permute-done = f32[16,27648]{1,0:T(8,128)S(1)} collective-permute-done((f32[16,27648]{1,0:T(8,128)}, f32[16,27648]{1,0:T(8,128)S(1)}, u32[]{:S(2)}, u32[]{:S(2)}) %collective-permute-start) | collective-permute-done | bytes 1769504 | tf_op jit(solution)/shard_map/while/body/eval_jaxpr/ppermute | solution.py:18
  193.7 1.9 collective-permute-start
  195.6 22.5 %collective-permute-done = f32[16,27648]{1,0:T(8,128)S(1)} collective-permute-done((f32[16,27648]{1,0:T(8,128)}, f32[16,27648]{1,0:T(8,128)S(1)}, u32[]{:S(2)}, u32[]{:S(2)}) %collective-permute-start) | collective-permute-done | bytes 1769504 | tf_op jit(solution)/shard_map/while/body/eval_jaxpr/ppermute | solution.py:18
  219.6 1.9 collective-permute-start
  221.5 22.5 %collective-permute-done = f32[16,27648]{1,0:T(8,128)S(1)} collective-permute-done((f32[16,27648]{1,0:T(8,128)}, f32[16,27648]{1,0:T(8,128)S(1)}, u32[]{:S(2)}, u32[]{:S(2)}) %collective-permute-start) | collective-permute-done | bytes 1769504 | tf_op jit(solution)/shard_map/while/body/eval_jaxpr/ppermute | solution.py:18
  245.5 1.9 collective-permute-start
  247.4 22.1 %collective-permute-done = f32[16,27648]{1,0:T(8,128)S(1)} collective-permute-done((f32[16,27648]{1,0:T(8,128)}, f32[16,27648]{1,0:T(8,128)S(1)}, u32[]{:S(2)}, u32[]{:S(2)}) %collective-permute-start) | collective-permute-done | bytes 1769504 | tf_op jit(solution)/shard_map/while/body/eval_jaxpr/ppermute | solution.py:18
  271.0 1.9 collective-permute-start
  272.9 22.1 %collective-permute-done = f32[16,27648]{1,0:T(8,128)S(1)} collective-permute-done((f32[16,27648]{1,0:T(8,128)}, f32[16,27648]{1,0:T(8,128)S(1)}, u32[]{:S(2)}, u32[]{:S(2)}) %collective-permute-start) | collective-permute-done | bytes 1769504 | tf_op jit(solution)/shard_map/while/body/eval_jaxpr/ppermute | solution.py:18
  296.5 1.9 collective-permute-start
  298.4 22.1 %collective-permute-done = f32[16,27648]{1,0:T(8,128)S(1)} collective-permute-done((f32[16,27648]{1,0:T(8,128)}, f32[16,27648]{1,0:T(8,128)S(1)}, u32[]{:S(2)}, u32[]{:S(2)}) %collective-permute-start) | collective-permute-done | bytes 1769504 | tf_op jit(solution)/shard_map/while/body/eval_jaxpr/ppermute | solution.py:18
  320.5 16.3 %convolution_add_fusion = f32[128,27648]{1,0:T(8,128)} fusion(f32[128,27648]{1,0:T(8,128)} %fusion.26, f32[16,27648]{1,0:T(8,128)S(1)} %get-tuple-element.27, f32[128]{0:T(128)S(1)} %iota_subtract_fusion.1, f32[16]{0:T(128)S(1)} %get-tuple-element.39, f32[16]{0:T(128)S(1)} %get-tuple-element.40), kind=kOutput, calls=%fused_computation.1 | convolution fusion | flops 683020288 | bytes 30081664 | tf_op jit(solution)/shard_map/dot_general | solution.py:124
  336.8 15.2 %copy.30 = f32[128,27648]{0,1:T(8,128)} copy(f32[128,27648]{1,0:T(8,128)} %convolution_add_fusion) | data formatting | bytes 28311552 | tf_op jit(solution)/shard_map/add | solution.py:124
  352.0 68.1 %fusion.13 = f32[128,3,9216]{0,2,1:T(8,128)} fusion(f32[128,3,9216]{0,2,1:T(8,128)} %copy.29, f32[128,2,9216]{0,2,1:T(8,128)} %collective-permute-done.3, f32[128,2,9216]{0,2,1:T(8,128)} %collective-permute-done.2, f32[128,3,9216]{0,2,1:T(8,128)} %bitcast.17, f32[9216]{0:T(1024)S(1)} %copy-done.3, f32[9216]{0:T(1024)S(1)} %copy-done.4, ...), kind=kLoop, calls=%fused_computation.20 | loop fusion | flops 116785152 | bytes 61599744 | tf_op jit(solution)/shard_map/sub | solution.py:130
  420.1 15.1 %copy.38 = f32[128,3,9216]{2,0,1:T(8,128)} copy(f32[128,3,9216]{0,2,1:T(8,128)} %fusion.13) | data formatting | bytes 28311552 | tf_op jit(solution)/shard_map/sub | solution.py:130
  (36 shorter events, 11.6 us)
Async XLA Ops:
  1.6 57.4 %collective-permute-start.1 = (f32[15,3,9216]{2,0,1:T(8,128)S(1)}, f32[15,3,9216]{2,0,1:T(8,128)}, u32[]{:S(2)}, u32[]{:S(2)}) collective-permute-start(f32[15,3,9216]{2,0,1:T(8,128)S(1)} %slice.57), channel_id=1, source_target_pairs={{16,0},{32,16},{48,32},{64,48},{80,64},{96,80},{112,96},{17,1},{33... | collective-permute-start | bytes 4976648 | tf_op jit(solution)/shard_map/ppermute | solution.py:18
  20.0 22.6 %copy-start.5 = (f32[16]{0:T(128)S(1)}, f32[16]{0:T(128)}, u32[]{:S(2)}) copy-start(f32[16]{0:T(128)} %param.8) | copy-start | bytes 196
  20.0 22.6 %copy-start.6 = (f32[16]{0:T(128)S(1)}, f32[16]{0:T(128)}, u32[]{:S(2)}) copy-start(f32[16]{0:T(128)} %param.9) | copy-start | bytes 196
  33.2 318.7 %collective-permute-start.2 = (f32[128,2,9216]{0,2,1:T(8,128)}, f32[128,2,9216]{0,2,1:T(8,128)}, u32[]{:S(2)}, u32[]{:S(2)}) collective-permute-start(f32[128,2,9216]{0,2,1:T(8,128)} %get-tuple-element.36), channel_id=1, source_target_pairs={{0,1},{1,2},{2,3},{3,4},{4,5},{5,6},{6,7},{7,8},{8,9},{9,10},{10,1... | collective-permute-start | bytes 28311560 | tf_op jit(solution)/shard_map/ppermute | solution.py:29
  40.5 311.4 %collective-permute-start.3 = (f32[128,2,9216]{0,2,1:T(8,128)}, f32[128,2,9216]{0,2,1:T(8,128)}, u32[]{:S(2)}, u32[]{:S(2)}) collective-permute-start(f32[128,2,9216]{0,2,1:T(8,128)} %get-tuple-element.37), channel_id=1, source_target_pairs={{1,0},{2,1},{3,2},{4,3},{5,4},{6,5},{7,6},{8,7},{9,8},{10,9},{11,1... | collective-permute-start | bytes 28311560 | tf_op jit(solution)/shard_map/ppermute | solution.py:31
  107.2 13.6 %copy-start.7 = (pred[143]{0:T(512)(128)(4,1)S(1)}, pred[143]{0:T(512)(128)(4,1)}, u32[]{:S(2)}) copy-start(pred[143]{0:T(512)(128)(4,1)} %iota_compare_fusion.1) | copy-start | bytes 433
  141.9 24.4 %collective-permute-start = (f32[16,27648]{1,0:T(8,128)}, f32[16,27648]{1,0:T(8,128)S(1)}, u32[]{:S(2)}, u32[]{:S(2)}) collective-permute-start(f32[16,27648]{1,0:T(8,128)} %multiply_add_fusion.2), channel_id=1, source_target_pairs={{16,0},{32,16},{48,32},{64,48},{80,64},{96,80},{112,96},{17,1},{33... | collective-permute-start | bytes 5308424 | tf_op jit(solution)/shard_map/while/body/eval_jaxpr/ppermute | solution.py:18
  167.8 24.4 %collective-permute-start = (f32[16,27648]{1,0:T(8,128)}, f32[16,27648]{1,0:T(8,128)S(1)}, u32[]{:S(2)}, u32[]{:S(2)}) collective-permute-start(f32[16,27648]{1,0:T(8,128)} %multiply_add_fusion.2), channel_id=1, source_target_pairs={{16,0},{32,16},{48,32},{64,48},{80,64},{96,80},{112,96},{17,1},{33... | collective-permute-start | bytes 5308424 | tf_op jit(solution)/shard_map/while/body/eval_jaxpr/ppermute | solution.py:18
  193.7 24.4 %collective-permute-start = (f32[16,27648]{1,0:T(8,128)}, f32[16,27648]{1,0:T(8,128)S(1)}, u32[]{:S(2)}, u32[]{:S(2)}) collective-permute-start(f32[16,27648]{1,0:T(8,128)} %multiply_add_fusion.2), channel_id=1, source_target_pairs={{16,0},{32,16},{48,32},{64,48},{80,64},{96,80},{112,96},{17,1},{33... | collective-permute-start | bytes 5308424 | tf_op jit(solution)/shard_map/while/body/eval_jaxpr/ppermute | solution.py:18
  219.6 24.4 %collective-permute-start = (f32[16,27648]{1,0:T(8,128)}, f32[16,27648]{1,0:T(8,128)S(1)}, u32[]{:S(2)}, u32[]{:S(2)}) collective-permute-start(f32[16,27648]{1,0:T(8,128)} %multiply_add_fusion.2), channel_id=1, source_target_pairs={{16,0},{32,16},{48,32},{64,48},{80,64},{96,80},{112,96},{17,1},{33... | collective-permute-start | bytes 5308424 | tf_op jit(solution)/shard_map/while/body/eval_jaxpr/ppermute | solution.py:18
  245.5 24.0 %collective-permute-start = (f32[16,27648]{1,0:T(8,128)}, f32[16,27648]{1,0:T(8,128)S(1)}, u32[]{:S(2)}, u32[]{:S(2)}) collective-permute-start(f32[16,27648]{1,0:T(8,128)} %multiply_add_fusion.2), channel_id=1, source_target_pairs={{16,0},{32,16},{48,32},{64,48},{80,64},{96,80},{112,96},{17,1},{33... | collective-permute-start | bytes 5308424 | tf_op jit(solution)/shard_map/while/body/eval_jaxpr/ppermute | solution.py:18
  271.0 24.0 %collective-permute-start = (f32[16,27648]{1,0:T(8,128)}, f32[16,27648]{1,0:T(8,128)S(1)}, u32[]{:S(2)}, u32[]{:S(2)}) collective-permute-start(f32[16,27648]{1,0:T(8,128)} %multiply_add_fusion.2), channel_id=1, source_target_pairs={{16,0},{32,16},{48,32},{64,48},{80,64},{96,80},{112,96},{17,1},{33... | collective-permute-start | bytes 5308424 | tf_op jit(solution)/shard_map/while/body/eval_jaxpr/ppermute | solution.py:18
  296.5 24.0 %collective-permute-start = (f32[16,27648]{1,0:T(8,128)}, f32[16,27648]{1,0:T(8,128)S(1)}, u32[]{:S(2)}, u32[]{:S(2)}) collective-permute-start(f32[16,27648]{1,0:T(8,128)} %multiply_add_fusion.2), channel_id=1, source_target_pairs={{16,0},{32,16},{48,32},{64,48},{80,64},{96,80},{112,96},{17,1},{33... | collective-permute-start | bytes 5308424 | tf_op jit(solution)/shard_map/while/body/eval_jaxpr/ppermute | solution.py:18
  336.8 15.2 %copy-start = (f32[3,9216]{1,0:T(4,128)S(1)}, f32[3,9216]{1,0:T(4,128)}, u32[]{:S(2)}) copy-start(f32[3,9216]{1,0:T(4,128)} %param.7) | copy-start | bytes 331780
  336.8 15.2 %copy-start.1 = (f32[9216]{0:T(1024)S(1)}, f32[9216]{0:T(1024)}, u32[]{:S(2)}) copy-start(f32[9216]{0:T(1024)} %get-tuple-element.45) | copy-start | bytes 110596
  336.8 15.2 %copy-start.2 = (f32[9216]{0:T(1024)S(1)}, f32[9216]{0:T(1024)}, u32[]{:S(2)}) copy-start(f32[9216]{0:T(1024)} %get-tuple-element.46) | copy-start | bytes 110596
  336.8 15.2 %copy-start.3 = (f32[9216]{0:T(1024)S(1)}, f32[9216]{0:T(1024)}, u32[]{:S(2)}) copy-start(f32[9216]{0:T(1024)} %get-tuple-element.43) | copy-start | bytes 110596
  336.8 15.2 %copy-start.4 = (f32[9216]{0:T(1024)S(1)}, f32[9216]{0:T(1024)}, u32[]{:S(2)}) copy-start(f32[9216]{0:T(1024)} %get-tuple-element.44) | copy-start | bytes 110596
where the time goes:
time: 436 us; the launch traced here: 435 us
  waiting for transfers between devices  156 us (36%)
  local copies, waits for them, and re-layouts  115 us (26%)
  other arithmetic  88 us (20%)
  matrix products  50.1 us (11%)
  starting transfers between devices  25.2 us (6%)
    ppermute x8, waiting for transfers between devices, shifted(): return lax.ppermute(block, axis, route)  156 us
    sub x1, other arithmetic, per_device(): history.reshape(adjoint_field.shape) + absorption[None] * adjoint_field  68.1 us
    unnamed x19, local copies, waits for them, and re-layouts  41 us
    concatenate x1, local copies, waits for them, and re-layouts, per_device(): extended = jnp.concatenate([adjoint_field, next_head], axis=0)  28.9 us
    dot_general x1, matrix products, per_device(): jnp.dot(kernel, flat_field, precision=lax.Precision.HIGHEST, preferred_el...  19.6 us
    ppermute x8, starting transfers between devices, shifted(): return lax.ppermute(block, axis, route)  16.6 us
    dot_general x1, matrix products, per_device(): jnp.dot(remote_gain, carried, precision=lax.Precision.HIGHEST, preferred_...  16.3 us
    add x1, local copies, waits for them, and re-layouts, per_device(): history + jnp.dot(remote_gain, carried, precision=lax.Precision.HIGHEST,...  15.2 us
  transfers between devices with their start and end apart: 10, of which 7 were waited for; matrix products, arithmetic and copies ran while one was open for 39% of the time, Pallas kernels for 0%

commit v1 on v0

v1 whole, which is shorter than its diff:
```python
import jax
import jax.numpy as jnp
from jax import lax
from jax.experimental import pallas as pl
from jax.experimental.pallas import tpu as pltpu
from jax.sharding import PartitionSpec as P


NY = 96
BAND = 16
DIFFUSION = 0.2
ORDER_EXP = 0.4
EDGE = 256
TILE = 2304
CHUNKS = (16, 64, 40, 8)
EXACT = lax.Precision.HIGHEST


def caputo_weights(count):
    steps_idx = jnp.arange(count, dtype=jnp.float32)
    increments = (steps_idx + 1.0) ** ORDER_EXP - steps_idx**ORDER_EXP
    earlier = jnp.concatenate([jnp.zeros((1,), jnp.float32), increments[:-1]])
    return increments - earlier


def history_tables(scaled, mode_gain, steps_dev):
    span_len = steps_dev + BAND
    row_idx = jnp.arange(steps_dev, dtype=jnp.int32)[:, None]
    col_idx = jnp.arange(span_len, dtype=jnp.int32)[None, :]
    lag = col_idx - row_idx
    lag_clip = jnp.clip(lag, 0, span_len).astype(jnp.float32)
    far = jnp.sum(
        mode_gain[:, None, None] * jnp.exp(-scaled[:, None, None] * lag_clip[None]), axis=0
    )
    onehot = (lag[None] == jnp.arange(BAND, dtype=jnp.int32)[:, None, None]).astype(jnp.float32)
    near = jnp.sum(caputo_weights(BAND)[:, None, None] * onehot, axis=0)
    in_band = (lag >= 0) & (lag < BAND)
    own = near + jnp.where(lag >= BAND, far, 0.0)
    ahead = jnp.where(in_band, near - far, 0.0)
    step_pos = jnp.arange(steps_dev, dtype=jnp.float32)
    remote = mode_gain[None, :] * jnp.exp(-scaled[None, :] * (steps_dev - step_pos)[:, None])
    table = jnp.concatenate(
        [jnp.where(col_idx < steps_dev, own, ahead), remote], axis=1
    )
    projector = jnp.exp(-scaled[:, None] * step_pos[None, :])
    return table, projector


def project_kernel(projector_ref, field_ref, out_ref):
    out_ref[0] = jnp.dot(
        projector_ref[...], field_ref[0], precision=EXACT, preferred_element_type=jnp.float32
    )


def block_sums(projector, field):
    depth, steps, plane = field.shape
    modes = projector.shape[0]
    return pl.pallas_call(
        project_kernel,
        out_shape=jax.ShapeDtypeStruct((depth, modes, plane), jnp.float32),
        grid=(depth, plane // TILE),
        in_specs=[
            pl.BlockSpec((modes, steps), lambda p, i: (0, 0)),
            pl.BlockSpec((1, steps, TILE), lambda p, i: (p, 0, i)),
        ],
        out_specs=pl.BlockSpec((1, modes, TILE), lambda p, i: (p, 0, i)),
        cost_estimate=pl.CostEstimate(
            flops=12 * modes * steps * depth * plane,
            bytes_accessed=4 * depth * plane * (steps + modes),
            transcendentals=0,
        ),
        name="block_sums",
    )(projector, field)


def local_kernel(
    table_ref, left_ref, mid_ref, right_ref, head_ref, carried_ref, absorb_ref, out_ref, wide, masks
):
    depth, steps, width = mid_ref.shape
    spot, spots = pl.program_id(0), pl.num_programs(0)
    column = lax.broadcasted_iota(jnp.int32, (8, width), 1) % NY
    for k, offset in enumerate((-2, -1, 1, 2)):
        good = (column + offset >= 0) & (column + offset < NY)
        masks[k] = jnp.where(good, 16.0 if offset in (-1, 1) else -1.0, 0.0)
    has_left = jnp.where(spot > 0, 1.0, 0.0)
    has_right = jnp.where(spot < spots - 1, 1.0, 0.0)
    factor = -DIFFUSION / 12.0
    for p in range(depth):
        wide[0:steps, 0:EDGE] = left_ref[p] * has_left
        wide[0:steps, EDGE : EDGE + width] = mid_ref[p]
        wide[0:steps, EDGE + width :] = right_ref[p] * has_right
        wide[steps : steps + BAND, EDGE : EDGE + width] = head_ref[p]
        wide[steps + BAND :, EDGE : EDGE + width] = carried_ref[p]
        out_ref[p] = jnp.dot(
            table_ref[...],
            wide[:, EDGE : EDGE + width],
            precision=EXACT,
            preferred_element_type=jnp.float32,
        )
        absorb = jnp.broadcast_to(absorb_ref[pl.ds(p, 1), :], (8, width)) - 90.0 * factor

        def some_steps(t, _, p=p, absorb=absorb):
            rows = pl.ds(pl.multiple_of(t * 8, 8), 8)

            def at(offset):
                return wide[rows, EDGE + offset : EDGE + offset + width]

            center = mid_ref[p, rows, :]
            near = at(-NY) + at(NY)
            far = at(-2 * NY) + at(2 * NY)
            for q in range(depth):
                if abs(q - p) == 1:
                    near = near + mid_ref[q, rows, :]
                if abs(q - p) == 2:
                    far = far + mid_ref[q, rows, :]
            total = 16.0 * near - far
            for k, offset in enumerate((-2, -1, 1, 2)):
                total = total + masks[k] * at(offset)
            out_ref[p, rows, :] = out_ref[p, rows, :] + absorb * center + factor * total
            return 0

        lax.fori_loop(0, steps // 8, some_steps, 0)


def local_part(table, field, head, carried, absorption):
    depth, steps, plane = field.shape
    per = TILE // EDGE
    last = plane // EDGE - 1
    cols = table.shape[1]
    return pl.pallas_call(
        local_kernel,
        out_shape=jax.ShapeDtypeStruct(field.shape, jnp.float32),
        grid=(plane // TILE,),
        in_specs=[
            pl.BlockSpec((steps, cols), lambda i: (0, 0)),
            pl.BlockSpec((depth, steps, EDGE), lambda i: (0, 0, jnp.maximum(i * per - 1, 0))),
            pl.BlockSpec((depth, steps, TILE), lambda i: (0, 0, i)),
            pl.BlockSpec((depth, steps, EDGE), lambda i: (0, 0, jnp.minimum(i * per + per, last))),
            pl.BlockSpec((depth, BAND, TILE), lambda i: (0, 0, i)),
            pl.BlockSpec((depth, cols - steps - BAND, TILE), lambda i: (0, 0, i)),
            pl.BlockSpec((depth, TILE), lambda i: (0, i)),
        ],
        out_specs=pl.BlockSpec((depth, steps, TILE), lambda i: (0, 0, i)),
        scratch_shapes=[
            pltpu.VMEM((cols, TILE + 2 * EDGE), jnp.float32),
            pltpu.VMEM((4, 8, TILE), jnp.float32),
        ],
        compiler_params=pltpu.CompilerParams(vmem_limit_bytes=48 * 1024 * 1024),
        cost_estimate=pl.CostEstimate(
            flops=12 * cols * steps * depth * plane,
            bytes_accessed=8 * depth * plane * steps,
            transcendentals=0,
        ),
        name="local_part",
    )(table, field, field, field, head, carried, absorption)


def edge_kernel(image_ref, below_ref, above_ref, out_ref):
    depth = image_ref.shape[0]
    factor = -DIFFUSION / 12.0
    ends = [None] * depth

    def add(p, value):
        if 0 <= p < depth:
            ends[p] = value if ends[p] is None else ends[p] + value

    add(0, 16.0 * below_ref[1] - below_ref[0])
    add(1, -below_ref[1])
    add(depth - 1, 16.0 * above_ref[0] - above_ref[1])
    add(depth - 2, -above_ref[0])
    for p in range(depth):
        image = image_ref[p]
        out_ref[p] = image if ends[p] is None else image + factor * ends[p]


def add_edges(image, below, above, first, rows, width):
    depth, _, plane = image.shape
    count = below.shape[1]
    at = first // rows
    return pl.pallas_call(
        edge_kernel,
        out_shape=jax.ShapeDtypeStruct(image.shape, jnp.float32),
        grid=(count // rows, plane // width),
        in_specs=[
            pl.BlockSpec((depth, rows, width), lambda i, j: (0, at + i, j)),
            pl.BlockSpec((2, rows, width), lambda i, j: (0, i, j)),
            pl.BlockSpec((2, rows, width), lambda i, j: (0, i, j)),
        ],
        out_specs=pl.BlockSpec((depth, rows, width), lambda i, j: (0, at + i, j)),
        input_output_aliases={0: 0},
        cost_estimate=pl.CostEstimate(
            flops=8 * depth * count * plane,
            bytes_accessed=4 * count * plane * (2 * depth + 4),
            transcendentals=0,
        ),
        name="add_edges",
    )(image, below, above)


def per_device(adjoint_field, absorption, mode_rates, mode_weights):
    steps, depth, plane = adjoint_field.shape
    groups = lax.axis_size("tm")
    slabs = lax.axis_size("space")
    field = jnp.transpose(adjoint_field, (1, 0, 2))

    up = [(i, i + 1) for i in range(slabs - 1)]
    down = [(i + 1, i) for i in range(slabs - 1)]
    below, above, starts = [], [], []
    first = 0
    source = field
    for count in CHUNKS:
        starts.append(first)
        high = source[depth - 2 :, first : first + count]
        low = source[:2, first : first + count]
        below.append(lax.ppermute(high, "space", up))
        above.append(lax.ppermute(low, "space", down))
        source, _, _ = lax.optimization_barrier((source, high, low))
        if len(starts) == 2:
            early = source
        first += count

    scaled = mode_rates / (steps * groups)
    mode_gain = mode_weights * jnp.sqrt(-jnp.expm1(-2.0 * scaled))
    table, projector = history_tables(scaled, mode_gain, steps)

    head = lax.ppermute(early[:, :BAND], "tm", [(g + 1, g) for g in range(groups - 1)])
    sums = block_sums(projector, early)
    decay = jnp.exp(-scaled * steps)[None, :, None]
    swap = [(g, g + 1 - 2 * (g % 2)) for g in range(groups)]
    other = lax.ppermute(sums, "tm", swap)
    core = lax.axis_index("tm") % 2
    half = plane // 2
    mine_half = lax.dynamic_slice_in_dim(sums, core * half, half, axis=2)
    other_half = lax.dynamic_slice_in_dim(other, core * half, half, axis=2)
    pair_half = jnp.where(
        core == 0, mine_half + decay * other_half, other_half + decay * mine_half
    )
    later = None
    for _ in range(groups // 2 - 1):
        sent = pair_half if later is None else pair_half + decay * decay * later
        later = lax.ppermute(sent, "tm", [(g + 2, g) for g in range(groups - 2)])
    later_other = lax.ppermute(later, "tm", swap)
    later_full = jnp.where(
        core == 0,
        jnp.concatenate([later, later_other], axis=2),
        jnp.concatenate([later_other, later], axis=2),
    )
    carried = jnp.where(core == 0, other + decay * later_full, later_full)

    image = local_part(table, field, head, carried, absorption)
    for first, lower, upper in zip(starts, below, above):
        count = lower.shape[1]
        image = add_edges(image, lower, upper, first, 8, plane if count > 8 else TILE)
    return jnp.transpose(image, (1, 0, 2))


def solution(mesh):
    return jax.shard_map(
        per_device,
        mesh=mesh,
        in_specs=(P("tm", "space", None), P("space", None), P(), P()),
        out_specs=P("tm", "space", None),
        check_vma=False,
    )
```

time: 436 us -> 319 us (0.73)
  the two profiles are of different devices: /device:TPU:1 before, /device:TPU:30 now
where the time goes in v1:
time: 319 us; the launch traced here: 318 us
  Pallas kernels  158 us (50%)
  waiting for transfers between devices  72 us (23%)
  starting transfers between devices  46.8 us (15%)
  local copies, waits for them, and re-layouts  29.1 us (9%)
  other arithmetic  12.1 us (4%)
    pallas_call x1, Pallas kernels, local_part(): pl.pallas_call(local_kernel, out_shape=jax.ShapeDtypeStruct(field.shape,...  120 us
    ppermute x4, waiting for transfers between devices, per_device(): below.append(lax.ppermute(high, 'space', up))  28.2 us
    pallas_call x4, Pallas kernels, add_edges(): pl.pallas_call(edge_kernel, out_shape=jax.ShapeDtypeStruct(image.shape, j...  24.6 us
    ppermute x3, waiting for transfers between devices, per_device(): later = lax.ppermute(sent, 'tm', [(g + 2, g) for g in range(groups - 2)])  22.5 us
    slice x4, local copies, waits for them, and re-layouts, per_device(): low = source[:2, first:first + count]  19.3 us
    ppermute x4, starting transfers between devices, per_device(): above.append(lax.ppermute(low, 'space', down))  18.4 us
    ppermute x1, waiting for transfers between devices, per_device(): lax.ppermute(early[:, :BAND], 'tm', [(g + 1, g) for g in range(groups - 1)])  17.4 us
    pallas_call x1, Pallas kernels, block_sums(): pl.pallas_call(project_kernel, out_shape=jax.ShapeDtypeStruct((depth, mod...  13.1 us
  transfers between devices with their start and end apart: 14, of which 6 were waited for; matrix products, arithmetic and copies ran while one was open for 8% of the time, Pallas kernels for 44%

profile of v1, /device:TPU:30, one launch (start us, length us, event | category | flops | bytes accessed | tf_op | source)
XLA Modules:
  0.0 317.7 jit_solution(8949162989687652853)
XLA Ops:
  0.0 2.8 fusion.10
  2.8 8.6 %fusion.9 = (f32[2,64,9216]{2,1,0:T(8,128)}, f32[2,64,9216]{2,1,0:T(8,128)}) fusion(f32[3,128,9216]{2,1,0:T(8,128)} %bitcast.4), kind=kLoop, calls=%fused_computation.31 | loop fusion | bytes 18874368 | tf_op jit(solution)/shard_map/slice | solution.py:214
  12.1 13.1 %block_sums.1 = f32[3,16,9216]{2,1,0:T(8,128)} custom-call(f32[16,128]{1,0:T(8,128)} %multiply_exponential_fusion.projector_ref, f32[3,128,9216]{2,1,0:T(8,128)} %bitcast.5), custom_call_target="tpu_custom_call" | custom-call | flops 679477248 | bytes 15925248 | tf_op jit(solution)/shard_map/block_sums/pallas_call | solution.py:58
  25.2 3.9 %collective-permute-done.1 = f32[3,16,9216]{2,1,0:T(8,128)S(1)} collective-permute-done((f32[3,16,9216]{2,1,0:T(8,128)}, f32[3,16,9216]{2,1,0:T(8,128)S(1)}, u32[]{:S(2)}, u32[]{:S(2)}) %collective-permute-start.1) | collective-permute-done | bytes 1769504 | tf_op jit(solution)/shard_map/ppermute | solution.py:230
  30.5 2.8 collective-permute-start.2
  33.3 3.8 %collective-permute-start.6 = (f32[2,16,9216]{2,1,0:T(8,128)}, f32[2,16,9216]{2,1,0:T(8,128)}, u32[]{:S(2)}, u32[]{:S(2)}) collective-permute-start(f32[2,16,9216]{2,1,0:T(8,128)} %get-tuple-element.18), channel_id=1, source_target_pairs={{0,1},{1,2},{2,3},{3,4},{4,5},{5,6},{6,7},{7,8},{8,9},{9,10},{10,1... | collective-permute-start | bytes 3538952 | tf_op jit(solution)/shard_map/ppermute | solution.py:215
  37.1 4.2 %collective-permute-start.7 = (f32[2,16,9216]{2,1,0:T(8,128)S(1)}, f32[2,16,9216]{2,1,0:T(8,128)}, u32[]{:S(2)}, u32[]{:S(2)}) collective-permute-start(f32[2,16,9216]{2,1,0:T(8,128)S(1)} %get-tuple-element.17), channel_id=1, source_target_pairs={{1,0},{2,1},{3,2},{4,3},{5,4},{6,5},{7,6},{8,7},{9,8},{10,9},{11,1... | collective-permute-start | bytes 3538952 | tf_op jit(solution)/shard_map/ppermute | solution.py:216
  41.3 1.9 collective-permute-start.8
  43.3 6.0 %collective-permute-start.9 = (f32[2,64,9216]{2,1,0:T(8,128)}, f32[2,64,9216]{2,1,0:T(8,128)}, u32[]{:S(2)}, u32[]{:S(2)}) collective-permute-start(f32[2,64,9216]{2,1,0:T(8,128)} %get-tuple-element.15), channel_id=1, source_target_pairs={{1,0},{2,1},{3,2},{4,3},{5,4},{6,5},{7,6},{8,7},{9,8},{10,9},{11,1... | collective-permute-start | bytes 14155784 | tf_op jit(solution)/shard_map/ppermute | solution.py:216
  49.3 3.1 collective-permute-done.2
  52.6 4.4 %collective-permute-start.3 = (f32[3,16,4608]{2,1,0:T(8,128)S(1)}, f32[3,16,4608]{2,1,0:T(8,128)S(1)}, u32[]{:S(2)}, u32[]{:S(2)}) collective-permute-start(f32[3,16,4608]{2,1,0:T(8,128)S(1)} %multiply_add_fusion.1), channel_id=1, source_target_pairs={{32,0},{48,16},{64,32},{80,48},{96,64},{112,80},{33,1},{49,17},{65... | collective-permute-start | bytes 2654216 | tf_op jit(solution)/shard_map/ppermute | solution.py:241
  57.0 5.8 %fusion.8 = (f32[2,40,9216]{2,1,0:T(8,128)}, f32[2,40,9216]{2,1,0:T(8,128)}) fusion(f32[3,128,9216]{2,1,0:T(8,128)} %bitcast.6), kind=kLoop, calls=%fused_computation.30 | loop fusion | bytes 11796480 | tf_op jit(solution)/shard_map/slice | solution.py:214
  62.8 12.6 %collective-permute-done.3 = f32[3,16,4608]{2,1,0:T(8,128)S(1)} collective-permute-done((f32[3,16,4608]{2,1,0:T(8,128)S(1)}, f32[3,16,4608]{2,1,0:T(8,128)S(1)}, u32[]{:S(2)}, u32[]{:S(2)}) %collective-permute-start.3) | collective-permute-done | bytes 884768 | tf_op jit(solution)/shard_map/ppermute | solution.py:241
  76.5 5.3 %collective-permute-start.4 = (f32[3,16,4608]{2,1,0:T(8,128)}, f32[3,16,4608]{2,1,0:T(8,128)}, u32[]{:S(2)}, u32[]{:S(2)}) collective-permute-start(f32[3,16,4608]{2,1,0:T(8,128)} %multiply_add_fusion), channel_id=1, source_target_pairs={{32,0},{48,16},{64,32},{80,48},{96,64},{112,80},{33,1},{49,17},{65... | collective-permute-start | bytes 2654216 | tf_op jit(solution)/shard_map/ppermute | solution.py:241
  81.8 2.1 fusion.7
  86.3 1.8 multiply_reduce_fusion
  90.4 1.6 copy.15
  92.1 6.8 %collective-permute-done.4 = f32[3,16,4608]{2,1,0:T(8,128)} collective-permute-done((f32[3,16,4608]{2,1,0:T(8,128)}, f32[3,16,4608]{2,1,0:T(8,128)}, u32[]{:S(2)}, u32[]{:S(2)}) %collective-permute-start.4) | collective-permute-done | bytes 884768 | tf_op jit(solution)/shard_map/ppermute | solution.py:241
  98.9 1.7 select_reduce_fusion
  103.2 3.8 %collective-permute-start.10 = (f32[2,40,9216]{2,1,0:T(8,128)}, f32[2,40,9216]{2,1,0:T(8,128)}, u32[]{:S(2)}, u32[]{:S(2)}) collective-permute-start(f32[2,40,9216]{2,1,0:T(8,128)} %get-tuple-element.14), channel_id=1, source_target_pairs={{0,1},{1,2},{2,3},{3,4},{4,5},{5,6},{6,7},{7,8},{8,9},{9,10},{10,1... | collective-permute-start | bytes 8847368 | tf_op jit(solution)/shard_map/ppermute | solution.py:215
  107.1 4.2 %collective-permute-start.11 = (f32[2,40,9216]{2,1,0:T(8,128)}, f32[2,40,9216]{2,1,0:T(8,128)}, u32[]{:S(2)}, u32[]{:S(2)}) collective-permute-start(f32[2,40,9216]{2,1,0:T(8,128)} %get-tuple-element.13), channel_id=1, source_target_pairs={{1,0},{2,1},{3,2},{4,3},{5,4},{6,5},{7,6},{8,7},{9,8},{10,9},{11,1... | collective-permute-start | bytes 8847368 | tf_op jit(solution)/shard_map/ppermute | solution.py:216
  113.1 4.4 %collective-permute-start = (f32[3,16,9216]{2,1,0:T(8,128)S(1)}, f32[3,16,9216]{2,1,0:T(8,128)S(1)}, u32[]{:S(2)}, u32[]{:S(2)}) collective-permute-start(f32[3,16,9216]{2,1,0:T(8,128)S(1)} %slice.35), channel_id=1, source_target_pairs={{16,0},{32,16},{48,32},{64,48},{80,64},{96,80},{112,96},{17,1},{33... | collective-permute-start | bytes 5308424 | tf_op jit(solution)/shard_map/ppermute | solution.py:226
  117.5 2.6 add_select_fusion.carried_ref
  120.1 17.4 %collective-permute-done.head_ref = f32[3,16,9216]{2,1,0:T(8,128)S(1)} collective-permute-done((f32[3,16,9216]{2,1,0:T(8,128)S(1)}, f32[3,16,9216]{2,1,0:T(8,128)S(1)}, u32[]{:S(2)}, u32[]{:S(2)}) %collective-permute-start) | collective-permute-done | bytes 1769504 | tf_op jit(solution)/shard_map/ppermute | solution.py:226
  137.5 1.9 collective-permute-start.12
  139.4 28.2 %collective-permute-done.8.below_ref = f32[2,64,9216]{2,1,0:T(8,128)} collective-permute-done((f32[2,64,9216]{2,1,0:T(8,128)}, f32[2,64,9216]{2,1,0:T(8,128)}, u32[]{:S(2)}, u32[]{:S(2)}) %collective-permute-start.8) | collective-permute-done | bytes 4718624 | tf_op jit(solution)/shard_map/ppermute | solution.py:215
  167.6 3.9 %collective-permute-start.13 = (f32[2,8,9216]{2,1,0:T(8,128)S(1)}, f32[2,8,9216]{2,1,0:T(8,128)S(1)}, u32[]{:S(2)}, u32[]{:S(2)}) collective-permute-start(f32[2,8,9216]{2,1,0:T(8,128)S(1)} %get-tuple-element.11), channel_id=1, source_target_pairs={{1,0},{2,1},{3,2},{4,3},{5,4},{6,5},{7,6},{8,7},{9,8},{10,9},{11,1... | collective-permute-start | bytes 1769480 | tf_op jit(solution)/shard_map/ppermute | solution.py:216
  171.6 119.8 %local_part.1.image_ref = f32[3,128,9216]{2,1,0:T(8,128)} custom-call(f32[128,160]{1,0:T(8,128)S(1)} %pad_maximum_fusion.table_ref, f32[3,128,9216]{2,1,0:T(8,128)} %bitcast.9, f32[3,128,9216]{2,1,0:T(8,128)} %bitcast.10, f32[3,128,9216]{2,1,0:T(8,128)} %bitcast.11, f32[3,16,9216]{2,1,0:T(8,128)S(1)} %collective-permute-done.head_ref, ...), custom_call_target="tpu_custom_call" | custom-call | flops 6794772480 | bytes 28311552 | tf_op jit(solution)/shard_map/local_part/pallas_call | solution.py:130
  291.4 3.2 %add_edges.4.image_ref = f32[3,128,9216]{2,1,0:T(8,128)} custom-call(f32[3,128,9216]{2,1,0:T(8,128)} %local_part.1.image_ref, f32[2,16,9216]{2,1,0:T(8,128)} %collective-permute-done.6.below_ref, f32[2,16,9216]{2,1,0:T(8,128)} %collective-permute-done.7.above_ref), custom_call_target="tpu_custom_call", output_to_operand_aliasing={{}: (0, {})} | custom-call | flops 3538944 | bytes 5898240 | tf_op jit(solution)/shard_map/add_edges/pallas_call | solution.py:180
  294.6 10.4 %add_edges.5.image_ref = f32[3,128,9216]{2,1,0:T(8,128)} custom-call(f32[3,128,9216]{2,1,0:T(8,128)} %add_edges.4.image_ref, f32[2,64,9216]{2,1,0:T(8,128)} %collective-permute-done.8.below_ref, f32[2,64,9216]{2,1,0:T(8,128)} %collective-permute-done.9.above_ref), custom_call_target="tpu_custom_call", output_to_operand_aliasing={{}: (0, {})} | custom-call | flops 14155776 | bytes 23592960 | tf_op jit(solution)/shard_map/add_edges/pallas_call | solution.py:180
  305.0 7.4 %add_edges.6.image_ref = f32[3,128,9216]{2,1,0:T(8,128)} custom-call(f32[3,128,9216]{2,1,0:T(8,128)} %add_edges.5.image_ref, f32[2,40,9216]{2,1,0:T(8,128)} %collective-permute-done.10.below_ref, f32[2,40,9216]{2,1,0:T(8,128)} %collective-permute-done.11.above_ref), custom_call_target="tpu_custom_call", output_to_operand_aliasing={{}: (0, {})} | custom-call | flops 8847360 | bytes 14745600 | tf_op jit(solution)/shard_map/add_edges/pallas_call | solution.py:180
  314.1 3.6 %add_edges.7 = f32[3,128,9216]{2,1,0:T(8,128)} custom-call(f32[3,128,9216]{2,1,0:T(8,128)} %add_edges.6.image_ref, f32[2,8,9216]{2,1,0:T(8,128)} %copy-done.2, f32[2,8,9216]{2,1,0:T(8,128)} %copy-done.3), custom_call_target="tpu_custom_call", output_to_operand_aliasing={{}: (0, {})} | custom-call | flops 1769472 | bytes 2949120 | tf_op jit(solution)/shard_map/add_edges/pallas_call | solution.py:180
  (40 shorter events, 14.1 us)
Async XLA Ops:
  2.8 8.6 %copy-start.4 = (f32[16]{0:T(128)S(1)}, f32[16]{0:T(128)}, u32[]{:S(2)}) copy-start(f32[16]{0:T(128)} %param.6) | copy-start | bytes 196
  2.8 8.6 %copy-start.5 = (f32[16]{0:T(128)S(1)}, f32[16]{0:T(128)}, u32[]{:S(2)}) copy-start(f32[16]{0:T(128)} %param.7) | copy-start | bytes 196
  25.2 3.9 %collective-permute-start.1 = (f32[3,16,9216]{2,1,0:T(8,128)}, f32[3,16,9216]{2,1,0:T(8,128)S(1)}, u32[]{:S(2)}, u32[]{:S(2)}) collective-permute-start(f32[3,16,9216]{2,1,0:T(8,128)} %block_sums.1), channel_id=1, source_target_pairs={{0,16},{16,0},{32,48},{48,32},{64,80},{80,64},{96,112},{112,96},{1... | collective-permute-start | bytes 5308424 | tf_op jit(solution)/shard_map/ppermute | solution.py:230
  30.5 21.9 %collective-permute-start.2 = (f32[3,16,4608]{2,1,0:T(8,128)S(1)}, f32[3,16,4608]{2,1,0:T(8,128)S(1)}, u32[]{:S(2)}, u32[]{:S(2)}) collective-permute-start(f32[3,16,4608]{2,1,0:T(8,128)S(1)} %add_select_fusion.1), channel_id=1, source_target_pairs={{32,0},{48,16},{64,32},{80,48},{96,64},{112,80},{33,1},{49,17},{65... | collective-permute-start | bytes 2654216 | tf_op jit(solution)/shard_map/ppermute | solution.py:241
  33.3 70.0 %collective-permute-start.6 = (f32[2,16,9216]{2,1,0:T(8,128)}, f32[2,16,9216]{2,1,0:T(8,128)}, u32[]{:S(2)}, u32[]{:S(2)}) collective-permute-start(f32[2,16,9216]{2,1,0:T(8,128)} %get-tuple-element.18), channel_id=1, source_target_pairs={{0,1},{1,2},{2,3},{3,4},{4,5},{5,6},{6,7},{7,8},{8,9},{9,10},{10,1... | collective-permute-start | bytes 3538952 | tf_op jit(solution)/shard_map/ppermute | solution.py:215
  37.1 70.0 %collective-permute-start.7 = (f32[2,16,9216]{2,1,0:T(8,128)S(1)}, f32[2,16,9216]{2,1,0:T(8,128)}, u32[]{:S(2)}, u32[]{:S(2)}) collective-permute-start(f32[2,16,9216]{2,1,0:T(8,128)S(1)} %get-tuple-element.17), channel_id=1, source_target_pairs={{1,0},{2,1},{3,2},{4,3},{5,4},{6,5},{7,6},{8,7},{9,8},{10,9},{11,1... | collective-permute-start | bytes 3538952 | tf_op jit(solution)/shard_map/ppermute | solution.py:216
  41.3 126.3 %collective-permute-start.8 = (f32[2,64,9216]{2,1,0:T(8,128)}, f32[2,64,9216]{2,1,0:T(8,128)}, u32[]{:S(2)}, u32[]{:S(2)}) collective-permute-start(f32[2,64,9216]{2,1,0:T(8,128)} %get-tuple-element.16), channel_id=1, source_target_pairs={{0,1},{1,2},{2,3},{3,4},{4,5},{5,6},{6,7},{7,8},{8,9},{9,10},{10,1... | collective-permute-start | bytes 14155784 | tf_op jit(solution)/shard_map/ppermute | solution.py:215
  43.3 251.3 %collective-permute-start.9 = (f32[2,64,9216]{2,1,0:T(8,128)}, f32[2,64,9216]{2,1,0:T(8,128)}, u32[]{:S(2)}, u32[]{:S(2)}) collective-permute-start(f32[2,64,9216]{2,1,0:T(8,128)} %get-tuple-element.15), channel_id=1, source_target_pairs={{1,0},{2,1},{3,2},{4,3},{5,4},{6,5},{7,6},{8,7},{9,8},{10,9},{11,1... | collective-permute-start | bytes 14155784 | tf_op jit(solution)/shard_map/ppermute | solution.py:216
  52.6 22.8 %collective-permute-start.3 = (f32[3,16,4608]{2,1,0:T(8,128)S(1)}, f32[3,16,4608]{2,1,0:T(8,128)S(1)}, u32[]{:S(2)}, u32[]{:S(2)}) collective-permute-start(f32[3,16,4608]{2,1,0:T(8,128)S(1)} %multiply_add_fusion.1), channel_id=1, source_target_pairs={{32,0},{48,16},{64,32},{80,48},{96,64},{112,80},{33,1},{49,17},{65... | collective-permute-start | bytes 2654216 | tf_op jit(solution)/shard_map/ppermute | solution.py:241
  76.5 22.4 %collective-permute-start.4 = (f32[3,16,4608]{2,1,0:T(8,128)}, f32[3,16,4608]{2,1,0:T(8,128)}, u32[]{:S(2)}, u32[]{:S(2)}) collective-permute-start(f32[3,16,4608]{2,1,0:T(8,128)} %multiply_add_fusion), channel_id=1, source_target_pairs={{32,0},{48,16},{64,32},{80,48},{96,64},{112,80},{33,1},{49,17},{65... | collective-permute-start | bytes 2654216 | tf_op jit(solution)/shard_map/ppermute | solution.py:241
  98.9 14.2 %collective-permute-start.5 = (f32[3,16,4608]{2,1,0:T(8,128)}, f32[3,16,4608]{2,1,0:T(8,128)}, u32[]{:S(2)}, u32[]{:S(2)}) collective-permute-start(f32[3,16,4608]{2,1,0:T(8,128)} %collective-permute-done.4), channel_id=1, source_target_pairs={{0,16},{16,0},{32,48},{48,32},{64,80},{80,64},{96,112},{112,96},{1... | collective-permute-start | bytes 2654216 | tf_op jit(solution)/shard_map/ppermute | solution.py:242
  103.2 201.7 %collective-permute-start.10 = (f32[2,40,9216]{2,1,0:T(8,128)}, f32[2,40,9216]{2,1,0:T(8,128)}, u32[]{:S(2)}, u32[]{:S(2)}) collective-permute-start(f32[2,40,9216]{2,1,0:T(8,128)} %get-tuple-element.14), channel_id=1, source_target_pairs={{0,1},{1,2},{2,3},{3,4},{4,5},{5,6},{6,7},{7,8},{8,9},{9,10},{10,1... | collective-permute-start | bytes 8847368 | tf_op jit(solution)/shard_map/ppermute | solution.py:215
  107.1 197.9 %collective-permute-start.11 = (f32[2,40,9216]{2,1,0:T(8,128)}, f32[2,40,9216]{2,1,0:T(8,128)}, u32[]{:S(2)}, u32[]{:S(2)}) collective-permute-start(f32[2,40,9216]{2,1,0:T(8,128)} %get-tuple-element.13), channel_id=1, source_target_pairs={{1,0},{2,1},{3,2},{4,3},{5,4},{6,5},{7,6},{8,7},{9,8},{10,9},{11,1... | collective-permute-start | bytes 8847368 | tf_op jit(solution)/shard_map/ppermute | solution.py:216
  113.1 24.4 %copy-start.1 = (f32[2,8,9216]{2,1,0:T(8,128)S(1)}, f32[2,8,9216]{2,1,0:T(8,128)}, u32[]{:S(2)}) copy-start(f32[2,8,9216]{2,1,0:T(8,128)} %get-tuple-element.12) | copy-start | bytes 1769476
  113.1 58.4 %copy-start = (f32[3,9216]{1,0:T(4,128)S(1)}, f32[3,9216]{1,0:T(4,128)}, u32[]{:S(2)}) copy-start(f32[3,9216]{1,0:T(4,128)} %absorb_ref.1) | copy-start | bytes 331780
  113.1 24.4 %collective-permute-start = (f32[3,16,9216]{2,1,0:T(8,128)S(1)}, f32[3,16,9216]{2,1,0:T(8,128)S(1)}, u32[]{:S(2)}, u32[]{:S(2)}) collective-permute-start(f32[3,16,9216]{2,1,0:T(8,128)S(1)} %slice.35), channel_id=1, source_target_pairs={{16,0},{32,16},{48,32},{64,48},{80,64},{96,80},{112,96},{17,1},{33... | collective-permute-start | bytes 5308424 | tf_op jit(solution)/shard_map/ppermute | solution.py:226
  137.5 174.9 %collective-permute-start.12 = (f32[2,8,9216]{2,1,0:T(8,128)S(1)}, f32[2,8,9216]{2,1,0:T(8,128)S(1)}, u32[]{:S(2)}, u32[]{:S(2)}) collective-permute-start(f32[2,8,9216]{2,1,0:T(8,128)S(1)} %copy-done.1), channel_id=1, source_target_pairs={{0,1},{1,2},{2,3},{3,4},{4,5},{5,6},{6,7},{7,8},{8,9},{9,10},{10,1... | collective-permute-start | bytes 1769480 | tf_op jit(solution)/shard_map/ppermute | solution.py:215
  167.6 144.8 %collective-permute-start.13 = (f32[2,8,9216]{2,1,0:T(8,128)S(1)}, f32[2,8,9216]{2,1,0:T(8,128)S(1)}, u32[]{:S(2)}, u32[]{:S(2)}) collective-permute-start(f32[2,8,9216]{2,1,0:T(8,128)S(1)} %get-tuple-element.11), channel_id=1, source_target_pairs={{1,0},{2,1},{3,2},{4,3},{5,4},{6,5},{7,6},{8,7},{9,8},{10,9},{11,1... | collective-permute-start | bytes 1769480 | tf_op jit(solution)/shard_map/ppermute | solution.py:216
  312.4 0.8 copy-start.2
  313.2 0.8 copy-start.3

commit v2 on v1

--- a/solution.py
+++ b/solution.py
@@ -12,8 +12,8 @@
 ORDER_EXP = 0.4
 EDGE = 256
 TILE = 2304
-CHUNKS = (16, 64, 40, 8)
-EXACT = lax.Precision.HIGHEST
+SPAN = 768
+CHUNKS = (16, 24, 56, 24, 8)
 
 
 def caputo_weights(count):
@@ -46,10 +46,24 @@
     return table, projector
 
 
+def parts(value):
+    high = value.astype(jnp.bfloat16)
+    return high, (value - high.astype(jnp.float32)).astype(jnp.bfloat16)
+
+
+def product(weights, high, low):
+    rows = weights.shape[0]
+    upper, lower = parts(weights)
+    both = jnp.dot(
+        jnp.concatenate([upper, lower], axis=0), high, preferred_element_type=jnp.float32
+    )
+    rest = jnp.dot(upper, low, preferred_element_type=jnp.float32)
+    return both[:rows] + both[rows:] + rest
+
+
 def project_kernel(projector_ref, field_ref, out_ref):
-    out_ref[0] = jnp.dot(
-        projector_ref[...], field_ref[0], precision=EXACT, preferred_element_type=jnp.float32
-    )
+    high, low = parts(field_ref[0])
+    out_ref[0] = product(projector_ref[...], high, low)
 
 
 def block_sums(projector, field):
@@ -65,7 +79,7 @@
         ],
         out_specs=pl.BlockSpec((1, modes, TILE), lambda p, i: (p, 0, i)),
         cost_estimate=pl.CostEstimate(
-            flops=12 * modes * steps * depth * plane,
+            flops=6 * modes * steps * depth * plane,
             bytes_accessed=4 * depth * plane * (steps + modes),
             transcendentals=0,
         ),
@@ -73,66 +87,95 @@
     )(projector, field)
 
 
+def stencil_bands():
+    shape = (SPAN // EDGE, SPAN, EDGE)
+    lane_out = lax.broadcasted_iota(jnp.int32, shape, 2)
+    offset = lax.broadcasted_iota(jnp.int32, shape, 1) - EDGE - lane_out
+    column = (lax.broadcasted_iota(jnp.int32, shape, 0) * EDGE + lane_out) % NY
+    inside = (column + offset >= 0) & (column + offset < NY)
+    size = jnp.abs(offset)
+    near = (size == NY) | ((size == 1) & inside)
+    far = (size == 2 * NY) | ((size == 2) & inside)
+    return jnp.where(near, 16.0, jnp.where(far, -1.0, 0.0)).astype(jnp.bfloat16)
+
+
 def local_kernel(
-    table_ref, left_ref, mid_ref, right_ref, head_ref, carried_ref, absorb_ref, out_ref, wide, masks
+    table_ref,
+    bands_ref,
+    left_ref,
+    mid_ref,
+    right_ref,
+    head_ref,
+    carried_ref,
+    absorb_ref,
+    out_ref,
+    high_ref,
+    low_ref,
 ):
     depth, steps, width = mid_ref.shape
     spot, spots = pl.program_id(0), pl.num_programs(0)
-    column = lax.broadcasted_iota(jnp.int32, (8, width), 1) % NY
-    for k, offset in enumerate((-2, -1, 1, 2)):
-        good = (column + offset >= 0) & (column + offset < NY)
-        masks[k] = jnp.where(good, 16.0 if offset in (-1, 1) else -1.0, 0.0)
     has_left = jnp.where(spot > 0, 1.0, 0.0)
     has_right = jnp.where(spot < spots - 1, 1.0, 0.0)
     factor = -DIFFUSION / 12.0
+    table = table_ref[...]
+
+    def put(p, rows, lanes, value):
+        high, low = parts(value)
+        high_ref[p, rows, lanes] = high
+        low_ref[p, rows, lanes] = low
+
+    own, ahead, later = slice(0, steps), slice(steps, steps + BAND), slice(steps + BAND, None)
+    inner = slice(EDGE, EDGE + width)
     for p in range(depth):
-        wide[0:steps, 0:EDGE] = left_ref[p] * has_left
-        wide[0:steps, EDGE : EDGE + width] = mid_ref[p]
-        wide[0:steps, EDGE + width :] = right_ref[p] * has_right
-        wide[steps : steps + BAND, EDGE : EDGE + width] = head_ref[p]
-        wide[steps + BAND :, EDGE : EDGE + width] = carried_ref[p]
-        out_ref[p] = jnp.dot(
-            table_ref[...],
-            wide[:, EDGE : EDGE + width],
-            precision=EXACT,
-            preferred_element_type=jnp.float32,
-        )
-        absorb = jnp.broadcast_to(absorb_ref[pl.ds(p, 1), :], (8, width)) - 90.0 * factor
-
-        def some_steps(t, _, p=p, absorb=absorb):
-            rows = pl.ds(pl.multiple_of(t * 8, 8), 8)
-
-            def at(offset):
-                return wide[rows, EDGE + offset : EDGE + offset + width]
-
-            center = mid_ref[p, rows, :]
-            near = at(-NY) + at(NY)
-            far = at(-2 * NY) + at(2 * NY)
+        put(p, own, slice(0, EDGE), left_ref[p] * has_left)
+        put(p, own, inner, mid_ref[p])
+        put(p, own, slice(EDGE + width, None), right_ref[p] * has_right)
+        put(p, ahead, inner, head_ref[p])
+        put(p, later, inner, carried_ref[p])
+
+    def one_span(g, _):
+        base = pl.multiple_of(g * SPAN, SPAN)
+        span = pl.ds(base, SPAN)
+        inner_span = pl.ds(pl.multiple_of(base + EDGE, EDGE), SPAN)
+        for p in range(depth):
+            total = product(table, high_ref[p, :, inner_span], low_ref[p, :, inner_span])
+            near, far = 0.0, 0.0
             for q in range(depth):
                 if abs(q - p) == 1:
-                    near = near + mid_ref[q, rows, :]
+                    near = near + mid_ref[q, :, span]
                 if abs(q - p) == 2:
-                    far = far + mid_ref[q, rows, :]
-            total = 16.0 * near - far
-            for k, offset in enumerate((-2, -1, 1, 2)):
-                total = total + masks[k] * at(offset)
-            out_ref[p, rows, :] = out_ref[p, rows, :] + absorb * center + factor * total
-            return 0
-
-        lax.fori_loop(0, steps // 8, some_steps, 0)
-
-
-def local_part(table, field, head, carried, absorption):
+                    far = far + mid_ref[q, :, span]
+            scale = absorb_ref[pl.ds(p, 1), span] - 90.0 * factor
+            out_ref[p, :, span] = (
+                total + scale * mid_ref[p, :, span] + factor * (16.0 * near - far)
+            )
+        for k in range(SPAN // EDGE):
+            window = pl.ds(pl.multiple_of(base + k * EDGE, EDGE), SPAN)
+            tile = pl.ds(pl.multiple_of(base + k * EDGE, EDGE), EDGE)
+            high = jnp.concatenate([high_ref[p, own, window] for p in range(depth)], axis=0)
+            low = jnp.concatenate([low_ref[p, own, window] for p in range(depth)], axis=0)
+            around = jnp.dot(high, bands_ref[k], preferred_element_type=jnp.float32)
+            around = around + jnp.dot(low, bands_ref[k], preferred_element_type=jnp.float32)
+            for p in range(depth):
+                out_ref[p, :, tile] += factor * around[p * steps : (p + 1) * steps]
+        return 0
+
+    lax.fori_loop(0, width // SPAN, one_span, 0)
+
+
+def local_part(table, bands, field, head, carried, absorption):
     depth, steps, plane = field.shape
     per = TILE // EDGE
     last = plane // EDGE - 1
     cols = table.shape[1]
+    wide = (depth, cols, TILE + 2 * EDGE)
     return pl.pallas_call(
         local_kernel,
         out_shape=jax.ShapeDtypeStruct(field.shape, jnp.float32),
         grid=(plane // TILE,),
         in_specs=[
             pl.BlockSpec((steps, cols), lambda i: (0, 0)),
+            pl.BlockSpec(bands.shape, lambda i: (0, 0, 0)),
             pl.BlockSpec((depth, steps, EDGE), lambda i: (0, 0, jnp.maximum(i * per - 1, 0))),
             pl.BlockSpec((depth, steps, TILE), lambda i: (0, 0, i)),
             pl.BlockSpec((depth, steps, EDGE), lambda i: (0, 0, jnp.minimum(i * per + per, last))),
@@ -141,18 +184,15 @@
             pl.BlockSpec((depth, TILE), lambda i: (0, i)),
         ],
         out_specs=pl.BlockSpec((depth, steps, TILE), lambda i: (0, 0, i)),
-        scratch_shapes=[
-            pltpu.VMEM((cols, TILE + 2 * EDGE), jnp.float32),
-            pltpu.VMEM((4, 8, TILE), jnp.float32),
-        ],
+        scratch_shapes=[pltpu.VMEM(wide, jnp.bfloat16), pltpu.VMEM(wide, jnp.bfloat16)],
         compiler_params=pltpu.CompilerParams(vmem_limit_bytes=48 * 1024 * 1024),
         cost_estimate=pl.CostEstimate(
-            flops=12 * cols * steps * depth * plane,
+            flops=6 * cols * steps * depth * plane,
             bytes_accessed=8 * depth * plane * steps,
             transcendentals=0,
         ),
         name="local_part",
-    )(table, field, field, field, head, carried, absorption)
+    )(table, bands, field, field, field, head, carried, absorption)
 
 
 def edge_kernel(image_ref, below_ref, above_ref, out_ref):
@@ -215,7 +255,7 @@
         below.append(lax.ppermute(high, "space", up))
         above.append(lax.ppermute(low, "space", down))
         source, _, _ = lax.optimization_barrier((source, high, low))
-        if len(starts) == 2:
+        if len(starts) == 1:
             early = source
         first += count
 
@@ -223,7 +263,8 @@
     mode_gain = mode_weights * jnp.sqrt(-jnp.expm1(-2.0 * scaled))
     table, projector = history_tables(scaled, mode_gain, steps)
 
-    head = lax.ppermute(early[:, :BAND], "tm", [(g + 1, g) for g in range(groups - 1)])
+    mine_first = early[:, :BAND]
+    head = lax.ppermute(mine_first, "tm", [(g + 1, g) for g in range(groups - 1)])
     sums = block_sums(projector, early)
     decay = jnp.exp(-scaled * steps)[None, :, None]
     swap = [(g, g + 1 - 2 * (g % 2)) for g in range(groups)]
@@ -247,7 +288,7 @@
     )
     carried = jnp.where(core == 0, other + decay * later_full, later_full)
 
-    image = local_part(table, field, head, carried, absorption)
+    image = local_part(table, stencil_bands(), field, head, carried, absorption)
     for first, lower, upper in zip(starts, below, above):
         count = lower.shape[1]
         image = add_edges(image, lower, upper, first, 8, plane if count > 8 else TILE)

time: 319 us -> 284 us (0.89)
  the two profiles are of different devices: /device:TPU:30 before, /device:TPU:1 now
where the time goes in v2:
time: 284 us; the launch traced here: 278 us
  waiting for transfers between devices  122 us (43%)
  Pallas kernels  65.8 us (23%)
  starting transfers between devices  41 us (14%)
  local copies, waits for them, and re-layouts  32 us (11%)
  other arithmetic  17.3 us (6%)
    ppermute x5, waiting for transfers between devices, per_device(): below.append(lax.ppermute(high, 'space', up))  46.8 us
    ppermute x3, waiting for transfers between devices, per_device(): later = lax.ppermute(sent, 'tm', [(g + 2, g) for g in range(groups - 2)])  38.6 us
    ppermute x5, waiting for transfers between devices, per_device(): above.append(lax.ppermute(low, 'space', down))  36.9 us
    pallas_call x1, Pallas kernels, local_part(): pl.pallas_call(local_kernel, out_shape=jax.ShapeDtypeStruct(field.shape,...  27.8 us
    pallas_call x5, Pallas kernels, add_edges(): pl.pallas_call(edge_kernel, out_shape=jax.ShapeDtypeStruct(image.shape, j...  26.6 us
    ppermute x5, starting transfers between devices, per_device(): below.append(lax.ppermute(high, 'space', up))  24.2 us
    slice x5, local copies, waits for them, and re-layouts, per_device(): low = source[:2, first:first + count]  21.4 us
    pallas_call x1, Pallas kernels, block_sums(): pl.pallas_call(project_kernel, out_shape=jax.ShapeDtypeStruct((depth, mod...  11.4 us
  transfers between devices with their start and end apart: 16, of which 7 were waited for; matrix products, arithmetic and copies ran while one was open for 16% of the time, Pallas kernels for 22%

profile of v2, /device:TPU:1, one launch (start us, length us, event | category | flops | bytes accessed | tf_op | source)
XLA Modules:
  0.0 278.5 jit_solution(10076324118188845057)
XLA Ops:
  0.0 3.2 %fusion.28 = (f32[2,16,9216]{2,1,0:T(8,128)}, f32[2,16,9216]{2,1,0:T(8,128)}) fusion(f32[3,128,9216]{2,1,0:T(8,128)} %bitcast.3), kind=kLoop, calls=%fused_computation.56 | loop fusion | bytes 4718592 | tf_op jit(solution)/shard_map/slice | solution.py:254
  3.2 5.4 %collective-permute-start.6 = (f32[2,16,9216]{2,1,0:T(8,128)}, f32[2,16,9216]{2,1,0:T(8,128)}, u32[]{:S(2)}, u32[]{:S(2)}) collective-permute-start(f32[2,16,9216]{2,1,0:T(8,128)} %get-tuple-element.22), channel_id=1, source_target_pairs={{0,1},{1,2},{2,3},{3,4},{4,5},{5,6},{6,7},{7,8},{8,9},{9,10},{10,1... | collective-permute-start | bytes 3538952 | tf_op jit(solution)/shard_map/ppermute | solution.py:255
  10.0 2.9 %slice.39 = f32[3,16,9216]{2,1,0:T(8,128)} slice(f32[3,128,9216]{2,1,0:T(8,128)} %bitcast.4), slice={[0:3], [0:16], [0:9216]} | slice | bytes 3538944 | tf_op jit(solution)/shard_map/slice | solution.py:266
  12.9 2.9 %collective-permute-start = (f32[3,16,9216]{2,1,0:T(8,128)}, f32[3,16,9216]{2,1,0:T(8,128)S(1)}, u32[]{:S(2)}, u32[]{:S(2)}) collective-permute-start(f32[3,16,9216]{2,1,0:T(8,128)} %slice.39), channel_id=1, source_target_pairs={{16,0},{32,16},{48,32},{64,48},{80,64},{96,80},{112,96},{17,1},{33... | collective-permute-start | bytes 5308424 | tf_op jit(solution)/shard_map/ppermute | solution.py:267
  16.5 11.4 %block_sums.1 = f32[3,16,9216]{2,1,0:T(8,128)} custom-call(f32[16,128]{1,0:T(8,128)} %multiply_exponential_fusion.projector_ref, f32[3,128,9216]{2,1,0:T(8,128)} %bitcast.5), custom_call_target="tpu_custom_call" | custom-call | flops 339738624 | bytes 15925248 | tf_op jit(solution)/shard_map/block_sums/pallas_call | solution.py:72
  27.9 4.0 %fusion.27 = (f32[2,24,9216]{2,1,0:T(8,128)}, f32[2,24,9216]{2,1,0:T(8,128)}) fusion(f32[3,128,9216]{2,1,0:T(8,128)} %bitcast.6), kind=kLoop, calls=%fused_computation.55 | loop fusion | bytes 7077888 | tf_op jit(solution)/shard_map/slice | solution.py:254
  31.9 7.8 %fusion.26 = (f32[2,56,9216]{2,1,0:T(8,128)}, f32[2,56,9216]{2,1,0:T(8,128)}) fusion(f32[3,128,9216]{2,1,0:T(8,128)} %bitcast.7), kind=kLoop, calls=%fused_computation.54 | loop fusion | bytes 16515072 | tf_op jit(solution)/shard_map/slice | solution.py:254
  39.7 6.2 %collective-permute-start.10 = (f32[2,56,9216]{2,1,0:T(8,128)}, f32[2,56,9216]{2,1,0:T(8,128)}, u32[]{:S(2)}, u32[]{:S(2)}) collective-permute-start(f32[2,56,9216]{2,1,0:T(8,128)} %get-tuple-element.18), channel_id=1, source_target_pairs={{0,1},{1,2},{2,3},{3,4},{4,5},{5,6},{6,7},{7,8},{8,9},{9,10},{10,1... | collective-permute-start | bytes 12386312 | tf_op jit(solution)/shard_map/ppermute | solution.py:255
  48.6 4.0 %fusion.25 = (f32[2,24,9216]{2,1,0:T(8,128)}, f32[2,24,9216]{2,1,0:T(8,128)}) fusion(f32[3,128,9216]{2,1,0:T(8,128)} %bitcast.8), kind=kLoop, calls=%fused_computation.53 | loop fusion | bytes 7077888 | tf_op jit(solution)/shard_map/slice | solution.py:254
  52.6 17.0 %collective-permute-done.2 = f32[3,16,4608]{2,1,0:T(8,128)S(1)} collective-permute-done((f32[3,16,4608]{2,1,0:T(8,128)S(1)}, f32[3,16,4608]{2,1,0:T(8,128)S(1)}, u32[]{:S(2)}, u32[]{:S(2)}) %collective-permute-start.2) | collective-permute-done | bytes 884768 | tf_op jit(solution)/shard_map/ppermute | solution.py:282
  71.1 2.3 fusion.24
  75.3 15.9 %collective-permute-done.3 = f32[3,16,4608]{2,1,0:T(8,128)S(1)} collective-permute-done((f32[3,16,4608]{2,1,0:T(8,128)S(1)}, f32[3,16,4608]{2,1,0:T(8,128)S(1)}, u32[]{:S(2)}, u32[]{:S(2)}) %collective-permute-start.3) | collective-permute-done | bytes 884768 | tf_op jit(solution)/shard_map/ppermute | solution.py:282
  93.6 2.5 collective-permute-start.8
  99.3 1.6 copy.16
  102.6 1.7 select_reduce_fusion
  104.3 1.8 multiply_reduce_fusion
  107.5 5.7 %collective-permute-done.4 = f32[3,16,4608]{2,1,0:T(8,128)} collective-permute-done((f32[3,16,4608]{2,1,0:T(8,128)}, f32[3,16,4608]{2,1,0:T(8,128)}, u32[]{:S(2)}, u32[]{:S(2)}) %collective-permute-start.4) | collective-permute-done | bytes 884768 | tf_op jit(solution)/shard_map/ppermute | solution.py:282
  113.2 3.4 %collective-permute-start.5 = (f32[3,16,4608]{2,1,0:T(8,128)}, f32[3,16,4608]{2,1,0:T(8,128)}, u32[]{:S(2)}, u32[]{:S(2)}) collective-permute-start(f32[3,16,4608]{2,1,0:T(8,128)} %collective-permute-done.4), channel_id=1, source_target_pairs={{0,16},{16,0},{32,48},{48,32},{64,80},{80,64},{96,112},{112,96},{1... | collective-permute-start | bytes 2654216 | tf_op jit(solution)/shard_map/ppermute | solution.py:283
  116.6 1.6 copy.19
  123.4 46.8 %collective-permute-done.8.below_ref = f32[2,24,9216]{2,1,0:T(8,128)} collective-permute-done((f32[2,24,9216]{2,1,0:T(8,128)}, f32[2,24,9216]{2,1,0:T(8,128)}, u32[]{:S(2)}, u32[]{:S(2)}) %collective-permute-start.8) | collective-permute-done | bytes 1769504 | tf_op jit(solution)/shard_map/ppermute | solution.py:255
  170.2 5.3 %collective-permute-start.12 = (f32[2,24,9216]{2,1,0:T(8,128)}, f32[2,24,9216]{2,1,0:T(8,128)}, u32[]{:S(2)}, u32[]{:S(2)}) collective-permute-start(f32[2,24,9216]{2,1,0:T(8,128)} %get-tuple-element.16), channel_id=1, source_target_pairs={{0,1},{1,2},{2,3},{3,4},{4,5},{5,6},{6,7},{7,8},{8,9},{9,10},{10,1... | collective-permute-start | bytes 5308424 | tf_op jit(solution)/shard_map/ppermute | solution.py:255
  176.8 4.8 %collective-permute-start.14 = (f32[2,8,9216]{2,1,0:T(8,128)}, f32[2,8,9216]{2,1,0:T(8,128)}, u32[]{:S(2)}, u32[]{:S(2)}) collective-permute-start(f32[2,8,9216]{2,1,0:T(8,128)} %get-tuple-element.14), channel_id=1, source_target_pairs={{0,1},{1,2},{2,3},{3,4},{4,5},{5,6},{6,7},{7,8},{8,9},{9,10},{10,1... | collective-permute-start | bytes 1769480 | tf_op jit(solution)/shard_map/ppermute | solution.py:255
  183.0 2.9 %add_select_fusion.1.carried_ref = f32[3,16,9216]{2,1,0:T(8,128)S(1)} fusion(f32[3,16,9216]{2,1,0:T(8,128)} %collective-permute-done.1, f32[3,16,4608]{2,1,0:T(8,128)} %collective-permute-done.4, f32[3,16,4608]{2,1,0:T(8,128)} %collective-permute-done.5, f32[16]{0:T(128)S(1)} %get-tuple-element.24, pred[]{:T(512)S(6)} %eq.53), kind=kLoop, calls=%fused_computation.22 | loop fusion | flops 2654208 | bytes 5308481 | tf_op jit(solution)/shard_map/jit(_where)/select_n | solution.py:289
  186.0 27.8 %local_part.1.image_ref = f32[3,128,9216]{2,1,0:T(8,128)} custom-call(f32[128,160]{1,0:T(8,128)S(1)} %pad_maximum_fusion.table_ref, bf16[3,768,256]{2,1,0:T(8,128)(2,1)S(1)} %select_convert_fusion.bands_ref, f32[3,128,9216]{2,1,0:T(8,128)} %bitcast.10, f32[3,128,9216]{2,1,0:T(8,128)} %bitcast.11, f32[3,128,9216]{2,1,0:T(8,128)} %bitcast.12, ...), custom_call_target="tpu_custom_call" | custom-call | flops 3397386240 | bytes 28311552 | tf_op jit(solution)/shard_map/local_part/pallas_call | solution.py:172
  213.8 3.2 %add_edges.5.image_ref = f32[3,128,9216]{2,1,0:T(8,128)} custom-call(f32[3,128,9216]{2,1,0:T(8,128)} %local_part.1.image_ref, f32[2,16,9216]{2,1,0:T(8,128)} %collective-permute-done.6.below_ref, f32[2,16,9216]{2,1,0:T(8,128)} %collective-permute-done.7.above_ref), custom_call_target="tpu_custom_call", output_to_operand_aliasing={{}: (0, {})} | custom-call | flops 3538944 | bytes 5898240 | tf_op jit(solution)/shard_map/add_edges/pallas_call | solution.py:220
  217.0 5.0 %add_edges.6.image_ref = f32[3,128,9216]{2,1,0:T(8,128)} custom-call(f32[3,128,9216]{2,1,0:T(8,128)} %add_edges.5.image_ref, f32[2,24,9216]{2,1,0:T(8,128)} %collective-permute-done.8.below_ref, f32[2,24,9216]{2,1,0:T(8,128)} %collective-permute-done.9.above_ref), custom_call_target="tpu_custom_call", output_to_operand_aliasing={{}: (0, {})} | custom-call | flops 5308416 | bytes 8847360 | tf_op jit(solution)/shard_map/add_edges/pallas_call | solution.py:220
  222.0 2.4 collective-permute-done.11.above_ref
  224.3 9.8 %add_edges.7.image_ref = f32[3,128,9216]{2,1,0:T(8,128)} custom-call(f32[3,128,9216]{2,1,0:T(8,128)} %add_edges.6.image_ref, f32[2,56,9216]{2,1,0:T(8,128)} %collective-permute-done.10.below_ref, f32[2,56,9216]{2,1,0:T(8,128)} %collective-permute-done.11.above_ref), custom_call_target="tpu_custom_call", output_to_operand_aliasing={{}: (0, {})} | custom-call | flops 12386304 | bytes 20643840 | tf_op jit(solution)/shard_map/add_edges/pallas_call | solution.py:220
  234.1 28.0 %collective-permute-done.13.above_ref = f32[2,24,9216]{2,1,0:T(8,128)S(1)} collective-permute-done((f32[2,24,9216]{2,1,0:T(8,128)}, f32[2,24,9216]{2,1,0:T(8,128)S(1)}, u32[]{:S(2)}, u32[]{:S(2)}) %collective-permute-start.13) | collective-permute-done | bytes 1769504 | tf_op jit(solution)/shard_map/ppermute | solution.py:256
  263.4 5.0 %add_edges.8.image_ref = f32[3,128,9216]{2,1,0:T(8,128)} custom-call(f32[3,128,9216]{2,1,0:T(8,128)} %add_edges.7.image_ref, f32[2,24,9216]{2,1,0:T(8,128)} %collective-permute-done.12.below_ref, f32[2,24,9216]{2,1,0:T(8,128)} %copy-done.3), custom_call_target="tpu_custom_call", output_to_operand_aliasing={{}: (0, {})} | custom-call | flops 5308416 | bytes 8847360 | tf_op jit(solution)/shard_map/add_edges/pallas_call | solution.py:220
  268.4 6.5 %collective-permute-done.15.above_ref = f32[2,8,9216]{2,1,0:T(8,128)} collective-permute-done((f32[2,8,9216]{2,1,0:T(8,128)}, f32[2,8,9216]{2,1,0:T(8,128)}, u32[]{:S(2)}, u32[]{:S(2)}) %collective-permute-start.15) | collective-permute-done | bytes 589856 | tf_op jit(solution)/shard_map/ppermute | solution.py:256
  274.9 3.6 %add_edges.9 = f32[3,128,9216]{2,1,0:T(8,128)} custom-call(f32[3,128,9216]{2,1,0:T(8,128)} %add_edges.8.image_ref, f32[2,8,9216]{2,1,0:T(8,128)} %collective-permute-done.14.below_ref, f32[2,8,9216]{2,1,0:T(8,128)} %collective-permute-done.15.above_ref), custom_call_target="tpu_custom_call", output_to_operand_aliasing={{}: (0, {})} | custom-call | flops 1769472 | bytes 2949120 | tf_op jit(solution)/shard_map/add_edges/pallas_call | solution.py:220
  (49 shorter events, 25.9 us)
Async XLA Ops:
  3.2 90.4 %collective-permute-start.6 = (f32[2,16,9216]{2,1,0:T(8,128)}, f32[2,16,9216]{2,1,0:T(8,128)}, u32[]{:S(2)}, u32[]{:S(2)}) collective-permute-start(f32[2,16,9216]{2,1,0:T(8,128)} %get-tuple-element.22), channel_id=1, source_target_pairs={{0,1},{1,2},{2,3},{3,4},{4,5},{5,6},{6,7},{7,8},{8,9},{9,10},{10,1... | collective-permute-start | bytes 3538952 | tf_op jit(solution)/shard_map/ppermute | solution.py:255
  8.6 7.1 %copy-start.4 = (f32[16]{0:T(128)S(1)}, f32[16]{0:T(128)}, u32[]{:S(2)}) copy-start(f32[16]{0:T(128)} %param.6) | copy-start | bytes 196
  8.6 7.2 %copy-start.5 = (f32[16]{0:T(128)S(1)}, f32[16]{0:T(128)}, u32[]{:S(2)}) copy-start(f32[16]{0:T(128)} %param.7) | copy-start | bytes 196
  8.6 87.5 %collective-permute-start.7 = (f32[2,16,9216]{2,1,0:T(8,128)}, f32[2,16,9216]{2,1,0:T(8,128)}, u32[]{:S(2)}, u32[]{:S(2)}) collective-permute-start(f32[2,16,9216]{2,1,0:T(8,128)} %get-tuple-element.21), channel_id=1, source_target_pairs={{1,0},{2,1},{3,2},{4,3},{5,4},{6,5},{7,6},{8,7},{9,8},{10,9},{11,1... | collective-permute-start | bytes 3538952 | tf_op jit(solution)/shard_map/ppermute | solution.py:256
  12.9 84.6 %collective-permute-start = (f32[3,16,9216]{2,1,0:T(8,128)}, f32[3,16,9216]{2,1,0:T(8,128)S(1)}, u32[]{:S(2)}, u32[]{:S(2)}) collective-permute-start(f32[3,16,9216]{2,1,0:T(8,128)} %slice.39), channel_id=1, source_target_pairs={{16,0},{32,16},{48,32},{64,48},{80,64},{96,80},{112,96},{17,1},{33... | collective-permute-start | bytes 5308424 | tf_op jit(solution)/shard_map/ppermute | solution.py:267
  27.9 18.0 %collective-permute-start.1 = (f32[3,16,9216]{2,1,0:T(8,128)}, f32[3,16,9216]{2,1,0:T(8,128)}, u32[]{:S(2)}, u32[]{:S(2)}) collective-permute-start(f32[3,16,9216]{2,1,0:T(8,128)} %block_sums.1), channel_id=1, source_target_pairs={{0,16},{16,0},{32,48},{48,32},{64,80},{80,64},{96,112},{112,96},{1... | collective-permute-start | bytes 5308424 | tf_op jit(solution)/shard_map/ppermute | solution.py:271
  31.9 14.0 %copy-start.1 = (f32[3,16,9216]{2,1,0:T(8,128)S(1)}, f32[3,16,9216]{2,1,0:T(8,128)}, u32[]{:S(2)}) copy-start(f32[3,16,9216]{2,1,0:T(8,128)} %block_sums.1) | copy-start | bytes 5308420
  39.7 137.1 %collective-permute-start.10 = (f32[2,56,9216]{2,1,0:T(8,128)}, f32[2,56,9216]{2,1,0:T(8,128)}, u32[]{:S(2)}, u32[]{:S(2)}) collective-permute-start(f32[2,56,9216]{2,1,0:T(8,128)} %get-tuple-element.18), channel_id=1, source_target_pairs={{0,1},{1,2},{2,3},{3,4},{4,5},{5,6},{6,7},{7,8},{8,9},{9,10},{10,1... | collective-permute-start | bytes 12386312 | tf_op jit(solution)/shard_map/ppermute | solution.py:255
  47.3 22.3 %collective-permute-start.2 = (f32[3,16,4608]{2,1,0:T(8,128)S(1)}, f32[3,16,4608]{2,1,0:T(8,128)S(1)}, u32[]{:S(2)}, u32[]{:S(2)}) collective-permute-start(f32[3,16,4608]{2,1,0:T(8,128)S(1)} %add_select_fusion.2), channel_id=1, source_target_pairs={{32,0},{48,16},{64,32},{80,48},{96,64},{112,80},{33,1},{49,17},{65... | collective-permute-start | bytes 2654216 | tf_op jit(solution)/shard_map/ppermute | solution.py:282
  69.8 21.5 %collective-permute-start.3 = (f32[3,16,4608]{2,1,0:T(8,128)S(1)}, f32[3,16,4608]{2,1,0:T(8,128)S(1)}, u32[]{:S(2)}, u32[]{:S(2)}) collective-permute-start(f32[3,16,4608]{2,1,0:T(8,128)S(1)} %multiply_add_fusion.1), channel_id=1, source_target_pairs={{32,0},{48,16},{64,32},{80,48},{96,64},{112,80},{33,1},{49,17},{65... | collective-permute-start | bytes 2654216 | tf_op jit(solution)/shard_map/ppermute | solution.py:282
  73.4 22.8 %copy-start.2 = (f32[2,24,9216]{2,1,0:T(8,128)S(1)}, f32[2,24,9216]{2,1,0:T(8,128)}, u32[]{:S(2)}) copy-start(f32[2,24,9216]{2,1,0:T(8,128)} %get-tuple-element.19) | copy-start | bytes 5308420
  92.3 20.9 %collective-permute-start.4 = (f32[3,16,4608]{2,1,0:T(8,128)}, f32[3,16,4608]{2,1,0:T(8,128)}, u32[]{:S(2)}, u32[]{:S(2)}) collective-permute-start(f32[3,16,4608]{2,1,0:T(8,128)} %multiply_add_fusion), channel_id=1, source_target_pairs={{32,0},{48,16},{64,32},{80,48},{96,64},{112,80},{33,1},{49,17},{65... | collective-permute-start | bytes 2654216 | tf_op jit(solution)/shard_map/ppermute | solution.py:282
  93.6 76.5 %collective-permute-start.8 = (f32[2,24,9216]{2,1,0:T(8,128)}, f32[2,24,9216]{2,1,0:T(8,128)}, u32[]{:S(2)}, u32[]{:S(2)}) collective-permute-start(f32[2,24,9216]{2,1,0:T(8,128)} %get-tuple-element.20), channel_id=1, source_target_pairs={{0,1},{1,2},{2,3},{3,4},{4,5},{5,6},{6,7},{7,8},{8,9},{9,10},{10,1... | collective-permute-start | bytes 5308424 | tf_op jit(solution)/shard_map/ppermute | solution.py:255
  96.2 79.3 %collective-permute-start.9 = (f32[2,24,9216]{2,1,0:T(8,128)S(1)}, f32[2,24,9216]{2,1,0:T(8,128)}, u32[]{:S(2)}, u32[]{:S(2)}) collective-permute-start(f32[2,24,9216]{2,1,0:T(8,128)S(1)} %copy-done.2), channel_id=1, source_target_pairs={{1,0},{2,1},{3,2},{4,3},{5,4},{6,5},{7,6},{8,7},{9,8},{10,9},{11,1... | collective-permute-start | bytes 5308424 | tf_op jit(solution)/shard_map/ppermute | solution.py:256
  97.5 126.8 %collective-permute-start.11 = (f32[2,56,9216]{2,1,0:T(8,128)}, f32[2,56,9216]{2,1,0:T(8,128)}, u32[]{:S(2)}, u32[]{:S(2)}) collective-permute-start(f32[2,56,9216]{2,1,0:T(8,128)} %get-tuple-element.17), channel_id=1, source_target_pairs={{1,0},{2,1},{3,2},{4,3},{5,4},{6,5},{7,6},{8,7},{9,8},{10,9},{11,1... | collective-permute-start | bytes 12386312 | tf_op jit(solution)/shard_map/ppermute | solution.py:256
  113.2 68.4 %collective-permute-start.5 = (f32[3,16,4608]{2,1,0:T(8,128)}, f32[3,16,4608]{2,1,0:T(8,128)}, u32[]{:S(2)}, u32[]{:S(2)}) collective-permute-start(f32[3,16,4608]{2,1,0:T(8,128)} %collective-permute-done.4), channel_id=1, source_target_pairs={{0,16},{16,0},{32,48},{48,32},{64,80},{80,64},{96,112},{112,96},{1... | collective-permute-start | bytes 2654216 | tf_op jit(solution)/shard_map/ppermute | solution.py:283
  170.2 63.9 %collective-permute-start.12 = (f32[2,24,9216]{2,1,0:T(8,128)}, f32[2,24,9216]{2,1,0:T(8,128)}, u32[]{:S(2)}, u32[]{:S(2)}) collective-permute-start(f32[2,24,9216]{2,1,0:T(8,128)} %get-tuple-element.16), channel_id=1, source_target_pairs={{0,1},{1,2},{2,3},{3,4},{4,5},{5,6},{6,7},{7,8},{8,9},{9,10},{10,1... | collective-permute-start | bytes 5308424 | tf_op jit(solution)/shard_map/ppermute | solution.py:255
  175.5 86.6 %collective-permute-start.13 = (f32[2,24,9216]{2,1,0:T(8,128)}, f32[2,24,9216]{2,1,0:T(8,128)S(1)}, u32[]{:S(2)}, u32[]{:S(2)}) collective-permute-start(f32[2,24,9216]{2,1,0:T(8,128)} %get-tuple-element.15), channel_id=1, source_target_pairs={{1,0},{2,1},{3,2},{4,3},{5,4},{6,5},{7,6},{8,7},{9,8},{10,9},{11,1... | collective-permute-start | bytes 5308424 | tf_op jit(solution)/shard_map/ppermute | solution.py:256
  176.8 91.6 %collective-permute-start.14 = (f32[2,8,9216]{2,1,0:T(8,128)}, f32[2,8,9216]{2,1,0:T(8,128)}, u32[]{:S(2)}, u32[]{:S(2)}) collective-permute-start(f32[2,8,9216]{2,1,0:T(8,128)} %get-tuple-element.14), channel_id=1, source_target_pairs={{0,1},{1,2},{2,3},{3,4},{4,5},{5,6},{6,7},{7,8},{8,9},{9,10},{10,1... | collective-permute-start | bytes 1769480 | tf_op jit(solution)/shard_map/ppermute | solution.py:255
  181.6 4.4 %copy-start = (f32[3,9216]{1,0:T(4,128)S(1)}, f32[3,9216]{1,0:T(4,128)}, u32[]{:S(2)}) copy-start(f32[3,9216]{1,0:T(4,128)} %absorb_ref.1) | copy-start | bytes 331780
  181.6 93.2 %collective-permute-start.15 = (f32[2,8,9216]{2,1,0:T(8,128)}, f32[2,8,9216]{2,1,0:T(8,128)}, u32[]{:S(2)}, u32[]{:S(2)}) collective-permute-start(f32[2,8,9216]{2,1,0:T(8,128)} %get-tuple-element.13), channel_id=1, source_target_pairs={{1,0},{2,1},{3,2},{4,3},{5,4},{6,5},{7,6},{8,7},{9,8},{10,9},{11,1... | collective-permute-start | bytes 1769480 | tf_op jit(solution)/shard_map/ppermute | solution.py:256
  262.1 1.2 copy-start.3

commit v3 on v2

--- a/solution.py
+++ b/solution.py
@@ -1,3 +1,5 @@
+import functools
+
 import jax
 import jax.numpy as jnp
 from jax import lax
@@ -13,7 +15,8 @@
 EDGE = 256
 TILE = 2304
 SPAN = 768
-CHUNKS = (16, 24, 56, 24, 8)
+MIB = 1024 * 1024
+CHUNKS = (8, 24, 64, 24, 8)
 
 
 def caputo_weights(count):
@@ -83,6 +86,7 @@
             bytes_accessed=4 * depth * plane * (steps + modes),
             transcendentals=0,
         ),
+        compiler_params=pltpu.CompilerParams(vmem_limit_bytes=16 * MIB),
         name="block_sums",
     )(projector, field)
 
@@ -185,7 +189,7 @@
         ],
         out_specs=pl.BlockSpec((depth, steps, TILE), lambda i: (0, 0, i)),
         scratch_shapes=[pltpu.VMEM(wide, jnp.bfloat16), pltpu.VMEM(wide, jnp.bfloat16)],
-        compiler_params=pltpu.CompilerParams(vmem_limit_bytes=48 * 1024 * 1024),
+        compiler_params=pltpu.CompilerParams(vmem_limit_bytes=44 * MIB),
         cost_estimate=pl.CostEstimate(
             flops=6 * cols * steps * depth * plane,
             bytes_accessed=8 * depth * plane * steps,
@@ -195,8 +199,7 @@
     )(table, bands, field, field, field, head, carried, absorption)
 
 
-def edge_kernel(image_ref, below_ref, above_ref, out_ref):
-    depth = image_ref.shape[0]
+def edge_terms(below, above, depth):
     factor = -DIFFUSION / 12.0
     ends = [None] * depth
 
@@ -204,13 +207,78 @@
         if 0 <= p < depth:
             ends[p] = value if ends[p] is None else ends[p] + value
 
-    add(0, 16.0 * below_ref[1] - below_ref[0])
-    add(1, -below_ref[1])
-    add(depth - 1, 16.0 * above_ref[0] - above_ref[1])
-    add(depth - 2, -above_ref[0])
+    add(0, 16.0 * below[1] - below[0])
+    add(1, -below[1])
+    add(depth - 1, 16.0 * above[0] - above[1])
+    add(depth - 2, -above[0])
+    return [0.0 if end is None else factor * end for end in ends]
+
+
+def edge_kernel(image_ref, below_ref, above_ref, out_ref):
+    depth = image_ref.shape[0]
+    terms = edge_terms((below_ref[0], below_ref[1]), (above_ref[0], above_ref[1]), depth)
     for p in range(depth):
-        image = image_ref[p]
-        out_ref[p] = image if ends[p] is None else image + factor * ends[p]
+        out_ref[p] = image_ref[p] + terms[p]
+
+
+def hold_kernel(first, image_ref, out_ref, sem):
+    rows = out_ref.shape[1]
+    copy = pltpu.make_async_copy(image_ref.at[:, pl.ds(first, rows)], out_ref, sem)
+    copy.start()
+    copy.wait()
+
+
+def hold_rows(image, first, rows):
+    depth, _, plane = image.shape
+    return pl.pallas_call(
+        functools.partial(hold_kernel, first),
+        out_shape=jax.ShapeDtypeStruct((depth, rows, plane), jnp.float32),
+        in_specs=[pl.BlockSpec(memory_space=pl.ANY)],
+        out_specs=pl.BlockSpec(memory_space=pltpu.VMEM),
+        scratch_shapes=[pltpu.SemaphoreType.DMA(())],
+        compiler_params=pltpu.CompilerParams(vmem_limit_bytes=44 * MIB),
+        name="hold_rows",
+    )(image)
+
+
+def last_kernel(first, width, image_ref, held_ref, below_ref, above_ref, out_ref, done, sems):
+    depth, rows, plane = held_ref.shape
+    copies = []
+    for j in range(plane // width):
+        lanes = pl.ds(j * width, width)
+        terms = edge_terms(
+            (below_ref[0, :, lanes], below_ref[1, :, lanes]),
+            (above_ref[0, :, lanes], above_ref[1, :, lanes]),
+            depth,
+        )
+        for p in range(depth):
+            done[p, :, lanes] = held_ref[p, :, lanes] + terms[p]
+        copy = pltpu.make_async_copy(
+            done.at[:, :, lanes], out_ref.at[:, pl.ds(first, rows), lanes], sems.at[j]
+        )
+        copy.start()
+        copies.append(copy)
+    for copy in copies:
+        copy.wait()
+
+
+def add_last(image, held, below, above, first):
+    depth, rows, plane = held.shape
+    width = TILE
+    vmem = pl.BlockSpec(memory_space=pltpu.VMEM)
+    return pl.pallas_call(
+        functools.partial(last_kernel, first, width),
+        out_shape=jax.ShapeDtypeStruct(image.shape, jnp.float32),
+        in_specs=[pl.BlockSpec(memory_space=pl.ANY), vmem, vmem, vmem],
+        out_specs=pl.BlockSpec(memory_space=pl.ANY),
+        scratch_shapes=[
+            pltpu.VMEM((depth, rows, plane), jnp.float32),
+            pltpu.SemaphoreType.DMA((plane // width,)),
+        ],
+        input_output_aliases={0: 0},
+        compiler_params=pltpu.CompilerParams(vmem_limit_bytes=8 * MIB),
+        name="add_last",
+    )(image, held, below, above)
 
 
 def add_edges(image, below, above, first, rows, width):
@@ -233,6 +301,7 @@
             bytes_accessed=4 * count * plane * (2 * depth + 4),
             transcendentals=0,
         ),
+        compiler_params=pltpu.CompilerParams(vmem_limit_bytes=16 * MIB),
         name="add_edges",
     )(image, below, above)
 
@@ -255,7 +324,7 @@
         below.append(lax.ppermute(high, "space", up))
         above.append(lax.ppermute(low, "space", down))
         source, _, _ = lax.optimization_barrier((source, high, low))
-        if len(starts) == 1:
+        if len(starts) == 3:
             early = source
         first += count
 
@@ -289,9 +358,10 @@
     carried = jnp.where(core == 0, other + decay * later_full, later_full)
 
     image = local_part(table, stencil_bands(), field, head, carried, absorption)
-    for first, lower, upper in zip(starts, below, above):
-        count = lower.shape[1]
-        image = add_edges(image, lower, upper, first, 8, plane if count > 8 else TILE)
+    held = hold_rows(image, starts[-1], CHUNKS[-1])
+    for first, lower, upper in zip(starts[:-1], below, above):
+        image = add_edges(image, lower, upper, first, 8, plane)
+    image = add_last(image, held, below[-1], above[-1], starts[-1])
     return jnp.transpose(image, (1, 0, 2))
 
 

time: 284 us -> 318 us (1.12)
  the two profiles are of different devices: /device:TPU:1 before, /device:TPU:28 now
where the time goes in v3:
time: 318 us; the launch traced here: 317 us
  waiting for transfers between devices  164 us (52%)
  Pallas kernels  56.3 us (18%)
  starting transfers between devices  53.3 us (17%)
  local copies, waits for them, and re-layouts  28.2 us (9%)
  other arithmetic  15.4 us (5%)
    ppermute x5, waiting for transfers between devices, per_device(): above.append(lax.ppermute(low, 'space', down))  66 us
    ppermute x3, waiting for transfers between devices, per_device(): later = lax.ppermute(sent, 'tm', [(g + 2, g) for g in range(groups - 2)])  57.3 us
    ppermute x5, waiting for transfers between devices, per_device(): below.append(lax.ppermute(high, 'space', up))  40.2 us
    ppermute x5, starting transfers between devices, per_device(): above.append(lax.ppermute(low, 'space', down))  32.2 us
    pallas_call x1, Pallas kernels, local_part(): pl.pallas_call(local_kernel, out_shape=jax.ShapeDtypeStruct(field.shape,...  27.8 us
    slice x5, local copies, waits for them, and re-layouts, per_device(): low = source[:2, first:first + count]  22.1 us
    pallas_call x4, Pallas kernels, add_edges(): pl.pallas_call(edge_kernel, out_shape=jax.ShapeDtypeStruct(image.shape, j...  21.8 us
    ppermute x5, starting transfers between devices, per_device(): below.append(lax.ppermute(high, 'space', up))  11.5 us
  transfers between devices with their start and end apart: 16, of which 4 were waited for; matrix products, arithmetic and copies ran while one was open for 9% of the time, Pallas kernels for 16%

profile of v3, /device:TPU:28, one launch (start us, length us, event | category | flops | bytes accessed | tf_op | source)
XLA Modules:
  0.0 317.0 jit_solution(9602211886513425775)
XLA Ops:
  0.0 2.4 fusion.28
  2.4 4.2 %fusion.27 = (f32[2,24,9216]{2,1,0:T(8,128)}, f32[2,24,9216]{2,1,0:T(8,128)}) fusion(f32[3,128,9216]{2,1,0:T(8,128)} %bitcast.4), kind=kLoop, calls=%fused_computation.55 | loop fusion | bytes 7077888 | tf_op jit(solution)/shard_map/slice | solution.py:323
  6.6 9.2 %fusion.26 = (f32[2,64,9216]{2,1,0:T(8,128)}, f32[2,64,9216]{2,1,0:T(8,128)}) fusion(f32[3,128,9216]{2,1,0:T(8,128)} %bitcast.5), kind=kLoop, calls=%fused_computation.54 | loop fusion | bytes 18874368 | tf_op jit(solution)/shard_map/slice | solution.py:323
  15.9 4.5 %block_sums.1 = f32[3,16,9216]{2,1,0:T(8,128)S(1)} custom-call(f32[16,128]{1,0:T(8,128)S(1)} %multiply_exponential_fusion.projector_ref, f32[3,128,9216]{2,1,0:T(8,128)S(1)} %bitcast.13), custom_call_target="tpu_custom_call" | custom-call | flops 339738624 | bytes 15925248 | tf_op jit(solution)/shard_map/block_sums/pallas_call | solution.py:75
  20.5 3.8 %collective-permute-start.6 = (f32[2,8,9216]{2,1,0:T(8,128)}, f32[2,8,9216]{2,1,0:T(8,128)}, u32[]{:S(2)}, u32[]{:S(2)}) collective-permute-start(f32[2,8,9216]{2,1,0:T(8,128)} %get-tuple-element.22), channel_id=1, source_target_pairs={{0,1},{1,2},{2,3},{3,4},{4,5},{5,6},{6,7},{7,8},{8,9},{9,10},{10,1... | collective-permute-start | bytes 1769480 | tf_op jit(solution)/shard_map/ppermute | solution.py:324
  24.3 4.2 %collective-permute-start.7 = (f32[2,8,9216]{2,1,0:T(8,128)}, f32[2,8,9216]{2,1,0:T(8,128)}, u32[]{:S(2)}, u32[]{:S(2)}) collective-permute-start(f32[2,8,9216]{2,1,0:T(8,128)} %get-tuple-element.21), channel_id=1, source_target_pairs={{1,0},{2,1},{3,2},{4,3},{5,4},{6,5},{7,6},{8,7},{9,8},{10,9},{11,1... | collective-permute-start | bytes 1769480 | tf_op jit(solution)/shard_map/ppermute | solution.py:325
  28.6 1.9 collective-permute-start.10
  31.8 2.2 collective-permute-start
  35.5 2.4 collective-permute-start.2
  37.9 4.1 %fusion.25 = (f32[2,24,9216]{2,1,0:T(8,128)}, f32[2,24,9216]{2,1,0:T(8,128)}) fusion(f32[3,128,9216]{2,1,0:T(8,128)} %bitcast.6), kind=kLoop, calls=%fused_computation.53 | loop fusion | bytes 7077888 | tf_op jit(solution)/shard_map/slice | solution.py:323
  42.0 42.7 %collective-permute-done.2 = f32[3,16,4608]{2,1,0:T(8,128)S(1)} collective-permute-done((f32[3,16,4608]{2,1,0:T(8,128)S(1)}, f32[3,16,4608]{2,1,0:T(8,128)S(1)}, u32[]{:S(2)}, u32[]{:S(2)}) %collective-permute-start.2) | collective-permute-done | bytes 884768 | tf_op jit(solution)/shard_map/ppermute | solution.py:351
  84.8 2.4 collective-permute-start.3
  87.3 2.3 fusion.24
  90.2 14.6 %collective-permute-done.3 = f32[3,16,4608]{2,1,0:T(8,128)S(1)} collective-permute-done((f32[3,16,4608]{2,1,0:T(8,128)S(1)}, f32[3,16,4608]{2,1,0:T(8,128)S(1)}, u32[]{:S(2)}, u32[]{:S(2)}) %collective-permute-start.3) | collective-permute-done | bytes 884768 | tf_op jit(solution)/shard_map/ppermute | solution.py:351
  104.8 9.3 %collective-permute-start.11 = (f32[2,64,9216]{2,1,0:T(8,128)}, f32[2,64,9216]{2,1,0:T(8,128)}, u32[]{:S(2)}, u32[]{:S(2)}) collective-permute-start(f32[2,64,9216]{2,1,0:T(8,128)} %get-tuple-element.17), channel_id=1, source_target_pairs={{1,0},{2,1},{3,2},{4,3},{5,4},{6,5},{7,6},{8,7},{9,8},{10,9},{11,1... | collective-permute-start | bytes 14155784 | tf_op jit(solution)/shard_map/ppermute | solution.py:325
  115.3 2.4 collective-permute-start.4
  119.7 1.9 collective-permute-start.8
  121.7 6.0 %collective-permute-start.9 = (f32[2,24,9216]{2,1,0:T(8,128)}, f32[2,24,9216]{2,1,0:T(8,128)}, u32[]{:S(2)}, u32[]{:S(2)}) collective-permute-start(f32[2,24,9216]{2,1,0:T(8,128)} %get-tuple-element.19), channel_id=1, source_target_pairs={{1,0},{2,1},{3,2},{4,3},{5,4},{6,5},{7,6},{8,7},{9,8},{10,9},{11,1... | collective-permute-start | bytes 5308424 | tf_op jit(solution)/shard_map/ppermute | solution.py:325
  128.4 1.7 select_reduce_fusion
  130.1 1.8 multiply_reduce_fusion
  139.7 40.2 %collective-permute-done.8.below_ref = f32[2,24,9216]{2,1,0:T(8,128)S(1)} collective-permute-done((f32[2,24,9216]{2,1,0:T(8,128)}, f32[2,24,9216]{2,1,0:T(8,128)S(1)}, u32[]{:S(2)}, u32[]{:S(2)}) %collective-permute-start.8) | collective-permute-done | bytes 1769504 | tf_op jit(solution)/shard_map/ppermute | solution.py:324
  179.8 1.9 collective-permute-start.12
  181.8 66.0 %collective-permute-done.9.above_ref = f32[2,24,9216]{2,1,0:T(8,128)} collective-permute-done((f32[2,24,9216]{2,1,0:T(8,128)}, f32[2,24,9216]{2,1,0:T(8,128)}, u32[]{:S(2)}, u32[]{:S(2)}) %collective-permute-start.9) | collective-permute-done | bytes 1769504 | tf_op jit(solution)/shard_map/ppermute | solution.py:325
  247.7 6.5 %collective-permute-start.13 = (f32[2,24,9216]{2,1,0:T(8,128)S(1)}, f32[2,24,9216]{2,1,0:T(8,128)S(1)}, u32[]{:S(2)}, u32[]{:S(2)}) collective-permute-start(f32[2,24,9216]{2,1,0:T(8,128)S(1)} %copy-done.1), channel_id=1, source_target_pairs={{1,0},{2,1},{3,2},{4,3},{5,4},{6,5},{7,6},{8,7},{9,8},{10,9},{11,1... | collective-permute-start | bytes 5308424 | tf_op jit(solution)/shard_map/ppermute | solution.py:325
  254.2 1.9 collective-permute-start.14
  256.2 6.2 %collective-permute-start.15 = (f32[2,8,9216]{2,1,0:T(8,128)}, f32[2,8,9216]{2,1,0:T(8,128)S(1)}, u32[]{:S(2)}, u32[]{:S(2)}) collective-permute-start(f32[2,8,9216]{2,1,0:T(8,128)} %get-tuple-element.13), channel_id=1, source_target_pairs={{1,0},{2,1},{3,2},{4,3},{5,4},{6,5},{7,6},{8,7},{9,8},{10,9},{11,1... | collective-permute-start | bytes 1769480 | tf_op jit(solution)/shard_map/ppermute | solution.py:325
  262.4 2.9 add_select_fusion.1.carried_ref
  265.2 27.8 %local_part.1.image_ref = f32[3,128,9216]{2,1,0:T(8,128)} custom-call(f32[128,160]{1,0:T(8,128)S(1)} %pad_maximum_fusion.table_ref, bf16[3,768,256]{2,1,0:T(8,128)(2,1)S(1)} %select_convert_fusion.bands_ref, f32[3,128,9216]{2,1,0:T(8,128)} %bitcast.8, f32[3,128,9216]{2,1,0:T(8,128)} %bitcast.9, f32[3,128,9216]{2,1,0:T(8,128)} %bitcast.10, ...), custom_call_target="tpu_custom_call" | custom-call | flops 3397386240 | bytes 28311552 | tf_op jit(solution)/shard_map/local_part/pallas_call | solution.py:176
  294.2 2.6 add_edges.4.image_ref
  296.8 4.6 %add_edges.5.image_ref = f32[3,128,9216]{2,1,0:T(8,128)} custom-call(f32[3,128,9216]{2,1,0:T(8,128)} %add_edges.4.image_ref, f32[2,24,9216]{2,1,0:T(8,128)S(1)} %collective-permute-done.8.below_ref, f32[2,24,9216]{2,1,0:T(8,128)} %collective-permute-done.9.above_ref), custom_call_target="tpu_custom_call", output_to_operand_aliasing={{}: (0, {})} | custom-call | flops 5308416 | bytes 8847360 | tf_op jit(solution)/shard_map/add_edges/pallas_call | solution.py:288
  301.4 10.4 %add_edges.6.image_ref = f32[3,128,9216]{2,1,0:T(8,128)} custom-call(f32[3,128,9216]{2,1,0:T(8,128)} %add_edges.5.image_ref, f32[2,64,9216]{2,1,0:T(8,128)} %collective-permute-done.10.below_ref, f32[2,64,9216]{2,1,0:T(8,128)} %collective-permute-done.11.above_ref), custom_call_target="tpu_custom_call", output_to_operand_aliasing={{}: (0, {})} | custom-call | flops 14155776 | bytes 23592960 | tf_op jit(solution)/shard_map/add_edges/pallas_call | solution.py:288
  311.8 4.3 %add_edges.7.image_ref = f32[3,128,9216]{2,1,0:T(8,128)} custom-call(f32[3,128,9216]{2,1,0:T(8,128)} %add_edges.6.image_ref, f32[2,24,9216]{2,1,0:T(8,128)S(1)} %collective-permute-done.12.below_ref, f32[2,24,9216]{2,1,0:T(8,128)S(1)} %collective-permute-done.13.above_ref), custom_call_target="tpu_custom_call", output_to_operand_aliasing={{}: (0, {})} | custom-call | flops 5308416 | bytes 8847360 | tf_op jit(solution)/shard_map/add_edges/pallas_call | solution.py:288
  (55 shorter events, 17.4 us)
Async XLA Ops:
  2.4 13.5 %slice-start = ((s8[14155776]{0:T(1024)(128)(4,1)}), s8[4194304]{0:T(1024)(128)(4,1)S(1)}, s32[]{:S(2)}) async-start(s8[14155776]{0:T(1024)(128)(4,1)} %bitcast.11), calls=%async_computation | async-start | bytes 8388608
  2.4 13.5 %slice-start.1 = ((s8[14155776]{0:T(1024)(128)(4,1)}), s8[4194304]{0:T(1024)(128)(4,1)S(1)}, s32[]{:S(2)}) async-start(s8[14155776]{0:T(1024)(128)(4,1)} %bitcast.11), calls=%async_computation.1 | async-start | bytes 8388608
  6.6 9.2 %copy-start.2 = (f32[16]{0:T(128)S(1)}, f32[16]{0:T(128)}, u32[]{:S(2)}) copy-start(f32[16]{0:T(128)} %param.6) | copy-start | bytes 196
  6.6 9.2 %copy-start.3 = (f32[16]{0:T(128)S(1)}, f32[16]{0:T(128)}, u32[]{:S(2)}) copy-start(f32[16]{0:T(128)} %param.7) | copy-start | bytes 196
  6.6 9.3 %slice-start.2 = ((s8[14155776]{0:T(1024)(128)(4,1)}), s8[4194304]{0:T(1024)(128)(4,1)S(1)}, s32[]{:S(2)}) async-start(s8[14155776]{0:T(1024)(128)(4,1)} %bitcast.11), calls=%async_computation.2 | async-start | bytes 8388608
  6.6 9.3 %slice-start.3 = ((s8[14155776]{0:T(1024)(128)(4,1)}), s8[1572864]{0:T(1024)(128)(4,1)S(1)}, s32[]{:S(2)}) async-start(s8[14155776]{0:T(1024)(128)(4,1)} %bitcast.11), calls=%async_computation.3 | async-start | bytes 3145728
  20.4 13.7 %collective-permute-start.1 = (f32[3,16,9216]{2,1,0:T(8,128)S(1)}, f32[3,16,9216]{2,1,0:T(8,128)}, u32[]{:S(2)}, u32[]{:S(2)}) collective-permute-start(f32[3,16,9216]{2,1,0:T(8,128)S(1)} %block_sums.1), channel_id=1, source_target_pairs={{0,16},{16,0},{32,48},{48,32},{64,80},{80,64},{96,112},{112,96},{1... | collective-permute-start | bytes 5308424 | tf_op jit(solution)/shard_map/ppermute | solution.py:340
  20.5 94.8 %collective-permute-start.6 = (f32[2,8,9216]{2,1,0:T(8,128)}, f32[2,8,9216]{2,1,0:T(8,128)}, u32[]{:S(2)}, u32[]{:S(2)}) collective-permute-start(f32[2,8,9216]{2,1,0:T(8,128)} %get-tuple-element.22), channel_id=1, source_target_pairs={{0,1},{1,2},{2,3},{3,4},{4,5},{5,6},{6,7},{7,8},{8,9},{9,10},{10,1... | collective-permute-start | bytes 1769480 | tf_op jit(solution)/shard_map/ppermute | solution.py:324
  24.3 95.4 %collective-permute-start.7 = (f32[2,8,9216]{2,1,0:T(8,128)}, f32[2,8,9216]{2,1,0:T(8,128)}, u32[]{:S(2)}, u32[]{:S(2)}) collective-permute-start(f32[2,8,9216]{2,1,0:T(8,128)} %get-tuple-element.21), channel_id=1, source_target_pairs={{1,0},{2,1},{3,2},{4,3},{5,4},{6,5},{7,6},{8,7},{9,8},{10,9},{11,1... | collective-permute-start | bytes 1769480 | tf_op jit(solution)/shard_map/ppermute | solution.py:325
  28.6 225.7 %collective-permute-start.10 = (f32[2,64,9216]{2,1,0:T(8,128)}, f32[2,64,9216]{2,1,0:T(8,128)}, u32[]{:S(2)}, u32[]{:S(2)}) collective-permute-start(f32[2,64,9216]{2,1,0:T(8,128)} %get-tuple-element.18), channel_id=1, source_target_pairs={{0,1},{1,2},{2,3},{3,4},{4,5},{5,6},{6,7},{7,8},{8,9},{9,10},{10,1... | collective-permute-start | bytes 14155784 | tf_op jit(solution)/shard_map/ppermute | solution.py:324
  31.8 89.9 %collective-permute-start = (f32[3,16,9216]{2,1,0:T(8,128)}, f32[3,16,9216]{2,1,0:T(8,128)S(1)}, u32[]{:S(2)}, u32[]{:S(2)}) collective-permute-start(f32[3,16,9216]{2,1,0:T(8,128)} %slice.43), channel_id=1, source_target_pairs={{16,0},{32,16},{48,32},{64,48},{80,64},{96,80},{112,96},{17,1},{33... | collective-permute-start | bytes 5308424 | tf_op jit(solution)/shard_map/ppermute | solution.py:336
  35.5 49.2 %collective-permute-start.2 = (f32[3,16,4608]{2,1,0:T(8,128)S(1)}, f32[3,16,4608]{2,1,0:T(8,128)S(1)}, u32[]{:S(2)}, u32[]{:S(2)}) collective-permute-start(f32[3,16,4608]{2,1,0:T(8,128)S(1)} %add_select_fusion.2), channel_id=1, source_target_pairs={{32,0},{48,16},{64,32},{80,48},{96,64},{112,80},{33,1},{49,17},{65... | collective-permute-start | bytes 2654216 | tf_op jit(solution)/shard_map/ppermute | solution.py:351
  84.8 20.0 %collective-permute-start.3 = (f32[3,16,4608]{2,1,0:T(8,128)S(1)}, f32[3,16,4608]{2,1,0:T(8,128)S(1)}, u32[]{:S(2)}, u32[]{:S(2)}) collective-permute-start(f32[3,16,4608]{2,1,0:T(8,128)S(1)} %multiply_add_fusion.1), channel_id=1, source_target_pairs={{32,0},{48,16},{64,32},{80,48},{96,64},{112,80},{33,1},{49,17},{65... | collective-permute-start | bytes 2654216 | tf_op jit(solution)/shard_map/ppermute | solution.py:351
  104.8 196.6 %collective-permute-start.11 = (f32[2,64,9216]{2,1,0:T(8,128)}, f32[2,64,9216]{2,1,0:T(8,128)}, u32[]{:S(2)}, u32[]{:S(2)}) collective-permute-start(f32[2,64,9216]{2,1,0:T(8,128)} %get-tuple-element.17), channel_id=1, source_target_pairs={{1,0},{2,1},{3,2},{4,3},{5,4},{6,5},{7,6},{8,7},{9,8},{10,9},{11,1... | collective-permute-start | bytes 14155784 | tf_op jit(solution)/shard_map/ppermute | solution.py:325
  115.3 17.4 %collective-permute-start.4 = (f32[3,16,4608]{2,1,0:T(8,128)}, f32[3,16,4608]{2,1,0:T(8,128)}, u32[]{:S(2)}, u32[]{:S(2)}) collective-permute-start(f32[3,16,4608]{2,1,0:T(8,128)} %multiply_add_fusion), channel_id=1, source_target_pairs={{32,0},{48,16},{64,32},{80,48},{96,64},{112,80},{33,1},{49,17},{65... | collective-permute-start | bytes 2654216 | tf_op jit(solution)/shard_map/ppermute | solution.py:351
  119.7 60.1 %collective-permute-start.8 = (f32[2,24,9216]{2,1,0:T(8,128)}, f32[2,24,9216]{2,1,0:T(8,128)S(1)}, u32[]{:S(2)}, u32[]{:S(2)}) collective-permute-start(f32[2,24,9216]{2,1,0:T(8,128)} %get-tuple-element.20), channel_id=1, source_target_pairs={{0,1},{1,2},{2,3},{3,4},{4,5},{5,6},{6,7},{7,8},{8,9},{9,10},{10,1... | collective-permute-start | bytes 5308424 | tf_op jit(solution)/shard_map/ppermute | solution.py:324
  121.7 126.1 %collective-permute-start.9 = (f32[2,24,9216]{2,1,0:T(8,128)}, f32[2,24,9216]{2,1,0:T(8,128)}, u32[]{:S(2)}, u32[]{:S(2)}) collective-permute-start(f32[2,24,9216]{2,1,0:T(8,128)} %get-tuple-element.19), channel_id=1, source_target_pairs={{1,0},{2,1},{3,2},{4,3},{5,4},{6,5},{7,6},{8,7},{9,8},{10,9},{11,1... | collective-permute-start | bytes 5308424 | tf_op jit(solution)/shard_map/ppermute | solution.py:325
  132.6 123.5 %collective-permute-start.5 = (f32[3,16,4608]{2,1,0:T(8,128)}, f32[3,16,4608]{2,1,0:T(8,128)}, u32[]{:S(2)}, u32[]{:S(2)}) collective-permute-start(f32[3,16,4608]{2,1,0:T(8,128)} %collective-permute-done.4), channel_id=1, source_target_pairs={{0,16},{16,0},{32,48},{48,32},{64,80},{80,64},{96,112},{112,96},{1... | collective-permute-start | bytes 2654216 | tf_op jit(solution)/shard_map/ppermute | solution.py:352
  135.9 111.8 %copy-start.1 = (f32[2,24,9216]{2,1,0:T(8,128)S(1)}, f32[2,24,9216]{2,1,0:T(8,128)}, u32[]{:S(2)}) copy-start(f32[2,24,9216]{2,1,0:T(8,128)} %get-tuple-element.15) | copy-start | bytes 5308420
  179.8 132.0 %collective-permute-start.12 = (f32[2,24,9216]{2,1,0:T(8,128)}, f32[2,24,9216]{2,1,0:T(8,128)S(1)}, u32[]{:S(2)}, u32[]{:S(2)}) collective-permute-start(f32[2,24,9216]{2,1,0:T(8,128)} %get-tuple-element.16), channel_id=1, source_target_pairs={{0,1},{1,2},{2,3},{3,4},{4,5},{5,6},{6,7},{7,8},{8,9},{9,10},{10,1... | collective-permute-start | bytes 5308424 | tf_op jit(solution)/shard_map/ppermute | solution.py:324
  247.7 64.1 %collective-permute-start.13 = (f32[2,24,9216]{2,1,0:T(8,128)S(1)}, f32[2,24,9216]{2,1,0:T(8,128)S(1)}, u32[]{:S(2)}, u32[]{:S(2)}) collective-permute-start(f32[2,24,9216]{2,1,0:T(8,128)S(1)} %copy-done.1), channel_id=1, source_target_pairs={{1,0},{2,1},{3,2},{4,3},{5,4},{6,5},{7,6},{8,7},{9,8},{10,9},{11,1... | collective-permute-start | bytes 5308424 | tf_op jit(solution)/shard_map/ppermute | solution.py:325
  254.2 61.8 %collective-permute-start.14 = (f32[2,8,9216]{2,1,0:T(8,128)}, f32[2,8,9216]{2,1,0:T(8,128)S(1)}, u32[]{:S(2)}, u32[]{:S(2)}) collective-permute-start(f32[2,8,9216]{2,1,0:T(8,128)} %get-tuple-element.14), channel_id=1, source_target_pairs={{0,1},{1,2},{2,3},{3,4},{4,5},{5,6},{6,7},{7,8},{8,9},{9,10},{10,1... | collective-permute-start | bytes 1769480 | tf_op jit(solution)/shard_map/ppermute | solution.py:324
  256.2 9.0 %copy-start = (f32[3,9216]{1,0:T(4,128)S(1)}, f32[3,9216]{1,0:T(4,128)}, u32[]{:S(2)}) copy-start(f32[3,9216]{1,0:T(4,128)} %absorb_ref.1) | copy-start | bytes 331780
  256.2 59.9 %collective-permute-start.15 = (f32[2,8,9216]{2,1,0:T(8,128)}, f32[2,8,9216]{2,1,0:T(8,128)S(1)}, u32[]{:S(2)}, u32[]{:S(2)}) collective-permute-start(f32[2,8,9216]{2,1,0:T(8,128)} %get-tuple-element.13), channel_id=1, source_target_pairs={{1,0},{2,1},{3,2},{4,3},{5,4},{6,5},{7,6},{8,7},{9,8},{10,9},{11,1... | collective-permute-start | bytes 1769480 | tf_op jit(solution)/shard_map/ppermute | solution.py:325

commit v4 on v3

--- a/solution.py
+++ b/solution.py
@@ -62,6 +62,64 @@
     )
     rest = jnp.dot(upper, low, preferred_element_type=jnp.float32)
     return both[:rows] + both[rows:] + rest
+
+
+def odd_slab():
+    return lax.axis_index("space") % 2
+
+
+def first_cut_kernel(first, field_ref, odd_ref, even_ref, sems):
+    depth = field_ref.shape[0]
+    rows = pl.ds(first, odd_ref.shape[1])
+    up = depth - 2
+    parity = odd_slab()
+    copies = [
+        pltpu.make_async_copy(field_ref.at[pl.ds(parity * up, 2), rows], odd_ref, sems.at[0]),
+        pltpu.make_async_copy(field_ref.at[pl.ds((1 - parity) * up, 2), rows], even_ref, sems.at[1]),
+    ]
+    for copy in copies:
+        copy.start()
+    for copy in copies:
+        copy.wait()
+
+
+def first_cut(field, first, rows):
+    piece = jax.ShapeDtypeStruct((2, rows, field.shape[2]), jnp.float32)
+    vmem = pl.BlockSpec(memory_space=pltpu.VMEM)
+    return pl.pallas_call(
+        functools.partial(first_cut_kernel, first),
+        out_shape=(piece, piece),
+        in_specs=[pl.BlockSpec(memory_space=pl.ANY)],
+        out_specs=(vmem, vmem),
+        scratch_shapes=[pltpu.SemaphoreType.DMA((2,))],
+        compiler_params=pltpu.CompilerParams(vmem_limit_bytes=46 * MIB),
+        name="first_cut",
+    )(field)
+
+
+def cut_kernel(field_ref, odd_ref, even_ref):
+    up = field_ref.shape[0] - 2
+    parity = odd_slab()
+    odd_ref[...] = field_ref[pl.ds(parity * up, 2)]
+    even_ref[...] = field_ref[pl.ds((1 - parity) * up, 2)]
+
+
+def cut(field, first, count):
+    depth, _, plane = field.shape
+    piece = jax.ShapeDtypeStruct((2, count, plane), jnp.float32)
+    block = pl.BlockSpec((2, 8, plane), lambda i: (0, i, 0))
+    return pl.pallas_call(
+        cut_kernel,
+        out_shape=(piece, piece),
+        grid=(count // 8,),
+        in_specs=[pl.BlockSpec((depth, 8, plane), lambda i: (0, first // 8 + i, 0))],
+        out_specs=(block, block),
+        compiler_params=pltpu.CompilerParams(vmem_limit_bytes=46 * MIB),
+        cost_estimate=pl.CostEstimate(
+            flops=0, bytes_accessed=4 * count * plane * (depth + 4), transcendentals=0
+        ),
+        name="cut",
+    )(field)
 
 
 def project_kernel(projector_ref, field_ref, out_ref):
@@ -86,7 +144,7 @@
             bytes_accessed=4 * depth * plane * (steps + modes),
             transcendentals=0,
         ),
-        compiler_params=pltpu.CompilerParams(vmem_limit_bytes=16 * MIB),
+        compiler_params=pltpu.CompilerParams(vmem_limit_bytes=46 * MIB),
         name="block_sums",
     )(projector, field)
 
@@ -214,9 +272,17 @@
     return [0.0 if end is None else factor * end for end in ends]
 
 
-def edge_kernel(image_ref, below_ref, above_ref, out_ref):
+def by_side(odd, even):
+    lower = odd_slab() == 0
+    below = [jnp.where(lower, odd[k], even[k]) for k in range(2)]
+    above = [jnp.where(lower, even[k], odd[k]) for k in range(2)]
+    return below, above
+
+
+def edge_kernel(image_ref, odd_ref, even_ref, out_ref):
     depth = image_ref.shape[0]
-    terms = edge_terms((below_ref[0], below_ref[1]), (above_ref[0], above_ref[1]), depth)
+    below, above = by_side(odd_ref, even_ref)
+    terms = edge_terms(below, above, depth)
     for p in range(depth):
         out_ref[p] = image_ref[p] + terms[p]
 
@@ -241,36 +307,34 @@
     )(image)
 
 
-def last_kernel(first, width, image_ref, held_ref, below_ref, above_ref, out_ref, done, sems):
+def last_kernel(first, width, image_ref, held_ref, odd_ref, even_ref, out_ref, done, sems):
     depth, rows, plane = held_ref.shape
-    copies = []
+    stores = []
     for j in range(plane // width):
         lanes = pl.ds(j * width, width)
-        terms = edge_terms(
-            (below_ref[0, :, lanes], below_ref[1, :, lanes]),
-            (above_ref[0, :, lanes], above_ref[1, :, lanes]),
-            depth,
-        )
+        below, above = by_side(odd_ref[:, :, lanes], even_ref[:, :, lanes])
+        terms = edge_terms(below, above, depth)
         for p in range(depth):
             done[p, :, lanes] = held_ref[p, :, lanes] + terms[p]
-        copy = pltpu.make_async_copy(
+        store = pltpu.make_async_copy(
             done.at[:, :, lanes], out_ref.at[:, pl.ds(first, rows), lanes], sems.at[j]
         )
-        copy.start()
-        copies.append(copy)
-    for copy in copies:
-        copy.wait()
-
-
-def add_last(image, held, below, above, first):
+        store.start()
+        stores.append(store)
+    for store in stores:
+        store.wait()
+
+
+def add_last(image, held, odd, even, first):
     depth, rows, plane = held.shape
     width = TILE
+    anywhere = pl.BlockSpec(memory_space=pl.ANY)
     vmem = pl.BlockSpec(memory_space=pltpu.VMEM)
     return pl.pallas_call(
         functools.partial(last_kernel, first, width),
         out_shape=jax.ShapeDtypeStruct(image.shape, jnp.float32),
-        in_specs=[pl.BlockSpec(memory_space=pl.ANY), vmem, vmem, vmem],
-        out_specs=pl.BlockSpec(memory_space=pl.ANY),
+        in_specs=[anywhere, vmem, vmem, vmem],
+        out_specs=anywhere,
         scratch_shapes=[
             pltpu.VMEM((depth, rows, plane), jnp.float32),
             pltpu.SemaphoreType.DMA((plane // width,)),
@@ -278,12 +342,12 @@
         input_output_aliases={0: 0},
         compiler_params=pltpu.CompilerParams(vmem_limit_bytes=8 * MIB),
         name="add_last",
-    )(image, held, below, above)
-
-
-def add_edges(image, below, above, first, rows, width):
+    )(image, held, odd, even)
+
+
+def add_edges(image, odd, even, first, rows, width):
     depth, _, plane = image.shape
-    count = below.shape[1]
+    count = odd.shape[1]
     at = first // rows
     return pl.pallas_call(
         edge_kernel,
@@ -303,29 +367,30 @@
         ),
         compiler_params=pltpu.CompilerParams(vmem_limit_bytes=16 * MIB),
         name="add_edges",
-    )(image, below, above)
+    )(image, odd, even)
 
 
 def per_device(adjoint_field, absorption, mode_rates, mode_weights):
-    steps, depth, plane = adjoint_field.shape
+    steps, _, plane = adjoint_field.shape
     groups = lax.axis_size("tm")
     slabs = lax.axis_size("space")
     field = jnp.transpose(adjoint_field, (1, 0, 2))
 
-    up = [(i, i + 1) for i in range(slabs - 1)]
-    down = [(i + 1, i) for i in range(slabs - 1)]
-    below, above, starts = [], [], []
+    def both_ways(lowest):
+        pairs = [(i, i + 1) for i in range(lowest, slabs - 1, 2)]
+        return pairs + [(j, i) for i, j in pairs]
+
+    odds, evens, starts = [], [], []
     first = 0
     source = field
-    for count in CHUNKS:
+    for k, count in enumerate(CHUNKS):
         starts.append(first)
-        high = source[depth - 2 :, first : first + count]
-        low = source[:2, first : first + count]
-        below.append(lax.ppermute(high, "space", up))
-        above.append(lax.ppermute(low, "space", down))
-        source, _, _ = lax.optimization_barrier((source, high, low))
+        over_odd, over_even = (first_cut if k == 0 else cut)(source, first, count)
+        odds.append(lax.ppermute(over_odd, "space", both_ways(1)))
+        evens.append(lax.ppermute(over_even, "space", both_ways(0)))
+        source, _, _ = lax.optimization_barrier((source, over_odd, over_even))
         if len(starts) == 3:
-            early = source
+            early, odds[0], evens[0] = lax.optimization_barrier((source, odds[0], evens[0]))
         first += count
 
     scaled = mode_rates / (steps * groups)
@@ -359,9 +424,9 @@
 
     image = local_part(table, stencil_bands(), field, head, carried, absorption)
     held = hold_rows(image, starts[-1], CHUNKS[-1])
-    for first, lower, upper in zip(starts[:-1], below, above):
+    for first, lower, upper in zip(starts[:-1], odds, evens):
         image = add_edges(image, lower, upper, first, 8, plane)
-    image = add_last(image, held, below[-1], above[-1], starts[-1])
+    image = add_last(image, held, odds[-1], evens[-1], starts[-1])
     return jnp.transpose(image, (1, 0, 2))
 
 

time: 318 us -> 273 us (0.86)
  the two profiles are of different devices: /device:TPU:28 before, /device:TPU:1 now
where the time goes in v4:
time: 273 us; the launch traced here: 271 us
  starting transfers between devices  114 us (42%)
  Pallas kernels  79.4 us (29%)
  waiting for transfers between devices  50.4 us (18%)
  local copies, waits for them, and re-layouts  14.3 us (5%)
  other arithmetic  12.3 us (5%)
    ppermute x5, starting transfers between devices, per_device(): evens.append(lax.ppermute(over_even, 'space', both_ways(0)))  96.8 us
    ppermute x3, waiting for transfers between devices, per_device(): later = lax.ppermute(sent, 'tm', [(g + 2, g) for g in range(groups - 2)])  40.9 us
    pallas_call x1, Pallas kernels, local_part(): pl.pallas_call(local_kernel, out_shape=jax.ShapeDtypeStruct(field.shape,...  27.8 us
    pallas_call x4, Pallas kernels, add_edges(): pl.pallas_call(edge_kernel, out_shape=jax.ShapeDtypeStruct(image.shape, j...  21.8 us
    pallas_call x4, Pallas kernels, cut(): pl.pallas_call(cut_kernel, out_shape=(piece, piece), grid=(count // 8,),...  15.7 us
    pallas_call x1, Pallas kernels, block_sums(): pl.pallas_call(project_kernel, out_shape=jax.ShapeDtypeStruct((depth, mod...  10.6 us
    ppermute x1, waiting for transfers between devices, per_device(): lax.ppermute(mine_first, 'tm', [(g + 1, g) for g in range(groups - 1)])  6.05 us
    ppermute x5, starting transfers between devices, per_device(): odds.append(lax.ppermute(over_odd, 'space', both_ways(1)))  5.8 us
  transfers between devices with their start and end apart: 16, of which 5 were waited for; matrix products, arithmetic and copies ran while one was open for 7% of the time, Pallas kernels for 25%

profile of v4, /device:TPU:1, one launch (start us, length us, event | category | flops | bytes accessed | tf_op | source)
XLA Modules:
  0.0 271.2 jit_solution(6493357270023747971)
XLA Ops:
  2.0 5.4 %collective-permute-start.1 = (f32[2,8,9216]{2,1,0:T(8,128)S(1)}, f32[2,8,9216]{2,1,0:T(8,128)S(1)}, u32[]{:S(2)}, u32[]{:S(2)}) collective-permute-start(f32[2,8,9216]{2,1,0:T(8,128)S(1)} %get-tuple-element.23), channel_id=1, source_target_pairs={{0,1},{2,3},{4,5},{6,7},{8,9},{10,11},{12,13},{14,15},{1,0},{3,2},... | collective-permute-start | bytes 1769480 | tf_op jit(solution)/shard_map/ppermute | solution.py:390
  7.4 3.9 %cut.4 = (f32[2,24,9216]{2,1,0:T(8,128)S(1)}, f32[2,24,9216]{2,1,0:T(8,128)}) custom-call(f32[3,128,9216]{2,1,0:T(8,128)} %bitcast.4), custom_call_target="tpu_custom_call" | custom-call | bytes 6193152 | tf_op jit(solution)/shard_map/cut/pallas_call | solution.py:111
  11.2 7.7 %cut.5 = (f32[2,64,9216]{2,1,0:T(8,128)S(1)}, f32[2,64,9216]{2,1,0:T(8,128)}) custom-call(f32[3,128,9216]{2,1,0:T(8,128)} %bitcast.5), custom_call_target="tpu_custom_call" | custom-call | bytes 16515072 | tf_op jit(solution)/shard_map/cut/pallas_call | solution.py:111
  19.0 2.2 copy-done.5
  21.3 10.6 %block_sums.1 = f32[3,16,9216]{2,1,0:T(8,128)S(1)} custom-call(f32[16,128]{1,0:T(8,128)S(1)} %multiply_exponential_fusion.projector_ref, f32[3,128,9216]{2,1,0:T(8,128)} %bitcast.6), custom_call_target="tpu_custom_call" | custom-call | flops 339738624 | bytes 15925248 | tf_op jit(solution)/shard_map/block_sums/pallas_call | solution.py:133
  31.9 1.3 collective-permute-start.3
  33.2 3.4 %collective-permute-done.3 = f32[3,16,9216]{2,1,0:T(8,128)} collective-permute-done((f32[3,16,9216]{2,1,0:T(8,128)S(1)}, f32[3,16,9216]{2,1,0:T(8,128)}, u32[]{:S(2)}, u32[]{:S(2)}) %collective-permute-start.3) | collective-permute-done | bytes 1769504 | tf_op jit(solution)/shard_map/ppermute | solution.py:405
  36.7 1.4 add_select_fusion.2
  39.4 2.9 %collective-permute-start.10 = (f32[2,64,9216]{2,1,0:T(8,128)}, f32[2,64,9216]{2,1,0:T(8,128)}, u32[]{:S(2)}, u32[]{:S(2)}) collective-permute-start(f32[2,64,9216]{2,1,0:T(8,128)} %copy-done.5), channel_id=1, source_target_pairs={{1,2},{3,4},{5,6},{7,8},{9,10},{11,12},{13,14},{2,1},{4,3},{6,5},{... | collective-permute-start | bytes 14155784 | tf_op jit(solution)/shard_map/ppermute | solution.py:389
  42.2 18.6 %collective-permute-done.4 = f32[3,16,4608]{2,1,0:T(8,128)S(1)} collective-permute-done((f32[3,16,4608]{2,1,0:T(8,128)S(1)}, f32[3,16,4608]{2,1,0:T(8,128)S(1)}, u32[]{:S(2)}, u32[]{:S(2)}) %collective-permute-start.4) | collective-permute-done | bytes 884768 | tf_op jit(solution)/shard_map/ppermute | solution.py:416
  63.0 2.6 collective-permute-start.9
  67.6 15.3 %collective-permute-done.5 = f32[3,16,4608]{2,1,0:T(8,128)S(1)} collective-permute-done((f32[3,16,4608]{2,1,0:T(8,128)S(1)}, f32[3,16,4608]{2,1,0:T(8,128)S(1)}, u32[]{:S(2)}, u32[]{:S(2)}) %collective-permute-start.5) | collective-permute-done | bytes 884768 | tf_op jit(solution)/shard_map/ppermute | solution.py:416
  85.9 1.6 copy.17
  87.5 1.6 copy.16
  89.1 2.9 %slice.7 = f32[3,16,9216]{2,1,0:T(8,128)} slice(f32[3,128,9216]{2,1,0:T(8,128)} %bitcast.7), slice={[0:3], [0:16], [0:9216]} | slice | bytes 3538944 | tf_op jit(solution)/shard_map/slice | solution.py:400
  92.0 3.9 %collective-permute-start.2 = (f32[3,16,9216]{2,1,0:T(8,128)}, f32[3,16,9216]{2,1,0:T(8,128)S(1)}, u32[]{:S(2)}, u32[]{:S(2)}) collective-permute-start(f32[3,16,9216]{2,1,0:T(8,128)} %slice.7), channel_id=1, source_target_pairs={{16,0},{32,16},{48,32},{64,48},{80,64},{96,80},{112,96},{17,1},{33... | collective-permute-start | bytes 5308424 | tf_op jit(solution)/shard_map/ppermute | solution.py:401
  98.4 7.0 %collective-permute-done.6 = f32[3,16,4608]{2,1,0:T(8,128)} collective-permute-done((f32[3,16,4608]{2,1,0:T(8,128)}, f32[3,16,4608]{2,1,0:T(8,128)}, u32[]{:S(2)}, u32[]{:S(2)}) %collective-permute-start.6) | collective-permute-done | bytes 884768 | tf_op jit(solution)/shard_map/ppermute | solution.py:416
  105.4 2.8 %collective-permute-start.7 = (f32[3,16,4608]{2,1,0:T(8,128)}, f32[3,16,4608]{2,1,0:T(8,128)}, u32[]{:S(2)}, u32[]{:S(2)}) collective-permute-start(f32[3,16,4608]{2,1,0:T(8,128)} %collective-permute-done.6), channel_id=1, source_target_pairs={{0,16},{16,0},{32,48},{48,32},{64,80},{80,64},{96,112},{112,96},{1... | collective-permute-start | bytes 2654216 | tf_op jit(solution)/shard_map/ppermute | solution.py:417
  108.3 2.7 cut.6
  113.5 1.6 copy.18
  115.1 1.6 copy.19
  116.8 1.4 cut.7
  118.3 1.6 select_convert_fusion.bands_ref
  120.8 6.0 %collective-permute-done.2.head_ref = f32[3,16,9216]{2,1,0:T(8,128)S(1)} collective-permute-done((f32[3,16,9216]{2,1,0:T(8,128)}, f32[3,16,9216]{2,1,0:T(8,128)S(1)}, u32[]{:S(2)}, u32[]{:S(2)}) %collective-permute-start.2) | collective-permute-done | bytes 1769504 | tf_op jit(solution)/shard_map/ppermute | solution.py:401
  126.8 81.7 %collective-permute-start.13 = (f32[2,24,9216]{2,1,0:T(8,128)S(1)}, f32[2,24,9216]{2,1,0:T(8,128)S(1)}, u32[]{:S(2)}, u32[]{:S(2)}) collective-permute-start(f32[2,24,9216]{2,1,0:T(8,128)S(1)} %copy-done.7), channel_id=1, source_target_pairs={{0,1},{2,3},{4,5},{6,7},{8,9},{10,11},{12,13},{14,15},{1,0},{3,2},... | collective-permute-start | bytes 5308424 | tf_op jit(solution)/shard_map/ppermute | solution.py:390
  209.3 7.0 %collective-permute-start.15 = (f32[2,8,9216]{2,1,0:T(8,128)S(1)}, f32[2,8,9216]{2,1,0:T(8,128)S(1)}, u32[]{:S(2)}, u32[]{:S(2)}) collective-permute-start(f32[2,8,9216]{2,1,0:T(8,128)S(1)} %get-tuple-element.38), channel_id=1, source_target_pairs={{0,1},{2,3},{4,5},{6,7},{8,9},{10,11},{12,13},{14,15},{1,0},{3,2},... | collective-permute-start | bytes 1769480 | tf_op jit(solution)/shard_map/ppermute | solution.py:390
  216.3 2.8 %add_select_fusion.1.carried_ref = f32[3,16,9216]{2,1,0:T(8,128)S(1)} fusion(f32[3,16,9216]{2,1,0:T(8,128)} %collective-permute-done.3, f32[3,16,4608]{2,1,0:T(8,128)} %collective-permute-done.6, f32[3,16,4608]{2,1,0:T(8,128)} %collective-permute-done.7, f32[16]{0:T(128)S(1)} %get-tuple-element.40, pred[]{:T(512)S(6)} %eq.53), kind=kLoop, calls=%fused_computation.22 | loop fusion | flops 2654208 | bytes 5308481 | tf_op jit(solution)/shard_map/jit(_where)/select_n | solution.py:423
  219.1 27.8 %local_part.1.image_ref = f32[3,128,9216]{2,1,0:T(8,128)} custom-call(f32[128,160]{1,0:T(8,128)S(1)} %pad_maximum_fusion.table_ref, bf16[3,768,256]{2,1,0:T(8,128)(2,1)S(1)} %select_convert_fusion.bands_ref, f32[3,128,9216]{2,1,0:T(8,128)} %bitcast.10, f32[3,128,9216]{2,1,0:T(8,128)} %bitcast.11, f32[3,128,9216]{2,1,0:T(8,128)} %bitcast.12, ...), custom_call_target="tpu_custom_call" | custom-call | flops 3397386240 | bytes 28311552 | tf_op jit(solution)/shard_map/local_part/pallas_call | solution.py:234
  248.4 2.3 add_edges.4.image_ref
  250.6 4.7 %add_edges.5.image_ref = f32[3,128,9216]{2,1,0:T(8,128)} custom-call(f32[3,128,9216]{2,1,0:T(8,128)} %add_edges.4.image_ref, f32[2,24,9216]{2,1,0:T(8,128)S(1)} %collective-permute-done.8.odd_ref, f32[2,24,9216]{2,1,0:T(8,128)} %collective-permute-done.9.even_ref), custom_call_target="tpu_custom_call", output_to_operand_aliasing={{}: (0, {})} | custom-call | flops 5308416 | bytes 8847360 | tf_op jit(solution)/shard_map/add_edges/pallas_call | solution.py:352
  255.3 10.5 %add_edges.6.image_ref = f32[3,128,9216]{2,1,0:T(8,128)} custom-call(f32[3,128,9216]{2,1,0:T(8,128)} %add_edges.5.image_ref, f32[2,64,9216]{2,1,0:T(8,128)} %collective-permute-done.10.odd_ref, f32[2,64,9216]{2,1,0:T(8,128)} %collective-permute-done.11.even_ref), custom_call_target="tpu_custom_call", output_to_operand_aliasing={{}: (0, {})} | custom-call | flops 14155776 | bytes 23592960 | tf_op jit(solution)/shard_map/add_edges/pallas_call | solution.py:352
  265.8 4.3 %add_edges.7.image_ref = f32[3,128,9216]{2,1,0:T(8,128)} custom-call(f32[3,128,9216]{2,1,0:T(8,128)} %add_edges.6.image_ref, f32[2,24,9216]{2,1,0:T(8,128)S(1)} %collective-permute-done.12.odd_ref, f32[2,24,9216]{2,1,0:T(8,128)S(1)} %collective-permute-done.13.even_ref), custom_call_target="tpu_custom_call", output_to_operand_aliasing={{}: (0, {})} | custom-call | flops 5308416 | bytes 8847360 | tf_op jit(solution)/shard_map/add_edges/pallas_call | solution.py:352
  (76 shorter events, 19.7 us)
Async XLA Ops:
  1.3 20.0 %collective-permute-start = (f32[2,8,9216]{2,1,0:T(8,128)S(1)}, f32[2,8,9216]{2,1,0:T(8,128)S(1)}, u32[]{:S(2)}, u32[]{:S(2)}) collective-permute-start(f32[2,8,9216]{2,1,0:T(8,128)S(1)} %get-tuple-element.22), channel_id=1, source_target_pairs={{1,2},{3,4},{5,6},{7,8},{9,10},{11,12},{13,14},{2,1},{4,3},{6,5},{... | collective-permute-start | bytes 1769480 | tf_op jit(solution)/shard_map/ppermute | solution.py:389
  2.0 19.3 %collective-permute-start.1 = (f32[2,8,9216]{2,1,0:T(8,128)S(1)}, f32[2,8,9216]{2,1,0:T(8,128)S(1)}, u32[]{:S(2)}, u32[]{:S(2)}) collective-permute-start(f32[2,8,9216]{2,1,0:T(8,128)S(1)} %get-tuple-element.23), channel_id=1, source_target_pairs={{0,1},{2,3},{4,5},{6,7},{8,9},{10,11},{12,13},{14,15},{1,0},{3,2},... | collective-permute-start | bytes 1769480 | tf_op jit(solution)/shard_map/ppermute | solution.py:390
  11.2 9.9 %copy-start.16 = (f32[16]{0:T(128)S(1)}, f32[16]{0:T(128)}, u32[]{:S(2)}) copy-start(f32[16]{0:T(128)} %param.6) | copy-start | bytes 196
  11.2 9.9 %copy-start.17 = (f32[16]{0:T(128)S(1)}, f32[16]{0:T(128)}, u32[]{:S(2)}) copy-start(f32[16]{0:T(128)} %param.7) | copy-start | bytes 196
  19.0 2.2 copy-start.5
  21.2 10.6 %copy-start = (f32[2,8,9216]{2,1,0:T(8,128)}, f32[2,8,9216]{2,1,0:T(8,128)S(1)}, u32[]{:S(2)}) copy-start(f32[2,8,9216]{2,1,0:T(8,128)S(1)} %collective-permute-done.odd_ref) | copy-start | bytes 1769476
  21.3 10.6 %copy-start.2 = (f32[2,8,9216]{2,1,0:T(8,128)}, f32[2,8,9216]{2,1,0:T(8,128)S(1)}, u32[]{:S(2)}) copy-start(f32[2,8,9216]{2,1,0:T(8,128)S(1)} %collective-permute-done.1.even_ref) | copy-start | bytes 1769476
  31.9 4.8 %collective-permute-start.3 = (f32[3,16,9216]{2,1,0:T(8,128)S(1)}, f32[3,16,9216]{2,1,0:T(8,128)}, u32[]{:S(2)}, u32[]{:S(2)}) collective-permute-start(f32[3,16,9216]{2,1,0:T(8,128)S(1)} %block_sums.1), channel_id=1, source_target_pairs={{0,16},{16,0},{32,48},{48,32},{64,80},{80,64},{96,112},{112,96},{1... | collective-permute-start | bytes 5308424 | tf_op jit(solution)/shard_map/ppermute | solution.py:405
  38.1 22.7 %collective-permute-start.4 = (f32[3,16,4608]{2,1,0:T(8,128)S(1)}, f32[3,16,4608]{2,1,0:T(8,128)S(1)}, u32[]{:S(2)}, u32[]{:S(2)}) collective-permute-start(f32[3,16,4608]{2,1,0:T(8,128)S(1)} %add_select_fusion.2), channel_id=1, source_target_pairs={{32,0},{48,16},{64,32},{80,48},{96,64},{112,80},{33,1},{49,17},{65... | collective-permute-start | bytes 2654216 | tf_op jit(solution)/shard_map/ppermute | solution.py:416
  39.4 169.2 %collective-permute-start.10 = (f32[2,64,9216]{2,1,0:T(8,128)}, f32[2,64,9216]{2,1,0:T(8,128)}, u32[]{:S(2)}, u32[]{:S(2)}) collective-permute-start(f32[2,64,9216]{2,1,0:T(8,128)} %copy-done.5), channel_id=1, source_target_pairs={{1,2},{3,4},{5,6},{7,8},{9,10},{11,12},{13,14},{2,1},{4,3},{6,5},{... | collective-permute-start | bytes 14155784 | tf_op jit(solution)/shard_map/ppermute | solution.py:389
  60.9 22.0 %collective-permute-start.5 = (f32[3,16,4608]{2,1,0:T(8,128)S(1)}, f32[3,16,4608]{2,1,0:T(8,128)S(1)}, u32[]{:S(2)}, u32[]{:S(2)}) collective-permute-start(f32[3,16,4608]{2,1,0:T(8,128)S(1)} %multiply_add_fusion.1), channel_id=1, source_target_pairs={{32,0},{48,16},{64,32},{80,48},{96,64},{112,80},{33,1},{49,17},{65... | collective-permute-start | bytes 2654216 | tf_op jit(solution)/shard_map/ppermute | solution.py:416
  62.2 29.7 %collective-permute-start.8 = (f32[2,24,9216]{2,1,0:T(8,128)S(1)}, f32[2,24,9216]{2,1,0:T(8,128)S(1)}, u32[]{:S(2)}, u32[]{:S(2)}) collective-permute-start(f32[2,24,9216]{2,1,0:T(8,128)S(1)} %get-tuple-element.25), channel_id=1, source_target_pairs={{1,2},{3,4},{5,6},{7,8},{9,10},{11,12},{13,14},{2,1},{4,3},{6,5},{... | collective-permute-start | bytes 5308424 | tf_op jit(solution)/shard_map/ppermute | solution.py:389
  63.0 57.0 %collective-permute-start.9 = (f32[2,24,9216]{2,1,0:T(8,128)}, f32[2,24,9216]{2,1,0:T(8,128)}, u32[]{:S(2)}, u32[]{:S(2)}) collective-permute-start(f32[2,24,9216]{2,1,0:T(8,128)} %get-tuple-element.26), channel_id=1, source_target_pairs={{0,1},{2,3},{4,5},{6,7},{8,9},{10,11},{12,13},{14,15},{1,0},{3,2},... | collective-permute-start | bytes 5308424 | tf_op jit(solution)/shard_map/ppermute | solution.py:390
  65.6 189.7 %collective-permute-start.11 = (f32[2,64,9216]{2,1,0:T(8,128)}, f32[2,64,9216]{2,1,0:T(8,128)}, u32[]{:S(2)}, u32[]{:S(2)}) collective-permute-start(f32[2,64,9216]{2,1,0:T(8,128)} %get-tuple-element.29), channel_id=1, source_target_pairs={{0,1},{2,3},{4,5},{6,7},{8,9},{10,11},{12,13},{14,15},{1,0},{3,2},... | collective-permute-start | bytes 14155784 | tf_op jit(solution)/shard_map/ppermute | solution.py:390
  84.0 21.4 %collective-permute-start.6 = (f32[3,16,4608]{2,1,0:T(8,128)}, f32[3,16,4608]{2,1,0:T(8,128)}, u32[]{:S(2)}, u32[]{:S(2)}) collective-permute-start(f32[3,16,4608]{2,1,0:T(8,128)} %multiply_add_fusion), channel_id=1, source_target_pairs={{32,0},{48,16},{64,32},{80,48},{96,64},{112,80},{33,1},{49,17},{65... | collective-permute-start | bytes 2654216 | tf_op jit(solution)/shard_map/ppermute | solution.py:416
  89.1 6.8 %copy-start.18 = (f32[16]{0:T(128)S(1)}, f32[16]{0:T(128)}, u32[]{:S(2)}) copy-start(f32[16]{0:T(128)} %fusion.22) | copy-start | bytes 196
  89.1 6.8 %copy-start.12 = (s32[128,144]{0,1:T(8,128)S(1)}, s32[128,144]{0,1:T(8,128)}, u32[]{:S(2)}) copy-start(s32[128,144]{0,1:T(8,128)} %copy.16) | copy-start | bytes 221188
  89.1 7.6 %copy-start.14 = (f32[128,144]{0,1:T(8,128)S(1)}, f32[128,144]{0,1:T(8,128)}, u32[]{:S(2)}) copy-start(f32[128,144]{0,1:T(8,128)} %copy.17) | copy-start | bytes 221188
  92.0 34.9 %collective-permute-start.2 = (f32[3,16,9216]{2,1,0:T(8,128)}, f32[3,16,9216]{2,1,0:T(8,128)S(1)}, u32[]{:S(2)}, u32[]{:S(2)}) collective-permute-start(f32[3,16,9216]{2,1,0:T(8,128)} %slice.7), channel_id=1, source_target_pairs={{16,0},{32,16},{48,32},{64,48},{80,64},{96,80},{112,96},{17,1},{33... | collective-permute-start | bytes 5308424 | tf_op jit(solution)/shard_map/ppermute | solution.py:401
  105.4 103.8 %collective-permute-start.7 = (f32[3,16,4608]{2,1,0:T(8,128)}, f32[3,16,4608]{2,1,0:T(8,128)}, u32[]{:S(2)}, u32[]{:S(2)}) collective-permute-start(f32[3,16,4608]{2,1,0:T(8,128)} %collective-permute-done.6), channel_id=1, source_target_pairs={{0,16},{16,0},{32,48},{48,32},{64,80},{80,64},{96,112},{112,96},{1... | collective-permute-start | bytes 2654216 | tf_op jit(solution)/shard_map/ppermute | solution.py:417
  116.7 1.4 copy-start.10
  116.7 1.4 copy-start.11
  116.7 1.4 copy-start.15
  116.7 1.5 copy-start.13
  116.8 3.2 %copy-start.9 = (f32[2,24,9216]{2,1,0:T(8,128)S(1)}, f32[2,24,9216]{2,1,0:T(8,128)}, u32[]{:S(2)}) copy-start(f32[2,24,9216]{2,1,0:T(8,128)} %copy-done.8) | copy-start | bytes 5308420
  118.2 8.6 %copy-start.7 = (f32[2,24,9216]{2,1,0:T(8,128)S(1)}, f32[2,24,9216]{2,1,0:T(8,128)}, u32[]{:S(2)}) copy-start(f32[2,24,9216]{2,1,0:T(8,128)} %copy-done.6) | copy-start | bytes 5308420
  120.0 145.8 %collective-permute-start.12 = (f32[2,24,9216]{2,1,0:T(8,128)S(1)}, f32[2,24,9216]{2,1,0:T(8,128)S(1)}, u32[]{:S(2)}, u32[]{:S(2)}) collective-permute-start(f32[2,24,9216]{2,1,0:T(8,128)S(1)} %copy-done.9), channel_id=1, source_target_pairs={{1,2},{3,4},{5,6},{7,8},{9,10},{11,12},{13,14},{2,1},{4,3},{6,5},{... | collective-permute-start | bytes 5308424 | tf_op jit(solution)/shard_map/ppermute | solution.py:389
  126.8 139.0 %collective-permute-start.13 = (f32[2,24,9216]{2,1,0:T(8,128)S(1)}, f32[2,24,9216]{2,1,0:T(8,128)S(1)}, u32[]{:S(2)}, u32[]{:S(2)}) collective-permute-start(f32[2,24,9216]{2,1,0:T(8,128)S(1)} %copy-done.7), channel_id=1, source_target_pairs={{0,1},{2,3},{4,5},{6,7},{8,9},{10,11},{12,13},{14,15},{1,0},{3,2},... | collective-permute-start | bytes 5308424 | tf_op jit(solution)/shard_map/ppermute | solution.py:390
  208.6 61.6 %collective-permute-start.14 = (f32[2,8,9216]{2,1,0:T(8,128)S(1)}, f32[2,8,9216]{2,1,0:T(8,128)S(1)}, u32[]{:S(2)}, u32[]{:S(2)}) collective-permute-start(f32[2,8,9216]{2,1,0:T(8,128)S(1)} %get-tuple-element.37), channel_id=1, source_target_pairs={{1,2},{3,4},{5,6},{7,8},{9,10},{11,12},{13,14},{2,1},{4,3},{6,5},{... | collective-permute-start | bytes 1769480 | tf_op jit(solution)/shard_map/ppermute | solution.py:389
  209.3 9.8 %copy-start.4 = (f32[3,9216]{1,0:T(4,128)S(1)}, f32[3,9216]{1,0:T(4,128)}, u32[]{:S(2)}) copy-start(f32[3,9216]{1,0:T(4,128)} %absorb_ref.1) | copy-start | bytes 331780
  209.3 60.9 %collective-permute-start.15 = (f32[2,8,9216]{2,1,0:T(8,128)S(1)}, f32[2,8,9216]{2,1,0:T(8,128)S(1)}, u32[]{:S(2)}, u32[]{:S(2)}) collective-permute-start(f32[2,8,9216]{2,1,0:T(8,128)S(1)} %get-tuple-element.38), channel_id=1, source_target_pairs={{0,1},{2,3},{4,5},{6,7},{8,9},{10,11},{12,13},{14,15},{1,0},{3,2},... | collective-permute-start | bytes 1769480 | tf_op jit(solution)/shard_map/ppermute | solution.py:390
  246.9 1.5 copy-start.3
  (3 other events, 3.8 us)

commit v5 on v4

--- a/solution.py
+++ b/solution.py
@@ -16,7 +16,8 @@
 TILE = 2304
 SPAN = 768
 MIB = 1024 * 1024
-CHUNKS = (8, 24, 64, 24, 8)
+PIECES = 4
+CHUNKS = (16, 24, 56, 24, 8)
 
 
 def caputo_weights(count):
@@ -68,32 +69,131 @@
     return lax.axis_index("space") % 2
 
 
-def first_cut_kernel(first, field_ref, odd_ref, even_ref, sems):
+def lead_kernel(
+    first,
+    slabs,
+    field_ref,
+    below_ref,
+    above_ref,
+    odd_ref,
+    even_ref,
+    zero,
+    planes,
+    send_sems,
+    recv_sems,
+    local_sems,
+    turn,
+):
     depth = field_ref.shape[0]
-    rows = pl.ds(first, odd_ref.shape[1])
+    rows, plane = below_ref.shape[1:]
+    width = plane // PIECES
+    slab, group = lax.axis_index("space"), lax.axis_index("tm")
+    core = group % 2
+    partner = group + 1 - 2 * core
+    has_up, has_down = slab < slabs - 1, slab > 0
+    mesh_id = pl.DeviceIdType.MESH
+
+    barrier = pltpu.get_barrier_semaphore()
+    pl.semaphore_signal(barrier, inc=1, device_id={"tm": partner}, device_id_type=mesh_id)
+
+    @pl.when(has_up)
+    def _():
+        pl.semaphore_signal(barrier, inc=1, device_id={"space": slab + 1}, device_id_type=mesh_id)
+
+    @pl.when(has_down)
+    def _():
+        pl.semaphore_signal(barrier, inc=1, device_id={"space": slab - 1}, device_id_type=mesh_id)
+
+    pl.semaphore_wait(barrier, 1 + has_up.astype(jnp.int32) + has_down.astype(jnp.int32))
+
+    def piece(way, j):
+        lanes = pl.ds(j * width, width)
+        start, target, step = ((depth - 2, below_ref, 1), (0, above_ref, -1))[way]
+        return pltpu.make_async_remote_copy(
+            src_ref=field_ref.at[pl.ds(start, 2), pl.ds(0, rows), lanes],
+            dst_ref=target.at[:, :, lanes],
+            send_sem=send_sems.at[way, j],
+            recv_sem=recv_sems.at[way, j],
+            device_id={"space": slab + step},
+            device_id_type=mesh_id,
+        )
+
+    def on_both(act, pieces):
+        for way, has in ((0, has_up), (1, has_down)):
+
+            @pl.when(has)
+            def _(way=way):
+                for j in pieces:
+                    act(piece(way, j))
+
+    @pl.when(core == 0)
+    def _():
+        on_both(lambda copy: copy.start(), range(PIECES))
+
+    count = odd_ref.shape[1]
+    load = pltpu.make_async_copy(field_ref.at[:, pl.ds(first, count)], planes, local_sems.at[0])
+    load.start()
+    zero[...] = jnp.zeros_like(zero)
+    load.wait()
+    parity = odd_slab()
     up = depth - 2
-    parity = odd_slab()
-    copies = [
-        pltpu.make_async_copy(field_ref.at[pl.ds(parity * up, 2), rows], odd_ref, sems.at[0]),
-        pltpu.make_async_copy(field_ref.at[pl.ds((1 - parity) * up, 2), rows], even_ref, sems.at[1]),
+    stores = [
+        pltpu.make_async_copy(planes.at[pl.ds(parity * up, 2)], odd_ref, local_sems.at[1]),
+        pltpu.make_async_copy(planes.at[pl.ds((1 - parity) * up, 2)], even_ref, local_sems.at[2]),
     ]
-    for copy in copies:
-        copy.start()
-    for copy in copies:
-        copy.wait()
-
-
-def first_cut(field, first, rows):
-    piece = jax.ShapeDtypeStruct((2, rows, field.shape[2]), jnp.float32)
-    vmem = pl.BlockSpec(memory_space=pltpu.VMEM)
-    return pl.pallas_call(
-        functools.partial(first_cut_kernel, first),
-        out_shape=(piece, piece),
-        in_specs=[pl.BlockSpec(memory_space=pl.ANY)],
-        out_specs=(vmem, vmem),
-        scratch_shapes=[pltpu.SemaphoreType.DMA((2,))],
-        compiler_params=pltpu.CompilerParams(vmem_limit_bytes=46 * MIB),
-        name="first_cut",
+    for store in stores:
+        store.start()
+    for store in stores:
+        store.wait()
+
+    @pl.when(core == 0)
+    def _():
+        on_both(lambda copy: copy.wait_send(), range(PIECES - 1))
+        pl.semaphore_signal(turn, inc=1, device_id={"tm": partner}, device_id_type=mesh_id)
+        on_both(lambda copy: copy.wait_send(), range(PIECES - 1, PIECES))
+
+    @pl.when(core == 1)
+    def _():
+        pl.semaphore_wait(turn, 1)
+        on_both(lambda copy: copy.start(), range(PIECES))
+        on_both(lambda copy: copy.wait_send(), range(PIECES))
+
+    for has, way, target in ((has_down, 0, below_ref), (has_up, 1, above_ref)):
+
+        @pl.when(has)
+        def _(way=way):
+            for j in range(PIECES):
+                piece(way, j).wait_recv()
+
+        @pl.when(jnp.logical_not(has))
+        def _(target=target):
+            fill = pltpu.make_async_copy(zero, target, local_sems.at[0])
+            fill.start()
+            fill.wait()
+
+
+def lead(field, rows, first, count, slabs):
+    depth, _, plane = field.shape
+    arrived = jax.ShapeDtypeStruct((2, rows, plane), jnp.float32)
+    piece = jax.ShapeDtypeStruct((2, count, plane), jnp.float32)
+    anywhere = pl.BlockSpec(memory_space=pl.ANY)
+    return pl.pallas_call(
+        functools.partial(lead_kernel, first, slabs),
+        out_shape=(arrived, arrived, piece, piece),
+        in_specs=[anywhere],
+        out_specs=(anywhere,) * 4,
+        scratch_shapes=[
+            pltpu.VMEM((2, rows, plane), jnp.float32),
+            pltpu.VMEM((depth, count, plane), jnp.float32),
+            pltpu.SemaphoreType.DMA((2, PIECES)),
+            pltpu.SemaphoreType.DMA((2, PIECES)),
+            pltpu.SemaphoreType.DMA((3,)),
+            pltpu.SemaphoreType.REGULAR,
+        ],
+        compiler_params=pltpu.CompilerParams(
+            collective_id=0, has_side_effects=True, vmem_limit_bytes=50 * MIB
+        ),
+        name="lead",
     )(field)
 
 
@@ -279,9 +379,9 @@
     return below, above
 
 
-def edge_kernel(image_ref, odd_ref, even_ref, out_ref):
+def edge_kernel(sided, image_ref, one_ref, other_ref, out_ref):
     depth = image_ref.shape[0]
-    below, above = by_side(odd_ref, even_ref)
+    below, above = (one_ref, other_ref) if sided else by_side(one_ref, other_ref)
     terms = edge_terms(below, above, depth)
     for p in range(depth):
         out_ref[p] = image_ref[p] + terms[p]
@@ -345,12 +445,12 @@
     )(image, held, odd, even)
 
 
-def add_edges(image, odd, even, first, rows, width):
+def add_edges(image, one, other, first, rows, width, sided=False):
     depth, _, plane = image.shape
-    count = odd.shape[1]
+    count = one.shape[1]
     at = first // rows
     return pl.pallas_call(
-        edge_kernel,
+        functools.partial(edge_kernel, sided),
         out_shape=jax.ShapeDtypeStruct(image.shape, jnp.float32),
         grid=(count // rows, plane // width),
         in_specs=[
@@ -367,7 +467,7 @@
         ),
         compiler_params=pltpu.CompilerParams(vmem_limit_bytes=16 * MIB),
         name="add_edges",
-    )(image, odd, even)
+    )(image, one, other)
 
 
 def per_device(adjoint_field, absorption, mode_rates, mode_weights):
@@ -380,18 +480,18 @@
         pairs = [(i, i + 1) for i in range(lowest, slabs - 1, 2)]
         return pairs + [(j, i) for i, j in pairs]
 
-    odds, evens, starts = [], [], []
-    first = 0
+    starts = [sum(CHUNKS[:k]) for k in range(len(CHUNKS))]
+    below, above, over_odd, over_even = lead(field, CHUNKS[0], CHUNKS[0], CHUNKS[1], slabs)
+    odds, evens = [], []
     source = field
-    for k, count in enumerate(CHUNKS):
-        starts.append(first)
-        over_odd, over_even = (first_cut if k == 0 else cut)(source, first, count)
+    for k, count in enumerate(CHUNKS[1:], 1):
+        if k > 1:
+            over_odd, over_even = cut(source, starts[k], count)
         odds.append(lax.ppermute(over_odd, "space", both_ways(1)))
         evens.append(lax.ppermute(over_even, "space", both_ways(0)))
         source, _, _ = lax.optimization_barrier((source, over_odd, over_even))
-        if len(starts) == 3:
-            early, odds[0], evens[0] = lax.optimization_barrier((source, odds[0], evens[0]))
-        first += count
+        if k == 2:
+            early = source
 
     scaled = mode_rates / (steps * groups)
     mode_gain = mode_weights * jnp.sqrt(-jnp.expm1(-2.0 * scaled))
@@ -424,8 +524,9 @@
 
     image = local_part(table, stencil_bands(), field, head, carried, absorption)
     held = hold_rows(image, starts[-1], CHUNKS[-1])
-    for first, lower, upper in zip(starts[:-1], odds, evens):
-        image = add_edges(image, lower, upper, first, 8, plane)
+    image = add_edges(image, below, above, 0, 8, plane, sided=True)
+    for k in range(1, len(CHUNKS) - 1):
+        image = add_edges(image, odds[k - 1], evens[k - 1], starts[k], 8, plane)
     image = add_last(image, held, odds[-1], evens[-1], starts[-1])
     return jnp.transpose(image, (1, 0, 2))
 

time: 273 us -> 276 us (1.011)
  the two profiles are of different devices: /device:TPU:1 before, /device:TPU:29 now
where the time goes in v5:
time: 276 us; the launch traced here: 274 us
  waiting for transfers between devices  109 us (39%)
  Pallas kernels  105 us (38%)
  starting transfers between devices  30.8 us (11%)
  local copies, waits for them, and re-layouts  15.3 us (6%)
  other arithmetic  14.3 us (5%)
    ppermute x4, waiting for transfers between devices, per_device(): odds.append(lax.ppermute(over_odd, 'space', both_ways(1)))  36.8 us
    pallas_call x1, Pallas kernels, lead(): pl.pallas_call(functools.partial(lead_kernel, first, slabs), out_shape=(a...  31.8 us
    pallas_call x1, Pallas kernels, local_part(): pl.pallas_call(local_kernel, out_shape=jax.ShapeDtypeStruct(field.shape,...  27.8 us
    ppermute x1, waiting for transfers between devices, per_device(): lax.ppermute(mine_first, 'tm', [(g + 1, g) for g in range(groups - 1)])  26 us
    ppermute x3, waiting for transfers between devices, per_device(): later = lax.ppermute(sent, 'tm', [(g + 2, g) for g in range(groups - 2)])  23.6 us
    pallas_call x4, Pallas kernels, add_edges(): pl.pallas_call(functools.partial(edge_kernel, sided), out_shape=jax.Shape...  21.4 us
    ppermute x4, waiting for transfers between devices, per_device(): evens.append(lax.ppermute(over_even, 'space', both_ways(0)))  18.7 us
    ppermute x4, starting transfers between devices, per_device(): odds.append(lax.ppermute(over_odd, 'space', both_ways(1)))  18.2 us
  transfers between devices with their start and end apart: 14, of which 7 were waited for; matrix products, arithmetic and copies ran while one was open for 8% of the time, Pallas kernels for 20%

profile of v5, /device:TPU:29, one launch (start us, length us, event | category | flops | bytes accessed | tf_op | source)
XLA Modules:
  0.0 274.4 jit_solution(11507872718626521123)
XLA Ops:
  0.0 31.8 %lead.1 = (f32[2,16,9216]{2,1,0:T(8,128)S(1)}, f32[2,16,9216]{2,1,0:T(8,128)S(1)}, f32[2,24,9216]{2,1,0:T(8,128)}, f32[2,24,9216]{2,1,0:T(8,128)}) custom-call(f32[3,128,9216]{2,1,0:T(8,128)} %bitcast.3), custom_call_target="tpu_custom_call" | custom-call | tf_op jit(solution)/shard_map/lead/pallas_call | solution.py:180
  34.0 7.3 %cut.3 = (f32[2,56,9216]{2,1,0:T(8,128)S(1)}, f32[2,56,9216]{2,1,0:T(8,128)}) custom-call(f32[3,128,9216]{2,1,0:T(8,128)} %bitcast.4), custom_call_target="tpu_custom_call" | custom-call | bytes 14450688 | tf_op jit(solution)/shard_map/cut/pallas_call | solution.py:211
  41.3 2.0 copy-done.5
  43.4 10.2 %block_sums.1 = f32[3,16,9216]{2,1,0:T(8,128)S(1)} custom-call(f32[16,128]{1,0:T(8,128)S(1)} %multiply_exponential_fusion.projector_ref, f32[3,128,9216]{2,1,0:T(8,128)} %bitcast.5), custom_call_target="tpu_custom_call" | custom-call | flops 339738624 | bytes 15925248 | tf_op jit(solution)/shard_map/block_sums/pallas_call | solution.py:233
  53.7 3.7 %collective-permute-done.1 = f32[3,16,9216]{2,1,0:T(8,128)S(1)} collective-permute-done((f32[3,16,9216]{2,1,0:T(8,128)S(1)}, f32[3,16,9216]{2,1,0:T(8,128)S(1)}, u32[]{:S(2)}, u32[]{:S(2)}) %collective-permute-start.1) | collective-permute-done | bytes 1769504 | tf_op jit(solution)/shard_map/ppermute | solution.py:505
  57.6 2.2 collective-permute-start.2
  59.7 5.4 %collective-permute-start.8 = (f32[2,56,9216]{2,1,0:T(8,128)}, f32[2,56,9216]{2,1,0:T(8,128)}, u32[]{:S(2)}, u32[]{:S(2)}) collective-permute-start(f32[2,56,9216]{2,1,0:T(8,128)} %copy-done.5), channel_id=1, source_target_pairs={{1,2},{3,4},{5,6},{7,8},{9,10},{11,12},{13,14},{2,1},{4,3},{6,5},{... | collective-permute-start | bytes 12386312 | tf_op jit(solution)/shard_map/ppermute | solution.py:490
  65.1 15.5 %collective-permute-done.2 = f32[3,16,4608]{2,1,0:T(8,128)S(1)} collective-permute-done((f32[3,16,4608]{2,1,0:T(8,128)S(1)}, f32[3,16,4608]{2,1,0:T(8,128)S(1)}, u32[]{:S(2)}, u32[]{:S(2)}) %collective-permute-start.2) | collective-permute-done | bytes 884768 | tf_op jit(solution)/shard_map/ppermute | solution.py:516
  80.8 2.2 collective-permute-start.3
  84.6 3.1 %collective-permute-start = (f32[3,16,9216]{2,1,0:T(8,128)S(1)}, f32[3,16,9216]{2,1,0:T(8,128)S(1)}, u32[]{:S(2)}, u32[]{:S(2)}) collective-permute-start(f32[3,16,9216]{2,1,0:T(8,128)S(1)} %slice.7), channel_id=1, source_target_pairs={{16,0},{32,16},{48,32},{64,48},{80,64},{96,80},{112,96},{17,1},{33... | collective-permute-start | bytes 5308424 | tf_op jit(solution)/shard_map/ppermute | solution.py:501
  87.7 5.4 %collective-permute-start.6 = (f32[2,24,9216]{2,1,0:T(8,128)}, f32[2,24,9216]{2,1,0:T(8,128)S(1)}, u32[]{:S(2)}, u32[]{:S(2)}) collective-permute-start(f32[2,24,9216]{2,1,0:T(8,128)} %get-tuple-element.18), channel_id=1, source_target_pairs={{1,2},{3,4},{5,6},{7,8},{9,10},{11,12},{13,14},{2,1},{4,3},{6,5},{... | collective-permute-start | bytes 5308424 | tf_op jit(solution)/shard_map/ppermute | solution.py:490
  95.1 8.1 %collective-permute-done.3 = f32[3,16,4608]{2,1,0:T(8,128)S(1)} collective-permute-done((f32[3,16,4608]{2,1,0:T(8,128)S(1)}, f32[3,16,4608]{2,1,0:T(8,128)S(1)}, u32[]{:S(2)}, u32[]{:S(2)}) %collective-permute-start.3) | collective-permute-done | bytes 884768 | tf_op jit(solution)/shard_map/ppermute | solution.py:516
  104.2 2.2 collective-permute-start.4
  106.9 26.0 %collective-permute-done.head_ref = f32[3,16,9216]{2,1,0:T(8,128)S(1)} collective-permute-done((f32[3,16,9216]{2,1,0:T(8,128)S(1)}, f32[3,16,9216]{2,1,0:T(8,128)S(1)}, u32[]{:S(2)}, u32[]{:S(2)}) %collective-permute-start) | collective-permute-done | bytes 1769504 | tf_op jit(solution)/shard_map/ppermute | solution.py:501
  136.4 1.6 copy.16
  138.8 1.7 select_reduce_fusion
  140.5 1.8 multiply_reduce_fusion
  143.7 2.7 cut.4
  148.9 1.6 copy.18
  150.5 1.6 copy.19
  153.8 1.6 select_convert_fusion.bands_ref
  155.4 36.8 %collective-permute-done.6.one_ref = f32[2,24,9216]{2,1,0:T(8,128)S(1)} collective-permute-done((f32[2,24,9216]{2,1,0:T(8,128)}, f32[2,24,9216]{2,1,0:T(8,128)S(1)}, u32[]{:S(2)}, u32[]{:S(2)}) %collective-permute-start.6) | collective-permute-done | bytes 1769504 | tf_op jit(solution)/shard_map/ppermute | solution.py:490
  192.2 5.4 %collective-permute-start.10 = (f32[2,24,9216]{2,1,0:T(8,128)S(1)}, f32[2,24,9216]{2,1,0:T(8,128)S(1)}, u32[]{:S(2)}, u32[]{:S(2)}) collective-permute-start(f32[2,24,9216]{2,1,0:T(8,128)S(1)} %copy-done.9), channel_id=1, source_target_pairs={{1,2},{3,4},{5,6},{7,8},{9,10},{11,12},{13,14},{2,1},{4,3},{6,5},{... | collective-permute-start | bytes 5308424 | tf_op jit(solution)/shard_map/ppermute | solution.py:490
  197.7 2.0 collective-permute-start.12
  201.2 2.4 add_select_fusion.1.carried_ref
  203.6 27.8 %local_part.1.image_ref = f32[3,128,9216]{2,1,0:T(8,128)} custom-call(f32[128,160]{1,0:T(8,128)S(1)} %pad_maximum_fusion.table_ref, bf16[3,768,256]{2,1,0:T(8,128)(2,1)S(1)} %select_convert_fusion.bands_ref, f32[3,128,9216]{2,1,0:T(8,128)} %bitcast.9, f32[3,128,9216]{2,1,0:T(8,128)} %bitcast.10, f32[3,128,9216]{2,1,0:T(8,128)} %bitcast.11, ...), custom_call_target="tpu_custom_call" | custom-call | flops 3397386240 | bytes 28311552 | tf_op jit(solution)/shard_map/local_part/pallas_call | solution.py:334
  233.3 2.5 add_edges.4.image_ref
  235.8 4.7 %add_edges.5.image_ref = f32[3,128,9216]{2,1,0:T(8,128)} custom-call(f32[3,128,9216]{2,1,0:T(8,128)} %add_edges.4.image_ref, f32[2,24,9216]{2,1,0:T(8,128)S(1)} %collective-permute-done.6.one_ref, f32[2,24,9216]{2,1,0:T(8,128)} %collective-permute-done.7.other_ref), custom_call_target="tpu_custom_call", output_to_operand_aliasing={{}: (0, {})} | custom-call | flops 5308416 | bytes 8847360 | tf_op jit(solution)/shard_map/add_edges/pallas_call | solution.py:452
  240.4 10.0 %add_edges.6.image_ref = f32[3,128,9216]{2,1,0:T(8,128)} custom-call(f32[3,128,9216]{2,1,0:T(8,128)} %add_edges.5.image_ref, f32[2,56,9216]{2,1,0:T(8,128)} %collective-permute-done.8.one_ref, f32[2,56,9216]{2,1,0:T(8,128)} %collective-permute-done.9.other_ref), custom_call_target="tpu_custom_call", output_to_operand_aliasing={{}: (0, {})} | custom-call | flops 12386304 | bytes 20643840 | tf_op jit(solution)/shard_map/add_edges/pallas_call | solution.py:452
  250.4 11.8 %collective-permute-done.11.other_ref = f32[2,24,9216]{2,1,0:T(8,128)S(1)} collective-permute-done((f32[2,24,9216]{2,1,0:T(8,128)S(1)}, f32[2,24,9216]{2,1,0:T(8,128)S(1)}, u32[]{:S(2)}, u32[]{:S(2)}) %collective-permute-start.11) | collective-permute-done | bytes 1769504 | tf_op jit(solution)/shard_map/ppermute | solution.py:491
  262.3 4.3 %add_edges.7.image_ref = f32[3,128,9216]{2,1,0:T(8,128)} custom-call(f32[3,128,9216]{2,1,0:T(8,128)} %add_edges.6.image_ref, f32[2,24,9216]{2,1,0:T(8,128)S(1)} %collective-permute-done.10.one_ref, f32[2,24,9216]{2,1,0:T(8,128)S(1)} %collective-permute-done.11.other_ref), custom_call_target="tpu_custom_call", output_to_operand_aliasing={{}: (0, {})} | custom-call | flops 5308416 | bytes 8847360 | tf_op jit(solution)/shard_map/add_edges/pallas_call | solution.py:452
  266.6 6.8 %collective-permute-done.13.even_ref = f32[2,8,9216]{2,1,0:T(8,128)S(1)} collective-permute-done((f32[2,8,9216]{2,1,0:T(8,128)S(1)}, f32[2,8,9216]{2,1,0:T(8,128)S(1)}, u32[]{:S(2)}, u32[]{:S(2)}) %collective-permute-start.13) | collective-permute-done | bytes 589856 | tf_op jit(solution)/shard_map/ppermute | solution.py:491
  (69 shorter events, 21.9 us)
Async XLA Ops:
  31.8 1.0 copy-start
  32.8 1.1 copy-start.2
  34.0 9.3 %copy-start.16 = (f32[16]{0:T(128)S(1)}, f32[16]{0:T(128)}, u32[]{:S(2)}) copy-start(f32[16]{0:T(128)} %param.6) | copy-start | bytes 196
  34.0 9.3 %copy-start.17 = (f32[16]{0:T(128)S(1)}, f32[16]{0:T(128)}, u32[]{:S(2)}) copy-start(f32[16]{0:T(128)} %param.7) | copy-start | bytes 196
  41.3 2.0 copy-start.5
  53.6 3.8 %collective-permute-start.1 = (f32[3,16,9216]{2,1,0:T(8,128)S(1)}, f32[3,16,9216]{2,1,0:T(8,128)S(1)}, u32[]{:S(2)}, u32[]{:S(2)}) collective-permute-start(f32[3,16,9216]{2,1,0:T(8,128)S(1)} %block_sums.1), channel_id=1, source_target_pairs={{0,16},{16,0},{32,48},{48,32},{64,80},{80,64},{96,112},{112,96},{1... | collective-permute-start | bytes 5308424 | tf_op jit(solution)/shard_map/ppermute | solution.py:505
  57.3 23.5 %copy-start.10 = (f32[3,16,9216]{2,1,0:T(8,128)}, f32[3,16,9216]{2,1,0:T(8,128)S(1)}, u32[]{:S(2)}) copy-start(f32[3,16,9216]{2,1,0:T(8,128)S(1)} %collective-permute-done.1) | copy-start | bytes 5308420
  57.6 23.1 %collective-permute-start.2 = (f32[3,16,4608]{2,1,0:T(8,128)S(1)}, f32[3,16,4608]{2,1,0:T(8,128)S(1)}, u32[]{:S(2)}, u32[]{:S(2)}) collective-permute-start(f32[3,16,4608]{2,1,0:T(8,128)S(1)} %add_select_fusion.2), channel_id=1, source_target_pairs={{32,0},{48,16},{64,32},{80,48},{96,64},{112,80},{33,1},{49,17},{65... | collective-permute-start | bytes 2654216 | tf_op jit(solution)/shard_map/ppermute | solution.py:516
  59.7 138.0 %collective-permute-start.8 = (f32[2,56,9216]{2,1,0:T(8,128)}, f32[2,56,9216]{2,1,0:T(8,128)}, u32[]{:S(2)}, u32[]{:S(2)}) collective-permute-start(f32[2,56,9216]{2,1,0:T(8,128)} %copy-done.5), channel_id=1, source_target_pairs={{1,2},{3,4},{5,6},{7,8},{9,10},{11,12},{13,14},{2,1},{4,3},{6,5},{... | collective-permute-start | bytes 12386312 | tf_op jit(solution)/shard_map/ppermute | solution.py:490
  80.8 22.3 %collective-permute-start.3 = (f32[3,16,4608]{2,1,0:T(8,128)S(1)}, f32[3,16,4608]{2,1,0:T(8,128)S(1)}, u32[]{:S(2)}, u32[]{:S(2)}) collective-permute-start(f32[3,16,4608]{2,1,0:T(8,128)S(1)} %multiply_add_fusion.1), channel_id=1, source_target_pairs={{32,0},{48,16},{64,32},{80,48},{96,64},{112,80},{33,1},{49,17},{65... | collective-permute-start | bytes 2654216 | tf_op jit(solution)/shard_map/ppermute | solution.py:516
  84.6 48.3 %collective-permute-start = (f32[3,16,9216]{2,1,0:T(8,128)S(1)}, f32[3,16,9216]{2,1,0:T(8,128)S(1)}, u32[]{:S(2)}, u32[]{:S(2)}) collective-permute-start(f32[3,16,9216]{2,1,0:T(8,128)S(1)} %slice.7), channel_id=1, source_target_pairs={{16,0},{32,16},{48,32},{64,48},{80,64},{96,80},{112,96},{17,1},{33... | collective-permute-start | bytes 5308424 | tf_op jit(solution)/shard_map/ppermute | solution.py:501
  87.7 104.5 %collective-permute-start.6 = (f32[2,24,9216]{2,1,0:T(8,128)}, f32[2,24,9216]{2,1,0:T(8,128)S(1)}, u32[]{:S(2)}, u32[]{:S(2)}) collective-permute-start(f32[2,24,9216]{2,1,0:T(8,128)} %get-tuple-element.18), channel_id=1, source_target_pairs={{1,2},{3,4},{5,6},{7,8},{9,10},{11,12},{13,14},{2,1},{4,3},{6,5},{... | collective-permute-start | bytes 5308424 | tf_op jit(solution)/shard_map/ppermute | solution.py:490
  93.1 104.5 %collective-permute-start.7 = (f32[2,24,9216]{2,1,0:T(8,128)}, f32[2,24,9216]{2,1,0:T(8,128)}, u32[]{:S(2)}, u32[]{:S(2)}) collective-permute-start(f32[2,24,9216]{2,1,0:T(8,128)} %get-tuple-element.19), channel_id=1, source_target_pairs={{0,1},{2,3},{4,5},{6,7},{8,9},{10,11},{12,13},{14,15},{1,0},{3,2},... | collective-permute-start | bytes 5308424 | tf_op jit(solution)/shard_map/ppermute | solution.py:491
  104.2 39.5 %collective-permute-start.4 = (f32[3,16,4608]{2,1,0:T(8,128)}, f32[3,16,4608]{2,1,0:T(8,128)}, u32[]{:S(2)}, u32[]{:S(2)}) collective-permute-start(f32[3,16,4608]{2,1,0:T(8,128)} %multiply_add_fusion), channel_id=1, source_target_pairs={{32,0},{48,16},{64,32},{80,48},{96,64},{112,80},{33,1},{49,17},{65... | collective-permute-start | bytes 2654216 | tf_op jit(solution)/shard_map/ppermute | solution.py:516
  132.9 107.5 %collective-permute-start.9 = (f32[2,56,9216]{2,1,0:T(8,128)}, f32[2,56,9216]{2,1,0:T(8,128)}, u32[]{:S(2)}, u32[]{:S(2)}) collective-permute-start(f32[2,56,9216]{2,1,0:T(8,128)} %get-tuple-element.22), channel_id=1, source_target_pairs={{0,1},{2,3},{4,5},{6,7},{8,9},{10,11},{12,13},{14,15},{1,0},{3,2},... | collective-permute-start | bytes 12386312 | tf_op jit(solution)/shard_map/ppermute | solution.py:491
  143.7 56.0 %collective-permute-start.5 = (f32[3,16,4608]{2,1,0:T(8,128)}, f32[3,16,4608]{2,1,0:T(8,128)}, u32[]{:S(2)}, u32[]{:S(2)}) collective-permute-start(f32[3,16,4608]{2,1,0:T(8,128)} %collective-permute-done.4), channel_id=1, source_target_pairs={{0,16},{16,0},{32,48},{48,32},{64,80},{80,64},{96,112},{112,96},{1... | collective-permute-start | bytes 2654216 | tf_op jit(solution)/shard_map/ppermute | solution.py:517
  146.4 1.2 copy-start.6
  147.6 1.3 copy-start.8
  152.2 1.4 copy-start.12
  152.2 1.4 copy-start.13
  152.2 1.5 copy-start.15
  152.2 1.5 copy-start.14
  152.2 40.0 %copy-start.9 = (f32[2,24,9216]{2,1,0:T(8,128)S(1)}, f32[2,24,9216]{2,1,0:T(8,128)}, u32[]{:S(2)}) copy-start(f32[2,24,9216]{2,1,0:T(8,128)} %copy-done.8) | copy-start | bytes 5308420
  152.2 49.0 %copy-start.11 = (f32[3,16,9216]{2,1,0:T(8,128)S(1)}, f32[3,16,9216]{2,1,0:T(8,128)}, u32[]{:S(2)}) copy-start(f32[3,16,9216]{2,1,0:T(8,128)} %copy-done.10) | copy-start | bytes 5308420
  153.6 44.0 %copy-start.7 = (f32[2,24,9216]{2,1,0:T(8,128)S(1)}, f32[2,24,9216]{2,1,0:T(8,128)}, u32[]{:S(2)}) copy-start(f32[2,24,9216]{2,1,0:T(8,128)} %copy-done.6) | copy-start | bytes 5308420
  192.2 58.2 %collective-permute-start.10 = (f32[2,24,9216]{2,1,0:T(8,128)S(1)}, f32[2,24,9216]{2,1,0:T(8,128)S(1)}, u32[]{:S(2)}, u32[]{:S(2)}) collective-permute-start(f32[2,24,9216]{2,1,0:T(8,128)S(1)} %copy-done.9), channel_id=1, source_target_pairs={{1,2},{3,4},{5,6},{7,8},{9,10},{11,12},{13,14},{2,1},{4,3},{6,5},{... | collective-permute-start | bytes 5308424 | tf_op jit(solution)/shard_map/ppermute | solution.py:490
  197.6 64.7 %collective-permute-start.11 = (f32[2,24,9216]{2,1,0:T(8,128)S(1)}, f32[2,24,9216]{2,1,0:T(8,128)S(1)}, u32[]{:S(2)}, u32[]{:S(2)}) collective-permute-start(f32[2,24,9216]{2,1,0:T(8,128)S(1)} %copy-done.7), channel_id=1, source_target_pairs={{0,1},{2,3},{4,5},{6,7},{8,9},{10,11},{12,13},{14,15},{1,0},{3,2},... | collective-permute-start | bytes 5308424 | tf_op jit(solution)/shard_map/ppermute | solution.py:491
  197.7 68.9 %collective-permute-start.12 = (f32[2,8,9216]{2,1,0:T(8,128)S(1)}, f32[2,8,9216]{2,1,0:T(8,128)S(1)}, u32[]{:S(2)}, u32[]{:S(2)}) collective-permute-start(f32[2,8,9216]{2,1,0:T(8,128)S(1)} %get-tuple-element.29), channel_id=1, source_target_pairs={{1,2},{3,4},{5,6},{7,8},{9,10},{11,12},{13,14},{2,1},{4,3},{6,5},{... | collective-permute-start | bytes 1769480 | tf_op jit(solution)/shard_map/ppermute | solution.py:490
  199.7 3.9 %copy-start.4 = (f32[3,9216]{1,0:T(4,128)S(1)}, f32[3,9216]{1,0:T(4,128)}, u32[]{:S(2)}) copy-start(f32[3,9216]{1,0:T(4,128)} %absorb_ref.1) | copy-start | bytes 331780
  199.7 73.7 %collective-permute-start.13 = (f32[2,8,9216]{2,1,0:T(8,128)S(1)}, f32[2,8,9216]{2,1,0:T(8,128)S(1)}, u32[]{:S(2)}, u32[]{:S(2)}) collective-permute-start(f32[2,8,9216]{2,1,0:T(8,128)S(1)} %get-tuple-element.30), channel_id=1, source_target_pairs={{0,1},{2,3},{4,5},{6,7},{8,9},{10,11},{12,13},{14,15},{1,0},{3,2},... | collective-permute-start | bytes 1769480 | tf_op jit(solution)/shard_map/ppermute | solution.py:491
  231.4 1.5 copy-start.1
  231.4 1.9 copy-start.3

commit v6 on v5

--- a/solution.py
+++ b/solution.py
@@ -17,7 +17,7 @@
 SPAN = 768
 MIB = 1024 * 1024
 PIECES = 4
-CHUNKS = (16, 24, 56, 24, 8)
+CHUNKS = (16, 32, 48, 24, 8)
 
 
 def caputo_weights(count):
@@ -191,7 +191,7 @@
             pltpu.SemaphoreType.REGULAR,
         ],
         compiler_params=pltpu.CompilerParams(
-            collective_id=0, has_side_effects=True, vmem_limit_bytes=50 * MIB
+            collective_id=0, has_side_effects=True, vmem_limit_bytes=58 * MIB
         ),
         name="lead",
     )(field)
@@ -490,7 +490,7 @@
         odds.append(lax.ppermute(over_odd, "space", both_ways(1)))
         evens.append(lax.ppermute(over_even, "space", both_ways(0)))
         source, _, _ = lax.optimization_barrier((source, over_odd, over_even))
-        if k == 2:
+        if k == 1:
             early = source
 
     scaled = mode_rates / (steps * groups)

time: 276 us -> 275 us (level)
  the two profiles are of different devices: /device:TPU:29 before, /device:TPU:1 now
where the time goes in v6:
time: 275 us; the launch traced here: 271 us
  Pallas kernels  102 us (37%)
  starting transfers between devices  96.3 us (35%)
  waiting for transfers between devices  48.3 us (18%)
  other arithmetic  13.5 us (5%)
  local copies, waits for them, and re-layouts  9.96 us (4%)
    ppermute x4, starting transfers between devices, per_device(): evens.append(lax.ppermute(over_even, 'space', both_ways(0)))  78.7 us
    pallas_call x1, Pallas kernels, lead(): pl.pallas_call(functools.partial(lead_kernel, first, slabs), out_shape=(a...  32 us
    pallas_call x1, Pallas kernels, local_part(): pl.pallas_call(local_kernel, out_shape=jax.ShapeDtypeStruct(field.shape,...  27.9 us
    ppermute x1, waiting for transfers between devices, per_device(): lax.ppermute(mine_first, 'tm', [(g + 1, g) for g in range(groups - 1)])  22.5 us
    ppermute x3, waiting for transfers between devices, per_device(): later = lax.ppermute(sent, 'tm', [(g + 2, g) for g in range(groups - 2)])  22.1 us
    pallas_call x4, Pallas kernels, add_edges(): pl.pallas_call(functools.partial(edge_kernel, sided), out_shape=jax.Shape...  19.8 us
    pallas_call x1, Pallas kernels, block_sums(): pl.pallas_call(project_kernel, out_shape=jax.ShapeDtypeStruct((depth, mod...  10.2 us
    pallas_call x3, Pallas kernels, cut(): pl.pallas_call(cut_kernel, out_shape=(piece, piece), grid=(count // 8,),...  9.92 us
  transfers between devices with their start and end apart: 14, of which 4 were waited for; matrix products, arithmetic and copies ran while one was open for 8% of the time, Pallas kernels for 22%

profile of v6, /device:TPU:1, one launch (start us, length us, event | category | flops | bytes accessed | tf_op | source)
XLA Modules:
  0.0 270.6 jit_solution(5722874593631889341)
XLA Ops:
  0.0 32.0 %lead.1 = (f32[2,16,9216]{2,1,0:T(8,128)}, f32[2,16,9216]{2,1,0:T(8,128)}, f32[2,32,9216]{2,1,0:T(8,128)}, f32[2,32,9216]{2,1,0:T(8,128)}) custom-call(f32[3,128,9216]{2,1,0:T(8,128)} %bitcast.3), custom_call_target="tpu_custom_call" | custom-call | tf_op jit(solution)/shard_map/lead/pallas_call | solution.py:180
  32.1 10.2 %block_sums.1 = f32[3,16,9216]{2,1,0:T(8,128)S(1)} custom-call(f32[16,128]{1,0:T(8,128)S(1)} %multiply_exponential_fusion.projector_ref, f32[3,128,9216]{2,1,0:T(8,128)} %bitcast.4), custom_call_target="tpu_custom_call" | custom-call | flops 339738624 | bytes 15925248 | tf_op jit(solution)/shard_map/block_sums/pallas_call | solution.py:233
  42.4 3.7 %collective-permute-done.1 = f32[3,16,9216]{2,1,0:T(8,128)S(1)} collective-permute-done((f32[3,16,9216]{2,1,0:T(8,128)S(1)}, f32[3,16,9216]{2,1,0:T(8,128)S(1)}, u32[]{:S(2)}, u32[]{:S(2)}) %collective-permute-start.1) | collective-permute-done | bytes 1769504 | tf_op jit(solution)/shard_map/ppermute | solution.py:505
  46.3 1.3 collective-permute-start.2
  47.6 21.7 %collective-permute-done.2 = f32[3,16,4608]{2,1,0:T(8,128)S(1)} collective-permute-done((f32[3,16,4608]{2,1,0:T(8,128)S(1)}, f32[3,16,4608]{2,1,0:T(8,128)S(1)}, u32[]{:S(2)}, u32[]{:S(2)}) %collective-permute-start.2) | collective-permute-done | bytes 884768 | tf_op jit(solution)/shard_map/ppermute | solution.py:516
  69.4 1.3 collective-permute-start.3
  70.7 5.9 %cut.3 = (f32[2,48,9216]{2,1,0:T(8,128)}, f32[2,48,9216]{2,1,0:T(8,128)S(1)}) custom-call(f32[3,128,9216]{2,1,0:T(8,128)} %bitcast.5), custom_call_target="tpu_custom_call" | custom-call | bytes 12386304 | tf_op jit(solution)/shard_map/cut/pallas_call | solution.py:211
  77.5 2.2 collective-permute-start.6
  79.7 3.7 %collective-permute-start.7 = (f32[2,32,9216]{2,1,0:T(8,128)}, f32[2,32,9216]{2,1,0:T(8,128)}, u32[]{:S(2)}, u32[]{:S(2)}) collective-permute-start(f32[2,32,9216]{2,1,0:T(8,128)} %get-tuple-element.19), channel_id=1, source_target_pairs={{0,1},{2,3},{4,5},{6,7},{8,9},{10,11},{12,13},{14,15},{1,0},{3,2},... | collective-permute-start | bytes 7077896 | tf_op jit(solution)/shard_map/ppermute | solution.py:491
  83.4 2.8 %slice.7 = f32[3,16,9216]{2,1,0:T(8,128)} slice(f32[3,128,9216]{2,1,0:T(8,128)} %bitcast.6), slice={[0:3], [0:16], [0:9216]} | slice | bytes 3538944 | tf_op jit(solution)/shard_map/slice | solution.py:500
  86.2 3.7 %collective-permute-start = (f32[3,16,9216]{2,1,0:T(8,128)}, f32[3,16,9216]{2,1,0:T(8,128)}, u32[]{:S(2)}, u32[]{:S(2)}) collective-permute-start(f32[3,16,9216]{2,1,0:T(8,128)} %slice.7), channel_id=1, source_target_pairs={{16,0},{32,16},{48,32},{64,48},{80,64},{96,80},{112,96},{17,1},{33... | collective-permute-start | bytes 5308424 | tf_op jit(solution)/shard_map/ppermute | solution.py:501
  94.6 1.6 copy.16
  96.9 1.7 select_reduce_fusion
  98.6 1.3 exponential_multiply_fusion
  100.0 22.5 %collective-permute-done.head_ref = f32[3,16,9216]{2,1,0:T(8,128)} collective-permute-done((f32[3,16,9216]{2,1,0:T(8,128)}, f32[3,16,9216]{2,1,0:T(8,128)}, u32[]{:S(2)}, u32[]{:S(2)}) %collective-permute-start) | collective-permute-done | bytes 1769504 | tf_op jit(solution)/shard_map/ppermute | solution.py:501
  123.4 1.6 copy.17
  125.1 1.8 multiply_reduce_fusion
  126.9 5.5 %collective-permute-start.5 = (f32[3,16,4608]{2,1,0:T(8,128)}, f32[3,16,4608]{2,1,0:T(8,128)}, u32[]{:S(2)}, u32[]{:S(2)}) collective-permute-start(f32[3,16,4608]{2,1,0:T(8,128)} %collective-permute-done.4), channel_id=1, source_target_pairs={{0,16},{16,0},{32,48},{48,32},{64,80},{80,64},{96,112},{112,96},{1... | collective-permute-start | bytes 2654216 | tf_op jit(solution)/shard_map/ppermute | solution.py:517
  132.3 1.6 copy.19
  134.0 1.6 copy.18
  135.6 2.7 cut.4
  138.4 1.3 cut.5
  139.9 1.6 select_convert_fusion.bands_ref
  142.3 67.7 %collective-permute-start.11 = (f32[2,24,9216]{2,1,0:T(8,128)S(1)}, f32[2,24,9216]{2,1,0:T(8,128)S(1)}, u32[]{:S(2)}, u32[]{:S(2)}) collective-permute-start(f32[2,24,9216]{2,1,0:T(8,128)S(1)} %get-tuple-element.27), channel_id=1, source_target_pairs={{0,1},{2,3},{4,5},{6,7},{8,9},{10,11},{12,13},{14,15},{1,0},{3,2},... | collective-permute-start | bytes 5308424 | tf_op jit(solution)/shard_map/ppermute | solution.py:491
  210.7 6.9 %collective-permute-start.13 = (f32[2,8,9216]{2,1,0:T(8,128)S(1)}, f32[2,8,9216]{2,1,0:T(8,128)S(1)}, u32[]{:S(2)}, u32[]{:S(2)}) collective-permute-start(f32[2,8,9216]{2,1,0:T(8,128)S(1)} %get-tuple-element.30), channel_id=1, source_target_pairs={{0,1},{2,3},{4,5},{6,7},{8,9},{10,11},{12,13},{14,15},{1,0},{3,2},... | collective-permute-start | bytes 1769480 | tf_op jit(solution)/shard_map/ppermute | solution.py:491
  217.6 2.3 add_select_fusion.1.carried_ref
  220.0 27.9 %local_part.1.image_ref = f32[3,128,9216]{2,1,0:T(8,128)} custom-call(f32[128,160]{1,0:T(8,128)S(1)} %pad_maximum_fusion.table_ref, bf16[3,768,256]{2,1,0:T(8,128)(2,1)S(1)} %select_convert_fusion.bands_ref, f32[3,128,9216]{2,1,0:T(8,128)} %bitcast.9, f32[3,128,9216]{2,1,0:T(8,128)} %bitcast.10, f32[3,128,9216]{2,1,0:T(8,128)} %bitcast.11, ...), custom_call_target="tpu_custom_call" | custom-call | flops 3397386240 | bytes 28311552 | tf_op jit(solution)/shard_map/local_part/pallas_call | solution.py:334
  247.9 1.3 hold_rows.1.held_ref
  249.8 2.5 add_edges.4.image_ref
  252.3 5.6 %add_edges.5.image_ref = f32[3,128,9216]{2,1,0:T(8,128)} custom-call(f32[3,128,9216]{2,1,0:T(8,128)} %add_edges.4.image_ref, f32[2,32,9216]{2,1,0:T(8,128)} %collective-permute-done.6.one_ref, f32[2,32,9216]{2,1,0:T(8,128)} %collective-permute-done.7.other_ref), custom_call_target="tpu_custom_call", output_to_operand_aliasing={{}: (0, {})} | custom-call | flops 7077888 | bytes 11796480 | tf_op jit(solution)/shard_map/add_edges/pallas_call | solution.py:452
  257.9 7.3 %add_edges.6.image_ref = f32[3,128,9216]{2,1,0:T(8,128)} custom-call(f32[3,128,9216]{2,1,0:T(8,128)} %add_edges.5.image_ref, f32[2,48,9216]{2,1,0:T(8,128)S(1)} %collective-permute-done.8.one_ref, f32[2,48,9216]{2,1,0:T(8,128)} %collective-permute-done.9.other_ref), custom_call_target="tpu_custom_call", output_to_operand_aliasing={{}: (0, {})} | custom-call | flops 10616832 | bytes 17694720 | tf_op jit(solution)/shard_map/add_edges/pallas_call | solution.py:452
  265.3 4.3 %add_edges.7.image_ref = f32[3,128,9216]{2,1,0:T(8,128)} custom-call(f32[3,128,9216]{2,1,0:T(8,128)} %add_edges.6.image_ref, f32[2,24,9216]{2,1,0:T(8,128)S(1)} %collective-permute-done.10.one_ref, f32[2,24,9216]{2,1,0:T(8,128)S(1)} %collective-permute-done.11.other_ref), custom_call_target="tpu_custom_call", output_to_operand_aliasing={{}: (0, {})} | custom-call | flops 5308416 | bytes 8847360 | tf_op jit(solution)/shard_map/add_edges/pallas_call | solution.py:452
  (57 shorter events, 10.9 us)
Async XLA Ops:
  0.0 32.0 %copy-start.10 = (f32[16]{0:T(128)S(1)}, f32[16]{0:T(128)}, u32[]{:S(2)}) copy-start(f32[16]{0:T(128)} %param.6) | copy-start | bytes 196
  0.0 32.0 %copy-start.11 = (f32[16]{0:T(128)S(1)}, f32[16]{0:T(128)}, u32[]{:S(2)}) copy-start(f32[16]{0:T(128)} %param.7) | copy-start | bytes 196
  42.3 3.8 %collective-permute-start.1 = (f32[3,16,9216]{2,1,0:T(8,128)S(1)}, f32[3,16,9216]{2,1,0:T(8,128)S(1)}, u32[]{:S(2)}, u32[]{:S(2)}) collective-permute-start(f32[3,16,9216]{2,1,0:T(8,128)S(1)} %block_sums.1), channel_id=1, source_target_pairs={{0,16},{16,0},{32,48},{48,32},{64,80},{80,64},{96,112},{112,96},{1... | collective-permute-start | bytes 5308424 | tf_op jit(solution)/shard_map/ppermute | solution.py:505
  46.1 23.3 %copy-start.4 = (f32[3,16,9216]{2,1,0:T(8,128)}, f32[3,16,9216]{2,1,0:T(8,128)S(1)}, u32[]{:S(2)}) copy-start(f32[3,16,9216]{2,1,0:T(8,128)S(1)} %collective-permute-done.1) | copy-start | bytes 5308420
  46.3 23.0 %collective-permute-start.2 = (f32[3,16,4608]{2,1,0:T(8,128)S(1)}, f32[3,16,4608]{2,1,0:T(8,128)S(1)}, u32[]{:S(2)}, u32[]{:S(2)}) collective-permute-start(f32[3,16,4608]{2,1,0:T(8,128)S(1)} %add_select_fusion.2), channel_id=1, source_target_pairs={{32,0},{48,16},{64,32},{80,48},{96,64},{112,80},{33,1},{49,17},{65... | collective-permute-start | bytes 2654216 | tf_op jit(solution)/shard_map/ppermute | solution.py:516
  69.4 22.2 %collective-permute-start.3 = (f32[3,16,4608]{2,1,0:T(8,128)S(1)}, f32[3,16,4608]{2,1,0:T(8,128)S(1)}, u32[]{:S(2)}, u32[]{:S(2)}) collective-permute-start(f32[3,16,4608]{2,1,0:T(8,128)S(1)} %multiply_add_fusion.1), channel_id=1, source_target_pairs={{32,0},{48,16},{64,32},{80,48},{96,64},{112,80},{33,1},{49,17},{65... | collective-permute-start | bytes 2654216 | tf_op jit(solution)/shard_map/ppermute | solution.py:516
  76.7 9.5 %copy-start.3 = (f32[2,48,9216]{2,1,0:T(8,128)}, f32[2,48,9216]{2,1,0:T(8,128)S(1)}, u32[]{:S(2)}) copy-start(f32[2,48,9216]{2,1,0:T(8,128)S(1)} %get-tuple-element.24) | copy-start | bytes 10616836
  76.7 133.3 %collective-permute-start.8 = (f32[2,48,9216]{2,1,0:T(8,128)}, f32[2,48,9216]{2,1,0:T(8,128)S(1)}, u32[]{:S(2)}, u32[]{:S(2)}) collective-permute-start(f32[2,48,9216]{2,1,0:T(8,128)} %get-tuple-element.23), channel_id=1, source_target_pairs={{1,2},{3,4},{5,6},{7,8},{9,10},{11,12},{13,14},{2,1},{4,3},{6,5},{... | collective-permute-start | bytes 10616840 | tf_op jit(solution)/shard_map/ppermute | solution.py:490
  77.5 64.0 %collective-permute-start.6 = (f32[2,32,9216]{2,1,0:T(8,128)}, f32[2,32,9216]{2,1,0:T(8,128)}, u32[]{:S(2)}, u32[]{:S(2)}) collective-permute-start(f32[2,32,9216]{2,1,0:T(8,128)} %get-tuple-element.18), channel_id=1, source_target_pairs={{1,2},{3,4},{5,6},{7,8},{9,10},{11,12},{13,14},{2,1},{4,3},{6,5},{... | collective-permute-start | bytes 7077896 | tf_op jit(solution)/shard_map/ppermute | solution.py:490
  79.7 62.6 %collective-permute-start.7 = (f32[2,32,9216]{2,1,0:T(8,128)}, f32[2,32,9216]{2,1,0:T(8,128)}, u32[]{:S(2)}, u32[]{:S(2)}) collective-permute-start(f32[2,32,9216]{2,1,0:T(8,128)} %get-tuple-element.19), channel_id=1, source_target_pairs={{0,1},{2,3},{4,5},{6,7},{8,9},{10,11},{12,13},{14,15},{1,0},{3,2},... | collective-permute-start | bytes 7077896 | tf_op jit(solution)/shard_map/ppermute | solution.py:491
  86.2 36.3 %collective-permute-start = (f32[3,16,9216]{2,1,0:T(8,128)}, f32[3,16,9216]{2,1,0:T(8,128)}, u32[]{:S(2)}, u32[]{:S(2)}) collective-permute-start(f32[3,16,9216]{2,1,0:T(8,128)} %slice.7), channel_id=1, source_target_pairs={{16,0},{32,16},{48,32},{64,48},{80,64},{96,80},{112,96},{17,1},{33... | collective-permute-start | bytes 5308424 | tf_op jit(solution)/shard_map/ppermute | solution.py:501
  92.7 34.2 %collective-permute-start.4 = (f32[3,16,4608]{2,1,0:T(8,128)}, f32[3,16,4608]{2,1,0:T(8,128)}, u32[]{:S(2)}, u32[]{:S(2)}) collective-permute-start(f32[3,16,4608]{2,1,0:T(8,128)} %multiply_add_fusion), channel_id=1, source_target_pairs={{32,0},{48,16},{64,32},{80,48},{96,64},{112,80},{33,1},{49,17},{65... | collective-permute-start | bytes 2654216 | tf_op jit(solution)/shard_map/ppermute | solution.py:516
  122.5 135.4 %collective-permute-start.9 = (f32[2,48,9216]{2,1,0:T(8,128)}, f32[2,48,9216]{2,1,0:T(8,128)}, u32[]{:S(2)}, u32[]{:S(2)}) collective-permute-start(f32[2,48,9216]{2,1,0:T(8,128)} %copy-done.3), channel_id=1, source_target_pairs={{0,1},{2,3},{4,5},{6,7},{8,9},{10,11},{12,13},{14,15},{1,0},{3,2},... | collective-permute-start | bytes 10616840 | tf_op jit(solution)/shard_map/ppermute | solution.py:491
  126.9 83.8 %collective-permute-start.5 = (f32[3,16,4608]{2,1,0:T(8,128)}, f32[3,16,4608]{2,1,0:T(8,128)}, u32[]{:S(2)}, u32[]{:S(2)}) collective-permute-start(f32[3,16,4608]{2,1,0:T(8,128)} %collective-permute-done.4), channel_id=1, source_target_pairs={{0,16},{16,0},{32,48},{48,32},{64,80},{80,64},{96,112},{112,96},{1... | collective-permute-start | bytes 2654216 | tf_op jit(solution)/shard_map/ppermute | solution.py:517
  138.3 1.4 copy-start.6
  138.3 1.4 copy-start.7
  138.3 1.4 copy-start.9
  138.4 1.4 copy-start.8
  139.7 77.9 %copy-start.5 = (f32[3,16,9216]{2,1,0:T(8,128)S(1)}, f32[3,16,9216]{2,1,0:T(8,128)}, u32[]{:S(2)}) copy-start(f32[3,16,9216]{2,1,0:T(8,128)} %copy-done.4) | copy-start | bytes 5308420
  141.5 123.8 %collective-permute-start.10 = (f32[2,24,9216]{2,1,0:T(8,128)S(1)}, f32[2,24,9216]{2,1,0:T(8,128)S(1)}, u32[]{:S(2)}, u32[]{:S(2)}) collective-permute-start(f32[2,24,9216]{2,1,0:T(8,128)S(1)} %get-tuple-element.26), channel_id=1, source_target_pairs={{1,2},{3,4},{5,6},{7,8},{9,10},{11,12},{13,14},{2,1},{4,3},{6,5},{... | collective-permute-start | bytes 5308424 | tf_op jit(solution)/shard_map/ppermute | solution.py:490
  142.3 123.0 %collective-permute-start.11 = (f32[2,24,9216]{2,1,0:T(8,128)S(1)}, f32[2,24,9216]{2,1,0:T(8,128)S(1)}, u32[]{:S(2)}, u32[]{:S(2)}) collective-permute-start(f32[2,24,9216]{2,1,0:T(8,128)S(1)} %get-tuple-element.27), channel_id=1, source_target_pairs={{0,1},{2,3},{4,5},{6,7},{8,9},{10,11},{12,13},{14,15},{1,0},{3,2},... | collective-permute-start | bytes 5308424 | tf_op jit(solution)/shard_map/ppermute | solution.py:491
  210.0 59.6 %collective-permute-start.12 = (f32[2,8,9216]{2,1,0:T(8,128)S(1)}, f32[2,8,9216]{2,1,0:T(8,128)S(1)}, u32[]{:S(2)}, u32[]{:S(2)}) collective-permute-start(f32[2,8,9216]{2,1,0:T(8,128)S(1)} %get-tuple-element.29), channel_id=1, source_target_pairs={{1,2},{3,4},{5,6},{7,8},{9,10},{11,12},{13,14},{2,1},{4,3},{6,5},{... | collective-permute-start | bytes 1769480 | tf_op jit(solution)/shard_map/ppermute | solution.py:490
  210.7 9.3 %copy-start.2 = (f32[3,9216]{1,0:T(4,128)S(1)}, f32[3,9216]{1,0:T(4,128)}, u32[]{:S(2)}) copy-start(f32[3,9216]{1,0:T(4,128)} %absorb_ref.1) | copy-start | bytes 331780
  210.7 58.9 %collective-permute-start.13 = (f32[2,8,9216]{2,1,0:T(8,128)S(1)}, f32[2,8,9216]{2,1,0:T(8,128)S(1)}, u32[]{:S(2)}, u32[]{:S(2)}) collective-permute-start(f32[2,8,9216]{2,1,0:T(8,128)S(1)} %get-tuple-element.30), channel_id=1, source_target_pairs={{0,1},{2,3},{4,5},{6,7},{8,9},{10,11},{12,13},{14,15},{1,0},{3,2},... | collective-permute-start | bytes 1769480 | tf_op jit(solution)/shard_map/ppermute | solution.py:491
  247.9 1.5 copy-start
  247.9 1.9 copy-start.1
